TPU v7x, 32 devices: a whole 2x2x4 slice. The times are simulated.
32 devices in a mesh: gx: 16 (over z, y, core), ga: 2 (over x).
Axes of the slice: x: 2, y: 2, z: 4, core: 2. Of those that a mesh axis runs over, the one named last changes fastest.
Arguments:
- velocity: float32 [6144, 4096], P('gx', 'ga'), may hold values from -12 to 12, as said below
- left_gram: float32 [25, 5], replicated, may hold values from -2.5 to 2.5
- right_gram: float32 [25, 5], replicated, may hold values from -2.5 to 2.5
Outputs:
- x_slope: float32 [6144, 4096], P('gx', 'ga')
- section_field: float32 [6144, 4096], P('gx', 'ga')
Inputs may be any that keep to these rules, and one draw needn't show every extreme that they name: velocity at the grid points.
All inputs are finite; a program needn't handle non-finite values.
Results may differ from a plain program's by a relative error of at most 0.000071.
Values sent between devices are 32-bit elements; how exact they have to be, the bound alone decides.
No kernel may reach another device: no remote copies, remote signals or barrier semaphores. Data moves between devices by JAX's collectives and lax.ppermute only.
A program may use at most 64 MiB of HBM per device.

v0:
```python
import math

import jax
import jax.numpy as jnp
import numpy as np
from jax import lax
from jax.experimental import pallas as pl
from jax.experimental.pallas import tpu as pltpu
from jax.sharding import PartitionSpec as P

courant = 0.5
epsilon = 1e-06
LANE = 128
GROUP = 8
BF = jnp.bfloat16
F32 = jnp.float32


def add(a, b):
    return b if a is None else a if b is None else a + b


def sub(a, b):
    return a if b is None else -b if a is None else a - b


def scale(a, c):
    return None if a is None else a * np.float32(c)


def turn(value, angle):
    c, s = math.cos(angle), math.sin(angle)
    re, im = value
    return (sub(scale(re, c), scale(im, s)), add(scale(im, c), scale(re, s)))


def real_transform(seq):
    size = len(seq)
    if size == 1:
        return [(seq[0], None)]
    if size == 3:
        far = add(seq[1], seq[2])
        gap = sub(seq[1], seq[2])
        return [
            (add(seq[0], far), None),
            (sub(seq[0], scale(far, 0.5)), scale(gap, -math.sqrt(0.75))),
        ]
    even = real_transform(seq[0::2])
    odd = real_transform(seq[1::2])
    out = [None] * (size // 2 + 1)
    for f in range((size + 3) // 4):
        e = even[f]
        o = odd[f] if f == 0 else turn(odd[f], -2.0 * math.pi * f / size)
        out[f] = (add(e[0], o[0]), add(e[1], o[1]))
        out[size // 2 - f] = (sub(e[0], o[0]), sub(o[1], e[1]))
    if size % 4 == 0:
        f = size // 4
        out[f] = (even[f][0], scale(odd[f][0], -1.0))
    return out


def real_inverse(spec, size, count):
    if count <= 0:
        return []
    if size == 1:
        return [spec[0][0]]
    if size == 3:
        out = [add(spec[0][0], spec[1][0])]
        if count > 1:
            base = sub(spec[0][0], scale(spec[1][0], 0.5))
            side = scale(spec[1][1], math.sqrt(0.75))
            out.append(sub(base, side))
            out.append(add(base, side))
        return out[:count]
    half = size // 2
    even = [None] * (half // 2 + 1)
    odd = [None] * (half // 2 + 1)
    for f in range((size + 3) // 4):
        a, b = spec[f], spec[half - f]
        even[f] = (add(a[0], b[0]), sub(a[1], b[1]))
        diff = (sub(a[0], b[0]), add(a[1], b[1]))
        odd[f] = diff if f == 0 else turn(diff, 2.0 * math.pi * f / size)
    if size % 4 == 0:
        f = size // 4
        even[f] = (spec[f][0], None)
        odd[f] = (scale(spec[f][1], -1.0), None)
    first = real_inverse(even, half, (count + 1) // 2)
    second = real_inverse(odd, half, count // 2)
    out = [None] * count
    out[0::2] = first
    out[1::2] = second
    return out


def transform_size(least):
    size = 1
    while True:
        if size >= least:
            return size
        if size % 2 == 0 and size // 2 * 3 >= least:
            return size // 2 * 3
        size *= 2


def slope_spectrum(period, block, out_blocks, size):
    offsets = np.arange(size)
    offsets = np.where(offsets < out_blocks, offsets, offsets - size)
    step = np.arange(2 * block)
    index = block * offsets[:, None] + block - step[None, :]
    wrapped = (index + period // 2) % period - period // 2
    safe = np.where(wrapped == 0, 1, wrapped)
    sign = np.where(safe % 2 == 0, 1.0, -1.0)
    values = sign * (math.pi / period) / np.sin(math.pi * safe / period)
    values = np.where(wrapped == 0, 0.0, values)
    spectrum = np.fft.fft(values, axis=0)[: size // 2 + 1] / size
    table = np.empty((size, 2 * block))
    table[0] = spectrum[0].real
    table[1] = spectrum[size // 2].real
    table[2::2] = 2.0 * spectrum[1 : size // 2].real
    table[3::2] = 2.0 * spectrum[1 : size // 2].imag
    return table.astype(np.float32)


def split_parts(value):
    high = value.astype(BF)
    rest = value - high.astype(F32)
    mid = rest.astype(BF)
    return high, mid, (rest - mid.astype(F32)).astype(BF)


def left_lanes(shape):
    return lax.broadcasted_iota(jnp.int32, shape, len(shape) - 1) < shape[-1] // 2


def swap(value):
    return pltpu.roll(value, value.shape[-1] // 2, value.ndim - 1)


def merge(left, right):
    return jnp.where(left_lanes(left.shape), left, right)


def toeplitz_tables(spectrum, block):
    slots = spectrum.shape[0] // 2

    def body(w_ref, o_ref):
        def fill(f, _):
            for side in range(2):
                lane = w_ref[pl.ds(2 * f + side, 1), :]
                rows = jnp.broadcast_to(lane, (block, 2 * block))
                rows = pltpu.roll(rows, 0, 1, stride=1, stride_axis=0)[:, block:]
                high, mid, low = split_parts(rows)
                for p, part in enumerate((mid, high, low)):
                    o_ref[f, p * block : (p + 1) * block, side * block : (side + 1) * block] = part
            return 0

        lax.fori_loop(0, slots, fill, 0)

    return pl.pallas_call(
        body,
        name="toeplitz_tables",
        out_shape=jax.ShapeDtypeStruct((slots, 3 * block, 2 * block), BF),
        compiler_params=pltpu.CompilerParams(vmem_limit_bytes=16 << 20),
        cost_estimate=pl.CostEstimate(
            flops=slots * block * block * 32,
            bytes_accessed=slots * 3 * block * block * 4,
            transcendentals=0,
        ),
    )(spectrum)


def far_copies(count, place, stacked, pieces, sem, outward):
    rows = stacked.shape[1]
    out = []
    for k in range(count):
        other = lax.rem(place + (k if outward else count - k), count)
        mine = stacked.at[other]
        piece = pieces[k].at[pl.ds(0, rows)]
        pair = (mine, piece) if outward else (piece, mine)
        out.append(pltpu.make_async_copy(pair[0], pair[1], sem.at[k]))
    return out


def run_copies(copies):
    for copy in copies:
        copy.start()
    for copy in copies:
        copy.wait()


ANY = pl.BlockSpec(memory_space=pl.ANY)
SMEM = pl.BlockSpec(memory_space=pltpu.SMEM)
VMEM = pl.BlockSpec(memory_space=pltpu.VMEM)


def pack(view, chunk, count, place, carried):
    per, _, half, lines = view.shape
    span = lines // 2
    width = span // count * 2
    depth = per * half
    quarter = half // 2
    steps = [(b, q * quarter) for b in range(per) for q in range(2)]
    parts = carried is not None

    def body(place_ref, v_ref, *refs):
        refs = list(refs)
        total = refs.pop(0)[...] if parts else jnp.zeros((8, width), F32)
        outs = [refs.pop(0) for _ in range(count if parts else 1)]
        sums, buf, packed, in_sem, out_sem, sum_sem = refs
        arrive = [
            pltpu.make_async_copy(
                v_ref.at[b, :, pl.ds(r, quarter), pl.ds(chunk * span, span)],
                buf.at[j],
                in_sem.at[j],
            )
            for j, (b, r) in enumerate(steps)
        ]
        for copy in arrive:
            copy.start()
        leave = []
        for j, (b, r) in enumerate(steps):
            arrive[j].wait()
            rows = pl.ds(b * half + r, quarter)
            for tile in range(count // 2):
                top = buf[j, 0, :, tile * width : (tile + 1) * width]
                low = buf[j, 1, :, tile * width : (tile + 1) * width]
                packed[2 * tile, rows, :] = merge(top, swap(low))
                packed[2 * tile + 1, rows, :] = merge(swap(top), low)
                square = top * top + low * low
                total += jnp.sum(square.reshape(quarter // 8, 8, width), axis=0)
            if not parts:
                leave.append(
                    pltpu.make_async_copy(packed.at[:, rows], outs[0].at[:, rows], out_sem.at[j])
                )
                leave[-1].start()
        sums[...] = total
        if parts:
            leave = far_copies(count, place_ref[0], packed, outs, out_sem, True)
            for k in range(count):
                below = outs[k].at[pl.ds(depth, 8)]
                leave.append(pltpu.make_async_copy(sums, below, sum_sem.at[k]))
            for copy in leave:
                copy.start()
        for copy in leave:
            copy.wait()

    if parts:
        outs = [jax.ShapeDtypeStruct((depth + 8, width), F32)] * count
    else:
        outs = [jax.ShapeDtypeStruct((count, depth, width), F32)]
    result = pl.pallas_call(
        body,
        name="pack_pieces" if parts else "pack_stacked",
        in_specs=[SMEM, ANY] + [VMEM] * parts,
        out_specs=[ANY] * len(outs) + [VMEM],
        out_shape=outs + [jax.ShapeDtypeStruct((8, width), F32)],
        scratch_shapes=[
            pltpu.VMEM((len(steps), 2, quarter, span), F32),
            pltpu.VMEM((count, depth, width), F32),
            pltpu.SemaphoreType.DMA((len(steps),)),
            pltpu.SemaphoreType.DMA((max(count, len(steps)),)),
            pltpu.SemaphoreType.DMA((count,)),
        ],
        compiler_params=pltpu.CompilerParams(vmem_limit_bytes=8 << 20),
        cost_estimate=pl.CostEstimate(
            flops=depth * lines * 2, bytes_accessed=depth * lines * 8, transcendentals=0
        ),
    )(place, view, *([carried] if parts else []))
    return (list(result[:count]) if parts else result[0]), result[-1]


def line_slopes(arrived, place, gram, tables, match, spread):
    gather = isinstance(arrived, list)
    count = len(arrived) if gather else arrived.shape[0]
    depth = arrived[0].shape[0] - 8 if gather else arrived.shape[1]
    width = arrived[0].shape[-1]
    slots, block = tables.shape[0], tables.shape[2] // 2
    half = block // 2
    per = depth // half
    out_blocks = per * count
    size = 2 * slots
    ext_rows = gram.shape[0]

    def body(place_ref, g_ref, t_ref, *refs):
        refs = list(refs)
        ins = [refs.pop(0) for _ in range(count if gather else 1)]
        outs = [refs.pop(0) for _ in range(count if spread else 1)]
        if gather:
            energy_ref, lines, tiles, in_sem, sum_sem = [refs.pop(0)] + refs[-4:]
            copies = far_copies(count, place_ref[0], lines, ins, in_sem, False)
            for k in range(count):
                copies.append(
                    pltpu.make_async_copy(
                        ins[k].at[pl.ds(depth, 8)], tiles.at[k], sum_sem.at[k]
                    )
                )
            run_copies(copies)
            energy = tiles[0]
            for k in range(1, count):
                energy += tiles[k]
            energy_ref[...] = energy
        else:
            lines = ins[0]
        spec, extra = refs[:2]
        result = refs[2] if spread else outs[0]

        def at_block(b, at):
            return b // per, pl.ds((b % per) * half + at, GROUP), slice(None)

        ext = jnp.zeros((ext_rows, width), F32)
        for j in range(match):
            ext += g_ref[:, j : j + 1] * lines[0, j : j + 1, :]
        for j in range(match):
            row = depth - match + j
            tail = swap(lines[count - 1, row : row + 1, :])
            ext += g_ref[:, match + j : match + j + 1] * tail
        extra[...] = jnp.zeros_like(extra)
        extra[:ext_rows, :] = merge(ext, jnp.zeros_like(ext))

        def forward(group, _):
            at = pl.multiple_of(group * GROUP, GROUP)
            seq = [lines[at_block(b, at)] for b in range(out_blocks)]
            seq.append(extra[pl.ds(at, GROUP), :])
            out = real_transform(seq + [None] * (size - out_blocks - 1))
            spec[0, pl.ds(at, GROUP), :width] = out[0][0]
            spec[0, pl.ds(at, GROUP), width:] = out[slots][0]
            for f in range(1, slots):
                spec[f, pl.ds(at, GROUP), :width] = out[f][0]
                spec[f, pl.ds(at, GROUP), width:] = out[f][1]
            return 0

        lax.fori_loop(0, half // GROUP, forward, 0)

        def product(f, blocks):
            high, mid, low = split_parts(jnp.concatenate(blocks, 0))
            one = jnp.dot(
                t_ref[f, : 2 * block, :],
                jnp.concatenate([high, mid], 1),
                preferred_element_type=F32,
            )
            two = jnp.dot(
                t_ref[f, block:, :],
                jnp.concatenate([low, high], 1),
                preferred_element_type=F32,
            )
            small = one[:block, width:] + (two[:block, :width] + two[block:, width:])
            got = one[block:, :width] + ((one[:block, :width] + one[block:, width:]) + small)
            top, bottom = got[:half], got[half:]
            spec[f, :, :width] = merge(top, swap(bottom))
            spec[f, :, width:] = merge(swap(top), bottom)

        re, im = spec[0, :, :width], spec[0, :, width:]
        none = jnp.zeros_like(re)
        product(
            0, [merge(re, none), merge(swap(re), none), merge(none, swap(im)), merge(none, im)]
        )

        def multiply(f, _):
            re, im = spec[f, :, :width], spec[f, :, width:]
            re_s, im_s = swap(re), swap(im)
            product(f, [merge(re, im_s), merge(re_s, im), merge(-im, re_s), merge(-im_s, re)])
            return 0

        lax.fori_loop(1, slots, multiply, 0, unroll=4)

        def backward(group, _):
            at = pl.multiple_of(group * GROUP, GROUP)
            values = [(spec[0, pl.ds(at, GROUP), :width], None)]
            for f in range(1, slots):
                values.append(
                    (spec[f, pl.ds(at, GROUP), :width], spec[f, pl.ds(at, GROUP), width:])
                )
            values.append((spec[0, pl.ds(at, GROUP), width:], None))
            for b, value in enumerate(real_inverse(values, size, out_blocks)):
                result[at_block(b, at)] = value
            return 0

        lax.fori_loop(0, half // GROUP, backward, 0)
        if spread:
            run_copies(far_copies(count, place_ref[0], result, outs, refs[3], True))

    scratch = [pltpu.VMEM((slots, half, 2 * width), F32), pltpu.VMEM((half, width), F32)]
    if spread:
        scratch += [pltpu.VMEM((count, depth, width), F32), pltpu.SemaphoreType.DMA((count,))]
        out_specs = [ANY] * count
        out_shape = [jax.ShapeDtypeStruct((depth, width), F32)] * count
    else:
        out_specs = [VMEM]
        out_shape = [jax.ShapeDtypeStruct((count, depth, width), F32)]
    if gather:
        scratch += [
            pltpu.VMEM((count, depth, width), F32),
            pltpu.VMEM((count, 8, width), F32),
            pltpu.SemaphoreType.DMA((count,)),
            pltpu.SemaphoreType.DMA((count,)),
        ]
        out_specs = out_specs + [VMEM]
        out_shape = out_shape + [jax.ShapeDtypeStruct((8, width), F32)]
    out = pl.pallas_call(
        body,
        name="line_slopes",
        in_specs=[SMEM, VMEM, VMEM] + ([ANY] * count if gather else [VMEM]),
        out_specs=out_specs,
        out_shape=out_shape,
        scratch_shapes=scratch,
        compiler_params=pltpu.CompilerParams(vmem_limit_bytes=28 << 20),
        cost_estimate=pl.CostEstimate(
            flops=16 * size * block * block * width,
            bytes_accessed=8 * count * depth * width,
            transcendentals=0,
        ),
    )(place, gram, tables, *(arrived if gather else [arrived]))
    energy = out[-1] if gather else None
    return (list(out[:count]) if spread else out[0]), energy


def advect(view, chunk, arrived, place, rate, earlier):
    gather = isinstance(arrived, list)
    per, _, half, lines = view.shape
    span = lines // 2
    count = len(arrived) if gather else arrived.shape[0]
    depth, width = per * half, arrived[0].shape[-1]
    quarter = half // 2
    steps = [(b, q * quarter) for b in range(per) for q in range(2)]
    kept = 0 if earlier is None else 2

    def body(place_ref, rate_ref, v_ref, *refs):
        refs = list(refs)[kept:]
        ins = [refs.pop(0) for _ in range(count if gather else 1)]
        s_ref, f_ref, v_buf, stacked, s_buf, f_buf, v_sem, in_sem, s_sem, f_sem = refs

        def part(ref, j):
            b, r = steps[j]
            return ref.at[b, :, pl.ds(r, quarter), pl.ds(chunk * span, span)]

        fields = [
            pltpu.make_async_copy(part(v_ref, j), v_buf.at[j], v_sem.at[j])
            for j in range(len(steps))
        ]
        if gather:
            pieces = far_copies(count, place_ref[0], stacked, ins, in_sem, False)
        else:
            pieces = [pltpu.make_async_copy(ins[0], stacked, in_sem.at[0])]
        for copy in pieces + fields:
            copy.start()
        for copy in pieces:
            copy.wait()
        rate = rate_ref[0, 0]
        leave = []
        for j, (b, r) in enumerate(steps):
            fields[j].wait()
            rows = pl.ds(b * half + r, quarter)
            for tile in range(count // 2):
                lanes = slice(tile * width, (tile + 1) * width)
                one = stacked[2 * tile, rows, :]
                two = stacked[2 * tile + 1, rows, :]
                for side, slope in enumerate((merge(one, swap(two)), merge(swap(one), two))):
                    field = v_buf[j, side, :, lanes]
                    s_buf[j, side, :, lanes] = slope
                    f_buf[j, side, :, lanes] = field - rate * field * slope
            leave.append(pltpu.make_async_copy(s_buf.at[j], part(s_ref, j), s_sem.at[j]))
            leave.append(pltpu.make_async_copy(f_buf.at[j], part(f_ref, j), f_sem.at[j]))
            leave[-2].start()
            leave[-1].start()
        for copy in leave:
            copy.wait()

    tiles = pltpu.VMEM((len(steps), 2, quarter, span), F32)
    step_sem = pltpu.SemaphoreType.DMA((len(steps),))
    return pl.pallas_call(
        body,
        name="advect",
        in_specs=[SMEM, SMEM, ANY] + [ANY] * kept + [ANY] * (count if gather else 1),
        out_specs=[ANY, ANY],
        out_shape=[jax.ShapeDtypeStruct(view.shape, F32)] * 2,
        scratch_shapes=[
            tiles,
            pltpu.VMEM((count, depth, width), F32),
            tiles,
            tiles,
            step_sem,
            pltpu.SemaphoreType.DMA((count,)),
            step_sem,
            step_sem,
        ],
        input_output_aliases={3: 0, 4: 1} if kept else {},
        compiler_params=pltpu.CompilerParams(vmem_limit_bytes=12 << 20),
        cost_estimate=pl.CostEstimate(
            flops=depth * lines * 3, bytes_accessed=depth * lines * 16, transcendentals=0
        ),
    )(place, rate, view, *(earlier or ()), *(arrived if gather else [arrived]))


def exchange(pieces, axis):
    if not isinstance(pieces, list):
        return lax.all_to_all(pieces, axis, split_axis=0, concat_axis=0, tiled=True)
    count = len(pieces)
    out = [pieces[0]]
    for k in range(1, count):
        moved = lax.ppermute(pieces[k], axis, [(i, (i + k) % count) for i in range(count)])
        out.append(moved)
    return out


def total_over(part, axis):
    size = lax.axis_size(axis)
    moving = part
    for _ in range(size - 1):
        moving = lax.ppermute(moving, axis, [(i, (i + 1) % size) for i in range(size)])
        part = part + moving
    return part


def per_device(velocity, left_gram, right_gram):
    row_count, line_total = velocity.shape
    cont, match = left_gram.shape
    gx_count = lax.axis_size("gx")
    ga_count = lax.axis_size("ga")
    place = lax.axis_index("gx").astype(jnp.int32).reshape(1)
    total = row_count * gx_count
    block = 2 * LANE
    while row_count % block or block > LANE:
        block //= 2
    half = block // 2
    assert cont <= half and match <= half and line_total % (gx_count * LANE) == 0
    out_blocks = total // block
    size = transform_size(2 * out_blocks)
    view = velocity.reshape(row_count // block, 2, half, line_total)

    first, sums = pack(view, 0, gx_count, place, None)
    first = exchange(first, "gx")
    second, _ = pack(view, 1, gx_count, place, sums)
    second = exchange(second, "gx")
    spectrum = slope_spectrum(total + cont, block, out_blocks, size)
    tables = toeplitz_tables(jnp.asarray(spectrum), block)
    gram = jnp.concatenate([left_gram, right_gram], axis=1)
    gram = jnp.pad(gram, ((0, -cont % 8), (0, 0)))
    first, _ = line_slopes(first, place, gram, tables, match, False)
    first = exchange(first, "gx")
    second, energy = line_slopes(second, place, gram, tables, match, True)
    second = exchange(second, "gx")
    energy = total_over(energy, "ga")
    mean_square = jnp.sum(energy) / (row_count * line_total * gx_count * ga_count)
    advect_rate = (courant / jnp.sqrt(mean_square + epsilon)).reshape(1, 1)
    done = advect(view, 0, first, place, advect_rate, None)
    done = advect(view, 1, second, place, advect_rate, done)
    return tuple(part.reshape(row_count, line_total) for part in done)


def solution(mesh):
    return jax.shard_map(
        per_device,
        mesh=mesh,
        in_specs=(P("gx", "ga"), P(), P()),
        out_specs=(P("gx", "ga"), P("gx", "ga")),
        check_vma=False,
    )
```

profile of v0, /device:TPU:0, one launch (start us, length us, event | category | flops | bytes accessed | tf_op | source)
XLA Modules:
  0.0 216.0 jit_solution(14783573682158956159)
XLA Ops:
  5.1 7.4 %all-to-all-start = ((f32[16,192,128]{2,1,0:T(8,128)}), f32[16,192,128]{2,1,0:T(8,128)S(1)}, u32[]{:S(2)}, u32[]{:S(2)}) async-start(f32[16,192,128]{2,1,0:T(8,128)} %copy-done.8), calls=%async_computation | async-start | bytes 3145728 | tf_op jit(solution)/shard_map/all_to_all | solution.py:496
  12.7 6.9 %toeplitz_tables.1.t_ref = bf16[48,384,256]{2,1,0:T(8,128)(2,1)S(1)} custom-call(f32[96,256]{1,0:T(8,128)S(1)} %copy-done.23), custom_call_target="tpu_custom_call" | custom-call | flops 25165824 | bytes 9437184 | tf_op jit(solution)/shard_map/toeplitz_tables/pallas_call | solution.py:159
  19.6 3.7 %copy-done.2 = bf16[48,384,256]{2,1,0:T(8,128)(2,1)} copy-done((bf16[48,384,256]{2,1,0:T(8,128)(2,1)}, bf16[48,384,256]{2,1,0:T(8,128)(2,1)S(1)}, u32[]{:S(2)}) %copy-start.2) | copy-done | bytes 9437208
  23.4 21.0 %all-to-all-done.refs_0_ = f32[16,192,128]{2,1,0:T(8,128)S(1)} async-done(((f32[16,192,128]{2,1,0:T(8,128)}), f32[16,192,128]{2,1,0:T(8,128)S(1)}, u32[]{:S(2)}, u32[]{:S(2)}) %all-to-all-start) | async-done | bytes 1572896 | tf_op jit(solution)/shard_map/all_to_all | solution.py:496
  45.5 3.7 %copy-done.3 = bf16[48,384,256]{2,1,0:T(8,128)(2,1)S(1)} copy-done((bf16[48,384,256]{2,1,0:T(8,128)(2,1)S(1)}, bf16[48,384,256]{2,1,0:T(8,128)(2,1)}, u32[]{:S(2)}) %copy-start.3) | copy-done | bytes 9437208
  50.6 11.1 %line_slopes.3 = f32[16,192,128]{2,1,0:T(8,128)S(1)} custom-call(s32[1]{0:T(128)} %bitcast.place_ref, f32[32,10]{1,0:T(8,128)S(1)} %select_maximum_fusion.g_ref, bf16[48,384,256]{2,1,0:T(8,128)(2,1)S(1)} %copy-done.3, f32[16,192,128]{2,1,0:T(8,128)S(1)} %copy-done.7), custom_call_target="tpu_custom_call" | custom-call | flops 3221225472 | bytes 3145728 | tf_op jit(solution)/shard_map/line_slopes/pallas_call | solution.py:399
  62.8 9.4 %all-to-all-start.1 = ((f32[16,192,128]{2,1,0:T(8,128)}), f32[16,192,128]{2,1,0:T(8,128)}, u32[]{:S(2)}, u32[]{:S(2)}) async-start(f32[16,192,128]{2,1,0:T(8,128)} %copy-done.5), calls=%async_computation.1 | async-start | bytes 3145728 | tf_op jit(solution)/shard_map/all_to_all | solution.py:496
  72.3 4.3 %pack_pieces.1 = (f32[200,128]{1,0:T(8,128)S(1)}, f32[200,128]{1,0:T(8,128)S(1)}, f32[200,128]{1,0:T(8,128)S(1)}, f32[200,128]{1,0:T(8,128)S(1)}, f32[200,128]{1...) custom-call(s32[1]{0:T(128)} %bitcast.place_ref, ...), custom_call_target="tpu_custom_call" | custom-call | flops 786432 | bytes 3145728 | tf_op jit(solution)/shard_map/pack_pieces/pallas_call | solution.py:251
  82.5 22.7 %collective-permute-done.refs_1_ = f32[200,128]{1,0:T(8,128)S(1)} collective-permute-done((f32[200,128]{1,0:T(8,128)S(1)}, f32[200,128]{1,0:T(8,128)S(1)}, u32[]{:S(2)}, u32[]{:S(2)}) %collective-permute-start) | collective-permute-done | bytes 102432 | tf_op jit(solution)/shard_map/ppermute | solution.py:500
  106.4 10.0 %collective-permute-start.6 = (f32[200,128]{1,0:T(8,128)S(1)}, f32[200,128]{1,0:T(8,128)S(1)}, u32[]{:S(2)}, u32[]{:S(2)}) collective-permute-start(f32[200,128]{1,0:T(8,128)S(1)} %get-tuple-element.49), channel_id=1, source_target_pairs={{0,14},{2,16},{4,18},{6,20},{8,22},{10,24},{12,26},{14,28},{16,30}... | collective-permute-start | bytes 307208 | tf_op jit(solution)/shard_map/ppermute | solution.py:500
  119.9 9.2 %collective-permute-done.4.refs_5_ = f32[200,128]{1,0:T(8,128)S(1)} collective-permute-done((f32[200,128]{1,0:T(8,128)S(1)}, f32[200,128]{1,0:T(8,128)S(1)}, u32[]{:S(2)}, u32[]{:S(2)}) %collective-permute-start.4) | collective-permute-done | bytes 102432 | tf_op jit(solution)/shard_map/ppermute | solution.py:500
  130.5 6.7 %collective-permute-start.11 = (f32[200,128]{1,0:T(8,128)S(1)}, f32[200,128]{1,0:T(8,128)S(1)}, u32[]{:S(2)}, u32[]{:S(2)}) collective-permute-start(f32[200,128]{1,0:T(8,128)S(1)} %get-tuple-element.54), channel_id=1, source_target_pairs={{0,24},{2,26},{4,28},{6,30},{8,0},{10,2},{12,4},{14,6},{16,8},{18,... | collective-permute-start | bytes 307208 | tf_op jit(solution)/shard_map/ppermute | solution.py:500
  137.3 2.5 %collective-permute-start.12 = (f32[200,128]{1,0:T(8,128)S(1)}, f32[200,128]{1,0:T(8,128)S(1)}, u32[]{:S(2)}, u32[]{:S(2)}) collective-permute-start(f32[200,128]{1,0:T(8,128)S(1)} %get-tuple-element.55), channel_id=1, source_target_pairs={{0,26},{2,28},{4,30},{6,0},{8,2},{10,4},{12,6},{14,8},{16,10},{18,... | collective-permute-start | bytes 307208 | tf_op jit(solution)/shard_map/ppermute | solution.py:500
  139.8 2.8 %collective-permute-start.13 = (f32[200,128]{1,0:T(8,128)S(1)}, f32[200,128]{1,0:T(8,128)S(1)}, u32[]{:S(2)}, u32[]{:S(2)}) collective-permute-start(f32[200,128]{1,0:T(8,128)S(1)} %get-tuple-element.56), channel_id=1, source_target_pairs={{0,28},{2,30},{4,0},{6,2},{8,4},{10,6},{12,8},{14,10},{16,12},{18,... | collective-permute-start | bytes 307208 | tf_op jit(solution)/shard_map/ppermute | solution.py:500
  144.8 2.5 %collective-permute-done.13.refs_14_ = f32[200,128]{1,0:T(8,128)S(1)} collective-permute-done((f32[200,128]{1,0:T(8,128)S(1)}, f32[200,128]{1,0:T(8,128)S(1)}, u32[]{:S(2)}, u32[]{:S(2)}) %collective-permute-start.13) | collective-permute-done | bytes 102432 | tf_op jit(solution)/shard_map/ppermute | solution.py:500
  147.5 3.7 %copy-done.4 = bf16[48,384,256]{2,1,0:T(8,128)(2,1)S(1)} copy-done((bf16[48,384,256]{2,1,0:T(8,128)(2,1)S(1)}, bf16[48,384,256]{2,1,0:T(8,128)(2,1)}, u32[]{:S(2)}) %copy-start.4) | copy-done | bytes 9437208
  151.2 16.5 %line_slopes.2 = (f32[192,128]{1,0:T(8,128)S(1)}, f32[192,128]{1,0:T(8,128)S(1)}, f32[192,128]{1,0:T(8,128)S(1)}, f32[192,128]{1,0:T(8,128)S(1)}, f32[192,128]{1...) custom-call(s32[1]{0:T(128)} %bitcast.place_ref, ...), custom_call_target="tpu_custom_call" | custom-call | flops 3221225472 | bytes 3145728 | tf_op jit(solution)/shard_map/line_slopes/pallas_call | solution.py:399
  176.1 2.8 %collective-permute-done.17.refs_4_ = f32[192,128]{1,0:T(8,128)S(1)} collective-permute-done((f32[192,128]{1,0:T(8,128)S(1)}, f32[192,128]{1,0:T(8,128)S(1)}, u32[]{:S(2)}, u32[]{:S(2)}) %collective-permute-start.17) | collective-permute-done | bytes 98336 | tf_op jit(solution)/shard_map/ppermute | solution.py:500
  180.8 2.9 %collective-permute-start.24 = (f32[192,128]{1,0:T(8,128)S(1)}, f32[192,128]{1,0:T(8,128)S(1)}, u32[]{:S(2)}, u32[]{:S(2)}) collective-permute-start(f32[192,128]{1,0:T(8,128)S(1)} %get-tuple-element.71), channel_id=1, source_target_pairs={{0,18},{2,20},{4,22},{6,24},{8,26},{10,28},{12,30},{14,0},{16,2},{... | collective-permute-start | bytes 294920 | tf_op jit(solution)/shard_map/ppermute | solution.py:500
  183.8 10.4 %collective-permute-done.20.refs_7_ = f32[192,128]{1,0:T(8,128)S(1)} collective-permute-done((f32[192,128]{1,0:T(8,128)S(1)}, f32[192,128]{1,0:T(8,128)S(1)}, u32[]{:S(2)}, u32[]{:S(2)}) %collective-permute-start.20) | collective-permute-done | bytes 98336 | tf_op jit(solution)/shard_map/ppermute | solution.py:500
  196.8 3.3 %collective-permute-start.27 = (f32[192,128]{1,0:T(8,128)}, f32[192,128]{1,0:T(8,128)}, u32[]{:S(2)}, u32[]{:S(2)}) collective-permute-start(f32[192,128]{1,0:T(8,128)} %get-tuple-element.74), channel_id=1, source_target_pairs={{0,24},{2,26},{4,28},{6,30},{8,0},{10,2},{12,4},{14,6},{16,8},{18,... | collective-permute-start | bytes 294920 | tf_op jit(solution)/shard_map/ppermute | solution.py:500
  202.3 3.1 %collective-permute-start.29 = (f32[192,128]{1,0:T(8,128)}, f32[192,128]{1,0:T(8,128)}, u32[]{:S(2)}, u32[]{:S(2)}) collective-permute-start(f32[192,128]{1,0:T(8,128)} %get-tuple-element.76), channel_id=1, source_target_pairs={{0,28},{2,30},{4,0},{6,2},{8,4},{10,6},{12,8},{14,10},{16,12},{18,... | collective-permute-start | bytes 294920 | tf_op jit(solution)/shard_map/ppermute | solution.py:500
  207.4 3.6 %advect.2 = (f32[3,2,64,2048]{3,2,1,0:T(8,128)}, f32[3,2,64,2048]{3,2,1,0:T(8,128)}) custom-call(s32[1]{0:T(128)} %bitcast.place_ref, f32[1,1]{1,0:T(1,128)} %bitcast.2.rate_ref, f32[3,2,64,2048]{3,2,1,0:T(8,128)S(1)} %bitcast.7, f32[16,192,128]{2,1,0:T(8,128)} %all-to-all-done.1.refs_0_), custom_call_target="tpu_custom_call" | custom-call | flops 1179648 | bytes 6291456 | tf_op jit(solution)/shard_map/advect/pallas_call | solution.py:470
  211.2 4.8 %advect.3 = (f32[3,2,64,2048]{3,2,1,0:T(8,128)}, f32[3,2,64,2048]{3,2,1,0:T(8,128)}) custom-call(s32[1]{0:T(128)} %bitcast.place_ref, f32[1,1]{1,0:T(1,128)} %bitcast.2.rate_ref, f32[3,2,64,2048]{3,2,1,0:T(8,128)S(1)} %bitcast.8, f32[3,2,64,2048]{3,2,1,0:T(8,128)} %get-tuple-element.60.refs_0_, ...), custom_call_target="tpu_custom_call", output_to_operand_aliasing={{0}: (3, {}), {1}: (4, {})} | custom-call | flops 1179648 | bytes 6291456 | tf_op jit(solution)/shard_map/advect/pallas_call | solution.py:470
  (105 shorter events, 39.1 us)
Async XLA Ops:
  5.1 39.3 %all-to-all-start = ((f32[16,192,128]{2,1,0:T(8,128)}), f32[16,192,128]{2,1,0:T(8,128)S(1)}, u32[]{:S(2)}, u32[]{:S(2)}) async-start(f32[16,192,128]{2,1,0:T(8,128)} %copy-done.8), calls=%async_computation | async-start | bytes 3145728 | tf_op jit(solution)/shard_map/all_to_all | solution.py:496
  62.8 144.5 %all-to-all-start.1 = ((f32[16,192,128]{2,1,0:T(8,128)}), f32[16,192,128]{2,1,0:T(8,128)}, u32[]{:S(2)}, u32[]{:S(2)}) async-start(f32[16,192,128]{2,1,0:T(8,128)} %copy-done.5), calls=%async_computation.1 | async-start | bytes 3145728 | tf_op jit(solution)/shard_map/all_to_all | solution.py:496
  76.6 28.6 %collective-permute-start = (f32[200,128]{1,0:T(8,128)S(1)}, f32[200,128]{1,0:T(8,128)S(1)}, u32[]{:S(2)}, u32[]{:S(2)}) collective-permute-start(f32[200,128]{1,0:T(8,128)S(1)} %get-tuple-element.43), channel_id=1, source_target_pairs={{0,2},{2,4},{4,6},{6,8},{8,10},{10,12},{12,14},{14,16},{16,18},{18... | collective-permute-start | bytes 307208 | tf_op jit(solution)/shard_map/ppermute | solution.py:500
  77.0 29.4 %collective-permute-start.1 = (f32[200,128]{1,0:T(8,128)S(1)}, f32[200,128]{1,0:T(8,128)S(1)}, u32[]{:S(2)}, u32[]{:S(2)}) collective-permute-start(f32[200,128]{1,0:T(8,128)S(1)} %get-tuple-element.44), channel_id=1, source_target_pairs={{0,4},{2,6},{4,8},{6,10},{8,12},{10,14},{12,16},{14,18},{16,20},{1... | collective-permute-start | bytes 307208 | tf_op jit(solution)/shard_map/ppermute | solution.py:500
  78.7 37.8 %collective-permute-start.2 = (f32[200,128]{1,0:T(8,128)S(1)}, f32[200,128]{1,0:T(8,128)S(1)}, u32[]{:S(2)}, u32[]{:S(2)}) collective-permute-start(f32[200,128]{1,0:T(8,128)S(1)} %get-tuple-element.45), channel_id=1, source_target_pairs={{0,6},{2,8},{4,10},{6,12},{8,14},{10,16},{12,18},{14,20},{16,22},{... | collective-permute-start | bytes 307208 | tf_op jit(solution)/shard_map/ppermute | solution.py:500
  80.9 36.7 %collective-permute-start.3 = (f32[200,128]{1,0:T(8,128)S(1)}, f32[200,128]{1,0:T(8,128)S(1)}, u32[]{:S(2)}, u32[]{:S(2)}) collective-permute-start(f32[200,128]{1,0:T(8,128)S(1)} %get-tuple-element.46), channel_id=1, source_target_pairs={{0,8},{2,10},{4,12},{6,14},{8,16},{10,18},{12,20},{14,22},{16,24},... | collective-permute-start | bytes 307208 | tf_op jit(solution)/shard_map/ppermute | solution.py:500
  82.4 46.7 %collective-permute-start.4 = (f32[200,128]{1,0:T(8,128)S(1)}, f32[200,128]{1,0:T(8,128)S(1)}, u32[]{:S(2)}, u32[]{:S(2)}) collective-permute-start(f32[200,128]{1,0:T(8,128)S(1)} %get-tuple-element.47), channel_id=1, source_target_pairs={{0,10},{2,12},{4,14},{6,16},{8,18},{10,20},{12,22},{14,24},{16,26}... | collective-permute-start | bytes 307208 | tf_op jit(solution)/shard_map/ppermute | solution.py:500
  105.2 25.0 %collective-permute-start.5 = (f32[200,128]{1,0:T(8,128)S(1)}, f32[200,128]{1,0:T(8,128)S(1)}, u32[]{:S(2)}, u32[]{:S(2)}) collective-permute-start(f32[200,128]{1,0:T(8,128)S(1)} %get-tuple-element.48), channel_id=1, source_target_pairs={{0,12},{2,14},{4,16},{6,18},{8,20},{10,22},{12,24},{14,26},{16,28}... | collective-permute-start | bytes 307208 | tf_op jit(solution)/shard_map/ppermute | solution.py:500
  106.4 24.2 %collective-permute-start.6 = (f32[200,128]{1,0:T(8,128)S(1)}, f32[200,128]{1,0:T(8,128)S(1)}, u32[]{:S(2)}, u32[]{:S(2)}) collective-permute-start(f32[200,128]{1,0:T(8,128)S(1)} %get-tuple-element.49), channel_id=1, source_target_pairs={{0,14},{2,16},{4,18},{6,20},{8,22},{10,24},{12,26},{14,28},{16,30}... | collective-permute-start | bytes 307208 | tf_op jit(solution)/shard_map/ppermute | solution.py:500
  116.4 20.9 %collective-permute-start.7 = (f32[200,128]{1,0:T(8,128)S(1)}, f32[200,128]{1,0:T(8,128)S(1)}, u32[]{:S(2)}, u32[]{:S(2)}) collective-permute-start(f32[200,128]{1,0:T(8,128)S(1)} %get-tuple-element.50), channel_id=1, source_target_pairs={{0,16},{2,18},{4,20},{6,22},{8,24},{10,26},{12,28},{14,30},{16,0},... | collective-permute-start | bytes 307208 | tf_op jit(solution)/shard_map/ppermute | solution.py:500
  117.6 22.3 %collective-permute-start.8 = (f32[200,128]{1,0:T(8,128)S(1)}, f32[200,128]{1,0:T(8,128)S(1)}, u32[]{:S(2)}, u32[]{:S(2)}) collective-permute-start(f32[200,128]{1,0:T(8,128)S(1)} %get-tuple-element.51), channel_id=1, source_target_pairs={{0,18},{2,20},{4,22},{6,24},{8,26},{10,28},{12,30},{14,0},{16,2},{... | collective-permute-start | bytes 307208 | tf_op jit(solution)/shard_map/ppermute | solution.py:500
  129.1 13.5 %collective-permute-start.9 = (f32[200,128]{1,0:T(8,128)S(1)}, f32[200,128]{1,0:T(8,128)S(1)}, u32[]{:S(2)}, u32[]{:S(2)}) collective-permute-start(f32[200,128]{1,0:T(8,128)S(1)} %get-tuple-element.52), channel_id=1, source_target_pairs={{0,20},{2,22},{4,24},{6,26},{8,28},{10,30},{12,0},{14,2},{16,4},{1... | collective-permute-start | bytes 307208 | tf_op jit(solution)/shard_map/ppermute | solution.py:500
  130.3 14.5 %collective-permute-start.10 = (f32[200,128]{1,0:T(8,128)S(1)}, f32[200,128]{1,0:T(8,128)S(1)}, u32[]{:S(2)}, u32[]{:S(2)}) collective-permute-start(f32[200,128]{1,0:T(8,128)S(1)} %get-tuple-element.53), channel_id=1, source_target_pairs={{0,22},{2,24},{4,26},{6,28},{8,30},{10,0},{12,2},{14,4},{16,6},{18... | collective-permute-start | bytes 307208 | tf_op jit(solution)/shard_map/ppermute | solution.py:500
  130.5 14.2 %collective-permute-start.11 = (f32[200,128]{1,0:T(8,128)S(1)}, f32[200,128]{1,0:T(8,128)S(1)}, u32[]{:S(2)}, u32[]{:S(2)}) collective-permute-start(f32[200,128]{1,0:T(8,128)S(1)} %get-tuple-element.54), channel_id=1, source_target_pairs={{0,24},{2,26},{4,28},{6,30},{8,0},{10,2},{12,4},{14,6},{16,8},{18,... | collective-permute-start | bytes 307208 | tf_op jit(solution)/shard_map/ppermute | solution.py:500
  172.8 21.4 %collective-permute-start.20 = (f32[192,128]{1,0:T(8,128)S(1)}, f32[192,128]{1,0:T(8,128)S(1)}, u32[]{:S(2)}, u32[]{:S(2)}) collective-permute-start(f32[192,128]{1,0:T(8,128)S(1)} %get-tuple-element.67), channel_id=1, source_target_pairs={{0,10},{2,12},{4,14},{6,16},{8,18},{10,20},{12,22},{14,24},{16,26}... | collective-permute-start | bytes 294920 | tf_op jit(solution)/shard_map/ppermute | solution.py:500
  176.0 18.8 %collective-permute-start.21 = (f32[192,128]{1,0:T(8,128)S(1)}, f32[192,128]{1,0:T(8,128)S(1)}, u32[]{:S(2)}, u32[]{:S(2)}) collective-permute-start(f32[192,128]{1,0:T(8,128)S(1)} %get-tuple-element.68), channel_id=1, source_target_pairs={{0,12},{2,14},{4,16},{6,18},{8,20},{10,22},{12,24},{14,26},{16,28}... | collective-permute-start | bytes 294920 | tf_op jit(solution)/shard_map/ppermute | solution.py:500
  178.9 17.3 %collective-permute-start.22 = (f32[192,128]{1,0:T(8,128)S(1)}, f32[192,128]{1,0:T(8,128)S(1)}, u32[]{:S(2)}, u32[]{:S(2)}) collective-permute-start(f32[192,128]{1,0:T(8,128)S(1)} %get-tuple-element.69), channel_id=1, source_target_pairs={{0,14},{2,16},{4,18},{6,20},{8,22},{10,24},{12,26},{14,28},{16,30}... | collective-permute-start | bytes 294920 | tf_op jit(solution)/shard_map/ppermute | solution.py:500
  179.0 21.2 %collective-permute-start.23 = (f32[192,128]{1,0:T(8,128)S(1)}, f32[192,128]{1,0:T(8,128)S(1)}, u32[]{:S(2)}, u32[]{:S(2)}) collective-permute-start(f32[192,128]{1,0:T(8,128)S(1)} %get-tuple-element.70), channel_id=1, source_target_pairs={{0,16},{2,18},{4,20},{6,22},{8,24},{10,26},{12,28},{14,30},{16,0},... | collective-permute-start | bytes 294920 | tf_op jit(solution)/shard_map/ppermute | solution.py:500
  180.8 20.9 %collective-permute-start.24 = (f32[192,128]{1,0:T(8,128)S(1)}, f32[192,128]{1,0:T(8,128)S(1)}, u32[]{:S(2)}, u32[]{:S(2)}) collective-permute-start(f32[192,128]{1,0:T(8,128)S(1)} %get-tuple-element.71), channel_id=1, source_target_pairs={{0,18},{2,20},{4,22},{6,24},{8,26},{10,28},{12,30},{14,0},{16,2},{... | collective-permute-start | bytes 294920 | tf_op jit(solution)/shard_map/ppermute | solution.py:500
  194.8 10.6 %collective-permute-start.25 = (f32[192,128]{1,0:T(8,128)S(1)}, f32[192,128]{1,0:T(8,128)S(1)}, u32[]{:S(2)}, u32[]{:S(2)}) collective-permute-start(f32[192,128]{1,0:T(8,128)S(1)} %get-tuple-element.72), channel_id=1, source_target_pairs={{0,20},{2,22},{4,24},{6,26},{8,28},{10,30},{12,0},{14,2},{16,4},{1... | collective-permute-start | bytes 294920 | tf_op jit(solution)/shard_map/ppermute | solution.py:500
  195.5 15.6 %collective-permute-start.26 = (f32[192,128]{1,0:T(8,128)}, f32[192,128]{1,0:T(8,128)}, u32[]{:S(2)}, u32[]{:S(2)}) collective-permute-start(f32[192,128]{1,0:T(8,128)} %get-tuple-element.73), channel_id=1, source_target_pairs={{0,22},{2,24},{4,26},{6,28},{8,30},{10,0},{12,2},{14,4},{16,6},{18... | collective-permute-start | bytes 294920 | tf_op jit(solution)/shard_map/ppermute | solution.py:500
  196.8 14.2 %collective-permute-start.27 = (f32[192,128]{1,0:T(8,128)}, f32[192,128]{1,0:T(8,128)}, u32[]{:S(2)}, u32[]{:S(2)}) collective-permute-start(f32[192,128]{1,0:T(8,128)} %get-tuple-element.74), channel_id=1, source_target_pairs={{0,24},{2,26},{4,28},{6,30},{8,0},{10,2},{12,4},{14,6},{16,8},{18,... | collective-permute-start | bytes 294920 | tf_op jit(solution)/shard_map/ppermute | solution.py:500
  200.8 10.3 %collective-permute-start.28 = (f32[192,128]{1,0:T(8,128)}, f32[192,128]{1,0:T(8,128)}, u32[]{:S(2)}, u32[]{:S(2)}) collective-permute-start(f32[192,128]{1,0:T(8,128)} %get-tuple-element.75), channel_id=1, source_target_pairs={{0,26},{2,28},{4,30},{6,0},{8,2},{10,4},{12,6},{14,8},{16,10},{18,... | collective-permute-start | bytes 294920 | tf_op jit(solution)/shard_map/ppermute | solution.py:500
  202.3 8.8 %collective-permute-start.29 = (f32[192,128]{1,0:T(8,128)}, f32[192,128]{1,0:T(8,128)}, u32[]{:S(2)}, u32[]{:S(2)}) collective-permute-start(f32[192,128]{1,0:T(8,128)} %get-tuple-element.76), channel_id=1, source_target_pairs={{0,28},{2,30},{4,0},{6,2},{8,4},{10,6},{12,8},{14,10},{16,12},{18,... | collective-permute-start | bytes 294920 | tf_op jit(solution)/shard_map/ppermute | solution.py:500
  (35 other events, 149.1 us)
where the time goes:
time: 216 us
  waiting for transfers between devices  72.1 us (33%)
  starting transfers between devices  70.4 us (33%)
  Pallas kernels  48.7 us (23%)
  local copies, waits for them, and re-layouts  22.4 us (10%)
    ppermute x30, starting transfers between devices, exchange(): lax.ppermute(pieces[k], axis, [(i, (i + k) % count) for i in range(count)])  52 us
    ppermute x30, waiting for transfers between devices, exchange(): lax.ppermute(pieces[k], axis, [(i, (i + k) % count) for i in range(count)])  51.2 us
    pallas_call x2, Pallas kernels, line_slopes(): pl.pallas_call(body, name='line_slopes', in_specs=[SMEM, VMEM, VMEM] + ([...  27.7 us
    unnamed x54, local copies, waits for them, and re-layouts  22.4 us
    all_to_all x2, waiting for transfers between devices, exchange(): return lax.all_to_all(pieces, axis, split_axis=0, concat_axis=0, tiled=True)  21 us
    all_to_all x2, starting transfers between devices, exchange(): return lax.all_to_all(pieces, axis, split_axis=0, concat_axis=0, tiled=True)  16.8 us
    pallas_call x2, Pallas kernels, advect(): pl.pallas_call(body, name='advect', in_specs=[SMEM, SMEM, ANY] + [ANY] *...  8.4 us
    pallas_call x1, Pallas kernels, toeplitz_tables(): pl.pallas_call(body, name='toeplitz_tables', out_shape=jax.ShapeDtypeStru...  6.92 us
  transfers between devices with their start and end apart: 33, of which 10 were waited for; matrix products, arithmetic and copies ran while one was open for 0% of the time, Pallas kernels for 15%

commit v1 on v0

--- a/solution.py
+++ b/solution.py
@@ -160,7 +160,7 @@
         body,
         name="toeplitz_tables",
         out_shape=jax.ShapeDtypeStruct((slots, 3 * block, 2 * block), BF),
-        compiler_params=pltpu.CompilerParams(vmem_limit_bytes=16 << 20),
+        compiler_params=pltpu.CompilerParams(vmem_limit_bytes=58 << 20),
         cost_estimate=pl.CostEstimate(
             flops=slots * block * block * 32,
             bytes_accessed=slots * 3 * block * block * 4,
@@ -188,25 +188,24 @@
         copy.wait()
 
 
-ANY = pl.BlockSpec(memory_space=pl.ANY)
+HBM = pl.BlockSpec(memory_space=pltpu.HBM)
 SMEM = pl.BlockSpec(memory_space=pltpu.SMEM)
 VMEM = pl.BlockSpec(memory_space=pltpu.VMEM)
 
 
-def pack(view, chunk, count, place, carried):
+def pack(view, chunk, count, place, carried, parts):
     per, _, half, lines = view.shape
     span = lines // 2
     width = span // count * 2
     depth = per * half
     quarter = half // 2
     steps = [(b, q * quarter) for b in range(per) for q in range(2)]
-    parts = carried is not None
 
     def body(place_ref, v_ref, *refs):
         refs = list(refs)
-        total = refs.pop(0)[...] if parts else jnp.zeros((8, width), F32)
+        total = jnp.zeros((8, width), F32) if carried is None else refs.pop(0)[...]
         outs = [refs.pop(0) for _ in range(count if parts else 1)]
-        sums, buf, packed, in_sem, out_sem, sum_sem = refs
+        sums, buf, packed, in_sem, out_sem = refs
         arrive = [
             pltpu.make_async_copy(
                 v_ref.at[b, :, pl.ds(r, quarter), pl.ds(chunk * span, span)],
@@ -236,73 +235,69 @@
         sums[...] = total
         if parts:
             leave = far_copies(count, place_ref[0], packed, outs, out_sem, True)
-            for k in range(count):
-                below = outs[k].at[pl.ds(depth, 8)]
-                leave.append(pltpu.make_async_copy(sums, below, sum_sem.at[k]))
             for copy in leave:
                 copy.start()
         for copy in leave:
             copy.wait()
 
     if parts:
-        outs = [jax.ShapeDtypeStruct((depth + 8, width), F32)] * count
+        outs = [jax.ShapeDtypeStruct((depth, width), F32)] * count
     else:
         outs = [jax.ShapeDtypeStruct((count, depth, width), F32)]
     result = pl.pallas_call(
         body,
         name="pack_pieces" if parts else "pack_stacked",
-        in_specs=[SMEM, ANY] + [VMEM] * parts,
-        out_specs=[ANY] * len(outs) + [VMEM],
+        in_specs=[SMEM, HBM] + [VMEM] * (carried is not None),
+        out_specs=[HBM] * len(outs) + [VMEM],
         out_shape=outs + [jax.ShapeDtypeStruct((8, width), F32)],
         scratch_shapes=[
             pltpu.VMEM((len(steps), 2, quarter, span), F32),
             pltpu.VMEM((count, depth, width), F32),
             pltpu.SemaphoreType.DMA((len(steps),)),
             pltpu.SemaphoreType.DMA((max(count, len(steps)),)),
-            pltpu.SemaphoreType.DMA((count,)),
         ],
-        compiler_params=pltpu.CompilerParams(vmem_limit_bytes=8 << 20),
+        compiler_params=pltpu.CompilerParams(vmem_limit_bytes=58 << 20),
         cost_estimate=pl.CostEstimate(
             flops=depth * lines * 2, bytes_accessed=depth * lines * 8, transcendentals=0
         ),
-    )(place, view, *([carried] if parts else []))
+    )(place, view, *([] if carried is None else [carried]))
     return (list(result[:count]) if parts else result[0]), result[-1]
 
 
-def line_slopes(arrived, place, gram, tables, match, spread):
+def line_slopes(arrived, place, gram, tables, match, sums):
     gather = isinstance(arrived, list)
+    spread = sums is not None
     count = len(arrived) if gather else arrived.shape[0]
-    depth = arrived[0].shape[0] - 8 if gather else arrived.shape[1]
-    width = arrived[0].shape[-1]
+    depth, width = arrived[0].shape[-2:]
     slots, block = tables.shape[0], tables.shape[2] // 2
     half = block // 2
     per = depth // half
     out_blocks = per * count
     size = 2 * slots
     ext_rows = gram.shape[0]
-
-    def body(place_ref, g_ref, t_ref, *refs):
+    cuts = 4
+    cut = slots // cuts
+
+    def body(place_ref, g_ref, table_ref, *refs):
         refs = list(refs)
+        sums_ref = refs.pop(0) if spread else None
         ins = [refs.pop(0) for _ in range(count if gather else 1)]
         outs = [refs.pop(0) for _ in range(count if spread else 1)]
+        t_ref, spec, extra, lines, result, table_sem, in_sem, out_sem, sum_sem = refs
+        load = [
+            pltpu.make_async_copy(
+                table_ref.at[pl.ds(c * cut, cut)], t_ref.at[pl.ds(c * cut, cut)], table_sem.at[c]
+            )
+            for c in range(cuts)
+        ]
         if gather:
-            energy_ref, lines, tiles, in_sem, sum_sem = [refs.pop(0)] + refs[-4:]
             copies = far_copies(count, place_ref[0], lines, ins, in_sem, False)
-            for k in range(count):
-                copies.append(
-                    pltpu.make_async_copy(
-                        ins[k].at[pl.ds(depth, 8)], tiles.at[k], sum_sem.at[k]
-                    )
-                )
-            run_copies(copies)
-            energy = tiles[0]
-            for k in range(1, count):
-                energy += tiles[k]
-            energy_ref[...] = energy
         else:
-            lines = ins[0]
-        spec, extra = refs[:2]
-        result = refs[2] if spread else outs[0]
+            copies = [pltpu.make_async_copy(ins[0], lines, in_sem.at[0])]
+        for copy in copies + load:
+            copy.start()
+        for copy in copies:
+            copy.wait()
 
         def at_block(b, at):
             return b // per, pl.ds((b % per) * half + at, GROUP), slice(None)
@@ -330,6 +325,8 @@
             return 0
 
         lax.fori_loop(0, half // GROUP, forward, 0)
+        for copy in load:
+            copy.wait()
 
         def product(f, blocks):
             high, mid, low = split_parts(jnp.concatenate(blocks, 0))
@@ -377,44 +374,47 @@
 
         lax.fori_loop(0, half // GROUP, backward, 0)
         if spread:
-            run_copies(far_copies(count, place_ref[0], result, outs, refs[3], True))
-
-    scratch = [pltpu.VMEM((slots, half, 2 * width), F32), pltpu.VMEM((half, width), F32)]
+            copies = far_copies(count, place_ref[0], result, outs, out_sem, True)
+            for k in range(count):
+                below = outs[k].at[pl.ds(depth, 8)]
+                copies.append(pltpu.make_async_copy(sums_ref, below, sum_sem.at[k]))
+        else:
+            copies = [pltpu.make_async_copy(result, outs[0], out_sem.at[0])]
+        run_copies(copies)
+
     if spread:
-        scratch += [pltpu.VMEM((count, depth, width), F32), pltpu.SemaphoreType.DMA((count,))]
-        out_specs = [ANY] * count
-        out_shape = [jax.ShapeDtypeStruct((depth, width), F32)] * count
+        out_shape = [jax.ShapeDtypeStruct((depth + 8, width), F32)] * count
     else:
-        out_specs = [VMEM]
         out_shape = [jax.ShapeDtypeStruct((count, depth, width), F32)]
-    if gather:
-        scratch += [
-            pltpu.VMEM((count, depth, width), F32),
-            pltpu.VMEM((count, 8, width), F32),
-            pltpu.SemaphoreType.DMA((count,)),
-            pltpu.SemaphoreType.DMA((count,)),
-        ]
-        out_specs = out_specs + [VMEM]
-        out_shape = out_shape + [jax.ShapeDtypeStruct((8, width), F32)]
+    stacked = pltpu.VMEM((count, depth, width), F32)
     out = pl.pallas_call(
         body,
         name="line_slopes",
-        in_specs=[SMEM, VMEM, VMEM] + ([ANY] * count if gather else [VMEM]),
-        out_specs=out_specs,
+        in_specs=[SMEM, VMEM, HBM] + [VMEM] * spread + [HBM] * (count if gather else 1),
+        out_specs=[HBM] * len(out_shape),
         out_shape=out_shape,
-        scratch_shapes=scratch,
-        compiler_params=pltpu.CompilerParams(vmem_limit_bytes=28 << 20),
+        scratch_shapes=[
+            pltpu.VMEM(tables.shape, BF),
+            pltpu.VMEM((slots, half, 2 * width), F32),
+            pltpu.VMEM((half, width), F32),
+            stacked,
+            stacked,
+            pltpu.SemaphoreType.DMA((cuts,)),
+            pltpu.SemaphoreType.DMA((count,)),
+            pltpu.SemaphoreType.DMA((count,)),
+            pltpu.SemaphoreType.DMA((count,)),
+        ],
+        compiler_params=pltpu.CompilerParams(vmem_limit_bytes=50 << 20),
         cost_estimate=pl.CostEstimate(
             flops=16 * size * block * block * width,
             bytes_accessed=8 * count * depth * width,
             transcendentals=0,
         ),
-    )(place, gram, tables, *(arrived if gather else [arrived]))
-    energy = out[-1] if gather else None
-    return (list(out[:count]) if spread else out[0]), energy
-
-
-def advect(view, chunk, arrived, place, rate, earlier):
+    )(place, gram, tables, *([sums] if spread else []), *(arrived if gather else [arrived]))
+    return list(out) if spread else out[0]
+
+
+def advect(view, chunk, arrived, place, points, energy, earlier):
     gather = isinstance(arrived, list)
     per, _, half, lines = view.shape
     span = lines // 2
@@ -424,10 +424,13 @@
     steps = [(b, q * quarter) for b in range(per) for q in range(2)]
     kept = 0 if earlier is None else 2
 
-    def body(place_ref, rate_ref, v_ref, *refs):
+    def body(place_ref, v_ref, *refs):
         refs = list(refs)[kept:]
+        energy_in = None if gather else refs.pop(0)
         ins = [refs.pop(0) for _ in range(count if gather else 1)]
-        s_ref, f_ref, v_buf, stacked, s_buf, f_buf, v_sem, in_sem, s_sem, f_sem = refs
+        s_ref, f_ref = refs.pop(0), refs.pop(0)
+        energy_out = refs.pop(0) if gather else None
+        v_buf, stacked, tiles, s_buf, f_buf, v_sem, in_sem, sum_sem, s_sem, f_sem = refs
 
         def part(ref, j):
             b, r = steps[j]
@@ -439,13 +442,25 @@
         ]
         if gather:
             pieces = far_copies(count, place_ref[0], stacked, ins, in_sem, False)
+            for k in range(count):
+                below = ins[k].at[pl.ds(depth, 8)]
+                pieces.append(pltpu.make_async_copy(below, tiles.at[k], sum_sem.at[k]))
         else:
             pieces = [pltpu.make_async_copy(ins[0], stacked, in_sem.at[0])]
         for copy in pieces + fields:
             copy.start()
         for copy in pieces:
             copy.wait()
-        rate = rate_ref[0, 0]
+        if gather:
+            tile = tiles[0]
+            for k in range(1, count):
+                tile += tiles[k]
+            energy_out[...] = tile
+        else:
+            tile = energy_in[...]
+        lane_sum = jnp.sum(tile, axis=0, keepdims=True)
+        mean_square = jnp.sum(lane_sum, axis=1, keepdims=True) / points
+        rate = jnp.broadcast_to(courant / jnp.sqrt(mean_square + epsilon), (quarter, width))
         leave = []
         for j, (b, r) in enumerate(steps):
             fields[j].wait()
@@ -465,30 +480,37 @@
         for copy in leave:
             copy.wait()
 
-    tiles = pltpu.VMEM((len(steps), 2, quarter, span), F32)
+    buffer = pltpu.VMEM((len(steps), 2, quarter, span), F32)
     step_sem = pltpu.SemaphoreType.DMA((len(steps),))
-    return pl.pallas_call(
+    piece_sem = pltpu.SemaphoreType.DMA((count,))
+    out = pl.pallas_call(
         body,
         name="advect",
-        in_specs=[SMEM, SMEM, ANY] + [ANY] * kept + [ANY] * (count if gather else 1),
-        out_specs=[ANY, ANY],
-        out_shape=[jax.ShapeDtypeStruct(view.shape, F32)] * 2,
+        in_specs=[SMEM, HBM]
+        + [HBM] * kept
+        + ([HBM] * count if gather else [VMEM, HBM]),
+        out_specs=[HBM, HBM] + [VMEM] * gather,
+        out_shape=[jax.ShapeDtypeStruct(view.shape, F32)] * 2
+        + [jax.ShapeDtypeStruct((8, width), F32)] * gather,
         scratch_shapes=[
-            tiles,
+            buffer,
             pltpu.VMEM((count, depth, width), F32),
-            tiles,
-            tiles,
+            pltpu.VMEM((count, 8, width), F32),
+            buffer,
+            buffer,
             step_sem,
-            pltpu.SemaphoreType.DMA((count,)),
+            piece_sem,
+            piece_sem,
             step_sem,
             step_sem,
         ],
-        input_output_aliases={3: 0, 4: 1} if kept else {},
+        input_output_aliases={2: 0, 3: 1} if kept else {},
         compiler_params=pltpu.CompilerParams(vmem_limit_bytes=12 << 20),
         cost_estimate=pl.CostEstimate(
             flops=depth * lines * 3, bytes_accessed=depth * lines * 16, transcendentals=0
         ),
-    )(place, rate, view, *(earlier or ()), *(arrived if gather else [arrived]))
+    )(place, view, *(earlier or ()), *(arrived if gather else [energy, arrived]))
+    return out[:2], (out[2] if gather else energy)
 
 
 def exchange(pieces, axis):
@@ -527,23 +549,23 @@
     size = transform_size(2 * out_blocks)
     view = velocity.reshape(row_count // block, 2, half, line_total)
 
-    first, sums = pack(view, 0, gx_count, place, None)
+    points = row_count * line_total * gx_count * ga_count
+
+    first, sums = pack(view, 0, gx_count, place, None, True)
     first = exchange(first, "gx")
-    second, _ = pack(view, 1, gx_count, place, sums)
+    second, sums = pack(view, 1, gx_count, place, sums, False)
     second = exchange(second, "gx")
+    sums = total_over(sums, "ga")
     spectrum = slope_spectrum(total + cont, block, out_blocks, size)
     tables = toeplitz_tables(jnp.asarray(spectrum), block)
     gram = jnp.concatenate([left_gram, right_gram], axis=1)
     gram = jnp.pad(gram, ((0, -cont % 8), (0, 0)))
-    first, _ = line_slopes(first, place, gram, tables, match, False)
+    first = line_slopes(first, place, gram, tables, match, sums)
     first = exchange(first, "gx")
-    second, energy = line_slopes(second, place, gram, tables, match, True)
+    second = line_slopes(second, place, gram, tables, match, None)
     second = exchange(second, "gx")
-    energy = total_over(energy, "ga")
-    mean_square = jnp.sum(energy) / (row_count * line_total * gx_count * ga_count)
-    advect_rate = (courant / jnp.sqrt(mean_square + epsilon)).reshape(1, 1)
-    done = advect(view, 0, first, place, advect_rate, None)
-    done = advect(view, 1, second, place, advect_rate, done)
+    done, energy = advect(view, 0, first, place, points, None, None)
+    done, _ = advect(view, 1, second, place, points, energy, done)
     return tuple(part.reshape(row_count, line_total) for part in done)
 
 

time: 216 us -> 216 us (level)
  local copies, waits for them, and re-layouts: 22.4 us -> 0.29 us
  Pallas kernels: 48.7 us -> 62 us
  waiting for transfers between devices: 72.1 us -> 77.9 us
  starting transfers between devices: 70.4 us -> 73.8 us
    unnamed x54 -> x42, local copies, waits for them, and re-layouts: 22.4 us -> 0.29 us
    pallas_call x4, Pallas kernels: 36.1 us -> 43 us  [the longest x2 34.2 us: line_slopes(): pl.pallas_call(body, name='line_slopes', in_specs=[SMEM, VMEM, HBM] + [VM...]
    ppermute x30, waiting for transfers between devices: 51.2 us -> 57.8 us  [exchange(): lax.ppermute(pieces[k], axis, [(i, (i + k) % count) for i in range(count)])]
    pallas_call x1, Pallas kernels: 6.92 us -> 11.5 us  [toeplitz_tables(): pl.pallas_call(body, name='toeplitz_tables', out_shape=jax.ShapeDtypeStru...]
    ppermute x30, starting transfers between devices: 52 us -> 55.5 us  [exchange(): lax.ppermute(pieces[k], axis, [(i, (i + k) % count) for i in range(count)])]
  transfers between devices with their start and end apart: 33 -> 33, of which waited for: 10 -> 13; matrix products, arithmetic and copies ran while one was open for 0% -> 0% of each run, Pallas kernels for 15% -> 16%
where the time goes in v1:
time: 216 us; the launch traced here: 215 us
  waiting for transfers between devices  77.9 us (36%)
  starting transfers between devices  73.8 us (34%)
  Pallas kernels  62 us (29%)
    ppermute x30, waiting for transfers between devices, exchange(): lax.ppermute(pieces[k], axis, [(i, (i + k) % count) for i in range(count)])  57.8 us
    ppermute x30, starting transfers between devices, exchange(): lax.ppermute(pieces[k], axis, [(i, (i + k) % count) for i in range(count)])  55.5 us
    pallas_call x2, Pallas kernels, line_slopes(): pl.pallas_call(body, name='line_slopes', in_specs=[SMEM, VMEM, HBM] + [VM...  34.2 us
    all_to_all x2, waiting for transfers between devices, exchange(): return lax.all_to_all(pieces, axis, split_axis=0, concat_axis=0, tiled=True)  20.1 us
    all_to_all x2, starting transfers between devices, exchange(): return lax.all_to_all(pieces, axis, split_axis=0, concat_axis=0, tiled=True)  16.7 us
    pallas_call x1, Pallas kernels, toeplitz_tables(): pl.pallas_call(body, name='toeplitz_tables', out_shape=jax.ShapeDtypeStru...  11.5 us
    pallas_call x2, Pallas kernels, advect(): pl.pallas_call(body, name='advect', in_specs=[SMEM, HBM] + [HBM] * kept +...  8.72 us
    pallas_call x2, Pallas kernels, pack(): pl.pallas_call(body, name='pack_pieces' if parts else 'pack_stacked', in_...  7.61 us
  transfers between devices with their start and end apart: 33, of which 13 were waited for; matrix products, arithmetic and copies ran while one was open for 0% of the time, Pallas kernels for 16%

profile of v1, /device:TPU:0, one launch (start us, length us, event | category | flops | bytes accessed | tf_op | source)
XLA Modules:
  0.0 215.0 jit_solution(8676411116945411194)
XLA Ops:
  0.6 3.7 %pack_pieces.1 = (f32[192,128]{1,0:T(8,128)}, f32[192,128]{1,0:T(8,128)}, f32[192,128]{1,0:T(8,128)}, f32[192,128]{1,0:T(8,128)}, f32[192,128]{1,0:T(8,128)}, /*...) custom-call(s32[1]{0:T(128)} %bitcast.place_ref, ...), custom_call_target="tpu_custom_call" | custom-call | flops 786432 | bytes 3145728 | tf_op jit(solution)/shard_map/pack_pieces/pallas_call | solution.py:247
  4.3 3.9 %pack_stacked.1 = (f32[16,192,128]{2,1,0:T(8,128)}, f32[8,128]{1,0:T(8,128)}) custom-call(s32[1]{0:T(128)} %bitcast.place_ref, f32[3,2,64,2048]{3,2,1,0:T(8,128)} %bitcast.5, f32[8,128]{1,0:T(8,128)} %get-tuple-element.42.refs_0_), custom_call_target="tpu_custom_call" | custom-call | flops 786432 | bytes 3145728 | tf_op jit(solution)/shard_map/pack_stacked/pallas_call | solution.py:247
  8.3 7.4 %all-to-all-start = ((f32[16,192,128]{2,1,0:T(8,128)}), f32[16,192,128]{2,1,0:T(8,128)S(1)}, u32[]{:S(2)}, u32[]{:S(2)}) async-start(f32[16,192,128]{2,1,0:T(8,128)} %get-tuple-element.79), calls=%async_computation | async-start | bytes 3145728 | tf_op jit(solution)/shard_map/all_to_all | solution.py:518
  15.9 11.5 %toeplitz_tables.1.table_ref = bf16[48,384,256]{2,1,0:T(8,128)(2,1)} custom-call(f32[96,256]{1,0:T(8,128)} %constant.11.clone.w_ref), custom_call_target="tpu_custom_call" | custom-call | flops 25165824 | bytes 9437184 | tf_op jit(solution)/shard_map/toeplitz_tables/pallas_call | solution.py:159
  27.5 20.1 %all-to-all-done.refs_0_ = f32[16,192,128]{2,1,0:T(8,128)S(1)} async-done(((f32[16,192,128]{2,1,0:T(8,128)}), f32[16,192,128]{2,1,0:T(8,128)S(1)}, u32[]{:S(2)}, u32[]{:S(2)}) %all-to-all-start) | async-done | bytes 1572896 | tf_op jit(solution)/shard_map/all_to_all | solution.py:518
  47.6 15.3 %line_slopes.3 = f32[16,192,128]{2,1,0:T(8,128)} custom-call(s32[1]{0:T(128)} %bitcast.place_ref, f32[32,10]{1,0:T(8,128)S(1)} %select_maximum_fusion.g_ref, bf16[48,384,256]{2,1,0:T(8,128)(2,1)} %toeplitz_tables.1.table_ref, f32[16,192,128]{2,1,0:T(8,128)S(1)} %all-to-all-done.refs_0_), custom_call_target="tpu_custom_call" | custom-call | flops 3221225472 | bytes 3145728 | tf_op jit(solution)/shard_map/line_slopes/pallas_call | solution.py:390
  63.1 9.3 %all-to-all-start.1 = ((f32[16,192,128]{2,1,0:T(8,128)}), f32[16,192,128]{2,1,0:T(8,128)}, u32[]{:S(2)}, u32[]{:S(2)}) async-start(f32[16,192,128]{2,1,0:T(8,128)} %line_slopes.3), calls=%async_computation.1 | async-start | bytes 3145728 | tf_op jit(solution)/shard_map/all_to_all | solution.py:518
  75.9 2.3 %collective-permute-start.3 = (f32[192,128]{1,0:T(8,128)S(1)}, f32[192,128]{1,0:T(8,128)S(1)}, u32[]{:S(2)}, u32[]{:S(2)}) collective-permute-start(f32[192,128]{1,0:T(8,128)S(1)} %copy-done.17), channel_id=1, source_target_pairs={{0,6},{2,8},{4,10},{6,12},{8,14},{10,16},{12,18},{14,20},{16,22},{... | collective-permute-start | bytes 294920 | tf_op jit(solution)/shard_map/ppermute | solution.py:522
  79.7 25.5 %collective-permute-done.1.refs_2_ = f32[192,128]{1,0:T(8,128)S(1)} collective-permute-done((f32[192,128]{1,0:T(8,128)S(1)}, f32[192,128]{1,0:T(8,128)S(1)}, u32[]{:S(2)}, u32[]{:S(2)}) %collective-permute-start.1) | collective-permute-done | bytes 98336 | tf_op jit(solution)/shard_map/ppermute | solution.py:522
  106.4 9.8 %collective-permute-start.7 = (f32[192,128]{1,0:T(8,128)S(1)}, f32[192,128]{1,0:T(8,128)S(1)}, u32[]{:S(2)}, u32[]{:S(2)}) collective-permute-start(f32[192,128]{1,0:T(8,128)S(1)} %copy-done.13), channel_id=1, source_target_pairs={{0,14},{2,16},{4,18},{6,20},{8,22},{10,24},{12,26},{14,28},{16,30}... | collective-permute-start | bytes 294920 | tf_op jit(solution)/shard_map/ppermute | solution.py:522
  119.8 8.6 %collective-permute-done.5.refs_6_ = f32[192,128]{1,0:T(8,128)S(1)} collective-permute-done((f32[192,128]{1,0:T(8,128)S(1)}, f32[192,128]{1,0:T(8,128)S(1)}, u32[]{:S(2)}, u32[]{:S(2)}) %collective-permute-start.5) | collective-permute-done | bytes 98336 | tf_op jit(solution)/shard_map/ppermute | solution.py:522
  129.8 3.4 %collective-permute-start.12 = (f32[192,128]{1,0:T(8,128)S(1)}, f32[192,128]{1,0:T(8,128)S(1)}, u32[]{:S(2)}, u32[]{:S(2)}) collective-permute-start(f32[192,128]{1,0:T(8,128)S(1)} %copy-done.8), channel_id=1, source_target_pairs={{0,24},{2,26},{4,28},{6,30},{8,0},{10,2},{12,4},{14,6},{16,8},{18,... | collective-permute-start | bytes 294920 | tf_op jit(solution)/shard_map/ppermute | solution.py:522
  133.2 6.0 %collective-permute-start.13 = (f32[192,128]{1,0:T(8,128)S(1)}, f32[192,128]{1,0:T(8,128)S(1)}, u32[]{:S(2)}, u32[]{:S(2)}) collective-permute-start(f32[192,128]{1,0:T(8,128)S(1)} %copy-done.7), channel_id=1, source_target_pairs={{0,26},{2,28},{4,30},{6,0},{8,2},{10,4},{12,6},{14,8},{16,10},{18,... | collective-permute-start | bytes 294920 | tf_op jit(solution)/shard_map/ppermute | solution.py:522
  139.2 2.4 %collective-permute-start.14 = (f32[192,128]{1,0:T(8,128)S(1)}, f32[192,128]{1,0:T(8,128)S(1)}, u32[]{:S(2)}, u32[]{:S(2)}) collective-permute-start(f32[192,128]{1,0:T(8,128)S(1)} %copy-done.6), channel_id=1, source_target_pairs={{0,28},{2,30},{4,0},{6,2},{8,4},{10,6},{12,8},{14,10},{16,12},{18,... | collective-permute-start | bytes 294920 | tf_op jit(solution)/shard_map/ppermute | solution.py:522
  146.3 18.9 %line_slopes.2 = (f32[200,128]{1,0:T(8,128)S(1)}, f32[200,128]{1,0:T(8,128)S(1)}, f32[200,128]{1,0:T(8,128)S(1)}, f32[200,128]{1,0:T(8,128)S(1)}, f32[200,128]{1...) custom-call(s32[1]{0:T(128)} %bitcast.place_ref, ...), custom_call_target="tpu_custom_call" | custom-call | flops 3221225472 | bytes 3145728 | tf_op jit(solution)/shard_map/line_slopes/pallas_call | solution.py:390
  168.2 3.2 %collective-permute-start.20 = (f32[200,128]{1,0:T(8,128)S(1)}, f32[200,128]{1,0:T(8,128)S(1)}, u32[]{:S(2)}, u32[]{:S(2)}) collective-permute-start(f32[200,128]{1,0:T(8,128)S(1)} %get-tuple-element.65), channel_id=1, source_target_pairs={{0,10},{2,12},{4,14},{6,16},{8,18},{10,20},{12,22},{14,24},{16,26}... | collective-permute-start | bytes 307208 | tf_op jit(solution)/shard_map/ppermute | solution.py:522
  172.3 3.0 %collective-permute-done.17.refs_2_ = f32[200,128]{1,0:T(8,128)S(1)} collective-permute-done((f32[200,128]{1,0:T(8,128)S(1)}, f32[200,128]{1,0:T(8,128)S(1)}, u32[]{:S(2)}, u32[]{:S(2)}) %collective-permute-start.17) | collective-permute-done | bytes 102432 | tf_op jit(solution)/shard_map/ppermute | solution.py:522
  176.5 3.0 %collective-permute-start.24 = (f32[200,128]{1,0:T(8,128)S(1)}, f32[200,128]{1,0:T(8,128)S(1)}, u32[]{:S(2)}, u32[]{:S(2)}) collective-permute-start(f32[200,128]{1,0:T(8,128)S(1)} %get-tuple-element.69), channel_id=1, source_target_pairs={{0,18},{2,20},{4,22},{6,24},{8,26},{10,28},{12,30},{14,0},{16,2},{... | collective-permute-start | bytes 307208 | tf_op jit(solution)/shard_map/ppermute | solution.py:522
  179.5 11.6 %collective-permute-done.20.refs_5_ = f32[200,128]{1,0:T(8,128)S(1)} collective-permute-done((f32[200,128]{1,0:T(8,128)S(1)}, f32[200,128]{1,0:T(8,128)S(1)}, u32[]{:S(2)}, u32[]{:S(2)}) %collective-permute-start.20) | collective-permute-done | bytes 102432 | tf_op jit(solution)/shard_map/ppermute | solution.py:522
  192.6 3.2 %collective-permute-start.27 = (f32[200,128]{1,0:T(8,128)S(1)}, f32[200,128]{1,0:T(8,128)S(1)}, u32[]{:S(2)}, u32[]{:S(2)}) collective-permute-start(f32[200,128]{1,0:T(8,128)S(1)} %get-tuple-element.72), channel_id=1, source_target_pairs={{0,24},{2,26},{4,28},{6,30},{8,0},{10,2},{12,4},{14,6},{16,8},{18,... | collective-permute-start | bytes 307208 | tf_op jit(solution)/shard_map/ppermute | solution.py:522
  195.9 2.7 %collective-permute-start.28 = (f32[200,128]{1,0:T(8,128)S(1)}, f32[200,128]{1,0:T(8,128)S(1)}, u32[]{:S(2)}, u32[]{:S(2)}) collective-permute-start(f32[200,128]{1,0:T(8,128)S(1)} %get-tuple-element.73), channel_id=1, source_target_pairs={{0,26},{2,28},{4,30},{6,0},{8,2},{10,4},{12,6},{14,8},{16,10},{18,... | collective-permute-start | bytes 307208 | tf_op jit(solution)/shard_map/ppermute | solution.py:522
  198.6 2.8 %collective-permute-start.29 = (f32[200,128]{1,0:T(8,128)S(1)}, f32[200,128]{1,0:T(8,128)S(1)}, u32[]{:S(2)}, u32[]{:S(2)}) collective-permute-start(f32[200,128]{1,0:T(8,128)S(1)} %get-tuple-element.74), channel_id=1, source_target_pairs={{0,28},{2,30},{4,0},{6,2},{8,4},{10,6},{12,8},{14,10},{16,12},{18,... | collective-permute-start | bytes 307208 | tf_op jit(solution)/shard_map/ppermute | solution.py:522
  206.2 5.0 %advect.2 = (f32[3,2,64,2048]{3,2,1,0:T(8,128)}, f32[3,2,64,2048]{3,2,1,0:T(8,128)}, f32[8,128]{1,0:T(8,128)S(1)}) custom-call(s32[1]{0:T(128)} %bitcast.place_ref, f32[3,2,64,2048]{3,2,1,0:T(8,128)S(1)} %bitcast.6, f32[200,128]{1,0:T(8,128)S(1)} %get-tuple-element.60.refs_0_, f32[200,128]{1,0:T(8,128)S(1)} %collective-permute-done.16.refs_1_, ...), custom_call_target="tpu_custom_call" | custom-call | flops 1179648 | bytes 6291456 | tf_op jit(solution)/shard_map/advect/pallas_call | solution.py:486
  211.2 3.7 %advect.3 = (f32[3,2,64,2048]{3,2,1,0:T(8,128)}, f32[3,2,64,2048]{3,2,1,0:T(8,128)}) custom-call(s32[1]{0:T(128)} %bitcast.place_ref, f32[3,2,64,2048]{3,2,1,0:T(8,128)S(1)} %bitcast.7, f32[3,2,64,2048]{3,2,1,0:T(8,128)} %get-tuple-element.76.refs_0_, f32[3,2,64,2048]{3,2,1,0:T(8,128)} %get-tuple-element.77.refs_1_, ...), custom_call_target="tpu_custom_call", output_to_operand_aliasing={{0}: (2, {}), {1}: (3, {})} | custom-call | flops 1179648 | bytes 6291456 | tf_op jit(solution)/shard_map/advect/pallas_call | solution.py:486
  (93 shorter events, 27.7 us)
Async XLA Ops:
  8.3 39.3 %all-to-all-start = ((f32[16,192,128]{2,1,0:T(8,128)}), f32[16,192,128]{2,1,0:T(8,128)S(1)}, u32[]{:S(2)}, u32[]{:S(2)}) async-start(f32[16,192,128]{2,1,0:T(8,128)} %get-tuple-element.79), calls=%async_computation | async-start | bytes 3145728 | tf_op jit(solution)/shard_map/all_to_all | solution.py:518
  63.1 148.2 %all-to-all-start.1 = ((f32[16,192,128]{2,1,0:T(8,128)}), f32[16,192,128]{2,1,0:T(8,128)}, u32[]{:S(2)}, u32[]{:S(2)}) async-start(f32[16,192,128]{2,1,0:T(8,128)} %line_slopes.3), calls=%async_computation.1 | async-start | bytes 3145728 | tf_op jit(solution)/shard_map/all_to_all | solution.py:518
  73.9 31.3 %collective-permute-start.1 = (f32[192,128]{1,0:T(8,128)S(1)}, f32[192,128]{1,0:T(8,128)S(1)}, u32[]{:S(2)}, u32[]{:S(2)}) collective-permute-start(f32[192,128]{1,0:T(8,128)S(1)} %copy-done.19), channel_id=1, source_target_pairs={{0,2},{2,4},{4,6},{6,8},{8,10},{10,12},{12,14},{14,16},{16,18},{18... | collective-permute-start | bytes 294920 | tf_op jit(solution)/shard_map/ppermute | solution.py:522
  74.0 32.4 %collective-permute-start.2 = (f32[192,128]{1,0:T(8,128)S(1)}, f32[192,128]{1,0:T(8,128)S(1)}, u32[]{:S(2)}, u32[]{:S(2)}) collective-permute-start(f32[192,128]{1,0:T(8,128)S(1)} %copy-done.18), channel_id=1, source_target_pairs={{0,4},{2,6},{4,8},{6,10},{8,12},{10,14},{12,16},{14,18},{16,20},{1... | collective-permute-start | bytes 294920 | tf_op jit(solution)/shard_map/ppermute | solution.py:522
  75.9 40.3 %collective-permute-start.3 = (f32[192,128]{1,0:T(8,128)S(1)}, f32[192,128]{1,0:T(8,128)S(1)}, u32[]{:S(2)}, u32[]{:S(2)}) collective-permute-start(f32[192,128]{1,0:T(8,128)S(1)} %copy-done.17), channel_id=1, source_target_pairs={{0,6},{2,8},{4,10},{6,12},{8,14},{10,16},{12,18},{14,20},{16,22},{... | collective-permute-start | bytes 294920 | tf_op jit(solution)/shard_map/ppermute | solution.py:522
  78.2 39.4 %collective-permute-start.4 = (f32[192,128]{1,0:T(8,128)S(1)}, f32[192,128]{1,0:T(8,128)S(1)}, u32[]{:S(2)}, u32[]{:S(2)}) collective-permute-start(f32[192,128]{1,0:T(8,128)S(1)} %copy-done.16), channel_id=1, source_target_pairs={{0,8},{2,10},{4,12},{6,14},{8,16},{10,18},{12,20},{14,22},{16,24},... | collective-permute-start | bytes 294920 | tf_op jit(solution)/shard_map/ppermute | solution.py:522
  79.7 48.8 %collective-permute-start.5 = (f32[192,128]{1,0:T(8,128)S(1)}, f32[192,128]{1,0:T(8,128)S(1)}, u32[]{:S(2)}, u32[]{:S(2)}) collective-permute-start(f32[192,128]{1,0:T(8,128)S(1)} %copy-done.15), channel_id=1, source_target_pairs={{0,10},{2,12},{4,14},{6,16},{8,18},{10,20},{12,22},{14,24},{16,26}... | collective-permute-start | bytes 294920 | tf_op jit(solution)/shard_map/ppermute | solution.py:522
  105.3 24.4 %collective-permute-start.6 = (f32[192,128]{1,0:T(8,128)S(1)}, f32[192,128]{1,0:T(8,128)S(1)}, u32[]{:S(2)}, u32[]{:S(2)}) collective-permute-start(f32[192,128]{1,0:T(8,128)S(1)} %copy-done.14), channel_id=1, source_target_pairs={{0,12},{2,14},{4,16},{6,18},{8,20},{10,22},{12,24},{14,26},{16,28}... | collective-permute-start | bytes 294920 | tf_op jit(solution)/shard_map/ppermute | solution.py:522
  106.4 23.4 %collective-permute-start.7 = (f32[192,128]{1,0:T(8,128)S(1)}, f32[192,128]{1,0:T(8,128)S(1)}, u32[]{:S(2)}, u32[]{:S(2)}) collective-permute-start(f32[192,128]{1,0:T(8,128)S(1)} %copy-done.13), channel_id=1, source_target_pairs={{0,14},{2,16},{4,18},{6,20},{8,22},{10,24},{12,26},{14,28},{16,30}... | collective-permute-start | bytes 294920 | tf_op jit(solution)/shard_map/ppermute | solution.py:522
  116.2 17.0 %collective-permute-start.8 = (f32[192,128]{1,0:T(8,128)S(1)}, f32[192,128]{1,0:T(8,128)S(1)}, u32[]{:S(2)}, u32[]{:S(2)}) collective-permute-start(f32[192,128]{1,0:T(8,128)S(1)} %copy-done.12), channel_id=1, source_target_pairs={{0,16},{2,18},{4,20},{6,22},{8,24},{10,26},{12,28},{14,30},{16,0},... | collective-permute-start | bytes 294920 | tf_op jit(solution)/shard_map/ppermute | solution.py:522
  117.5 21.7 %collective-permute-start.9 = (f32[192,128]{1,0:T(8,128)S(1)}, f32[192,128]{1,0:T(8,128)S(1)}, u32[]{:S(2)}, u32[]{:S(2)}) collective-permute-start(f32[192,128]{1,0:T(8,128)S(1)} %copy-done.11), channel_id=1, source_target_pairs={{0,18},{2,20},{4,22},{6,24},{8,26},{10,28},{12,30},{14,0},{16,2},{... | collective-permute-start | bytes 294920 | tf_op jit(solution)/shard_map/ppermute | solution.py:522
  128.5 13.1 %collective-permute-start.10 = (f32[192,128]{1,0:T(8,128)S(1)}, f32[192,128]{1,0:T(8,128)S(1)}, u32[]{:S(2)}, u32[]{:S(2)}) collective-permute-start(f32[192,128]{1,0:T(8,128)S(1)} %copy-done.10), channel_id=1, source_target_pairs={{0,20},{2,22},{4,24},{6,26},{8,28},{10,30},{12,0},{14,2},{16,4},{1... | collective-permute-start | bytes 294920 | tf_op jit(solution)/shard_map/ppermute | solution.py:522
  129.6 14.0 %collective-permute-start.11 = (f32[192,128]{1,0:T(8,128)S(1)}, f32[192,128]{1,0:T(8,128)S(1)}, u32[]{:S(2)}, u32[]{:S(2)}) collective-permute-start(f32[192,128]{1,0:T(8,128)S(1)} %copy-done.9), channel_id=1, source_target_pairs={{0,22},{2,24},{4,26},{6,28},{8,30},{10,0},{12,2},{14,4},{16,6},{18... | collective-permute-start | bytes 294920 | tf_op jit(solution)/shard_map/ppermute | solution.py:522
  129.8 13.8 %collective-permute-start.12 = (f32[192,128]{1,0:T(8,128)S(1)}, f32[192,128]{1,0:T(8,128)S(1)}, u32[]{:S(2)}, u32[]{:S(2)}) collective-permute-start(f32[192,128]{1,0:T(8,128)S(1)} %copy-done.8), channel_id=1, source_target_pairs={{0,24},{2,26},{4,28},{6,30},{8,0},{10,2},{12,4},{14,6},{16,8},{18,... | collective-permute-start | bytes 294920 | tf_op jit(solution)/shard_map/ppermute | solution.py:522
  133.2 10.4 %collective-permute-start.13 = (f32[192,128]{1,0:T(8,128)S(1)}, f32[192,128]{1,0:T(8,128)S(1)}, u32[]{:S(2)}, u32[]{:S(2)}) collective-permute-start(f32[192,128]{1,0:T(8,128)S(1)} %copy-done.7), channel_id=1, source_target_pairs={{0,26},{2,28},{4,30},{6,0},{8,2},{10,4},{12,6},{14,8},{16,10},{18,... | collective-permute-start | bytes 294920 | tf_op jit(solution)/shard_map/ppermute | solution.py:522
  166.7 8.6 %collective-permute-start.17 = (f32[200,128]{1,0:T(8,128)S(1)}, f32[200,128]{1,0:T(8,128)S(1)}, u32[]{:S(2)}, u32[]{:S(2)}) collective-permute-start(f32[200,128]{1,0:T(8,128)S(1)} %get-tuple-element.62), channel_id=1, source_target_pairs={{0,4},{2,6},{4,8},{6,10},{8,12},{10,14},{12,16},{14,18},{16,20},{1... | collective-permute-start | bytes 307208 | tf_op jit(solution)/shard_map/ppermute | solution.py:522
  168.2 22.9 %collective-permute-start.20 = (f32[200,128]{1,0:T(8,128)S(1)}, f32[200,128]{1,0:T(8,128)S(1)}, u32[]{:S(2)}, u32[]{:S(2)}) collective-permute-start(f32[200,128]{1,0:T(8,128)S(1)} %get-tuple-element.65), channel_id=1, source_target_pairs={{0,10},{2,12},{4,14},{6,16},{8,18},{10,20},{12,22},{14,24},{16,26}... | collective-permute-start | bytes 307208 | tf_op jit(solution)/shard_map/ppermute | solution.py:522
  172.2 19.2 %collective-permute-start.21 = (f32[200,128]{1,0:T(8,128)S(1)}, f32[200,128]{1,0:T(8,128)S(1)}, u32[]{:S(2)}, u32[]{:S(2)}) collective-permute-start(f32[200,128]{1,0:T(8,128)S(1)} %get-tuple-element.66), channel_id=1, source_target_pairs={{0,12},{2,14},{4,16},{6,18},{8,20},{10,22},{12,24},{14,26},{16,28}... | collective-permute-start | bytes 307208 | tf_op jit(solution)/shard_map/ppermute | solution.py:522
  175.2 17.4 %collective-permute-start.22 = (f32[200,128]{1,0:T(8,128)S(1)}, f32[200,128]{1,0:T(8,128)S(1)}, u32[]{:S(2)}, u32[]{:S(2)}) collective-permute-start(f32[200,128]{1,0:T(8,128)S(1)} %get-tuple-element.67), channel_id=1, source_target_pairs={{0,14},{2,16},{4,18},{6,20},{8,22},{10,24},{12,26},{14,28},{16,30}... | collective-permute-start | bytes 307208 | tf_op jit(solution)/shard_map/ppermute | solution.py:522
  175.2 20.6 %collective-permute-start.23 = (f32[200,128]{1,0:T(8,128)S(1)}, f32[200,128]{1,0:T(8,128)S(1)}, u32[]{:S(2)}, u32[]{:S(2)}) collective-permute-start(f32[200,128]{1,0:T(8,128)S(1)} %get-tuple-element.68), channel_id=1, source_target_pairs={{0,16},{2,18},{4,20},{6,22},{8,24},{10,26},{12,28},{14,30},{16,0},... | collective-permute-start | bytes 307208 | tf_op jit(solution)/shard_map/ppermute | solution.py:522
  176.5 22.1 %collective-permute-start.24 = (f32[200,128]{1,0:T(8,128)S(1)}, f32[200,128]{1,0:T(8,128)S(1)}, u32[]{:S(2)}, u32[]{:S(2)}) collective-permute-start(f32[200,128]{1,0:T(8,128)S(1)} %get-tuple-element.69), channel_id=1, source_target_pairs={{0,18},{2,20},{4,22},{6,24},{8,26},{10,28},{12,30},{14,0},{16,2},{... | collective-permute-start | bytes 307208 | tf_op jit(solution)/shard_map/ppermute | solution.py:522
  191.2 10.2 %collective-permute-start.25 = (f32[200,128]{1,0:T(8,128)S(1)}, f32[200,128]{1,0:T(8,128)S(1)}, u32[]{:S(2)}, u32[]{:S(2)}) collective-permute-start(f32[200,128]{1,0:T(8,128)S(1)} %get-tuple-element.70), channel_id=1, source_target_pairs={{0,20},{2,22},{4,24},{6,26},{8,28},{10,30},{12,0},{14,2},{16,4},{1... | collective-permute-start | bytes 307208 | tf_op jit(solution)/shard_map/ppermute | solution.py:522
  191.3 11.9 %collective-permute-start.26 = (f32[200,128]{1,0:T(8,128)S(1)}, f32[200,128]{1,0:T(8,128)S(1)}, u32[]{:S(2)}, u32[]{:S(2)}) collective-permute-start(f32[200,128]{1,0:T(8,128)S(1)} %get-tuple-element.71), channel_id=1, source_target_pairs={{0,22},{2,24},{4,26},{6,28},{8,30},{10,0},{12,2},{14,4},{16,6},{18... | collective-permute-start | bytes 307208 | tf_op jit(solution)/shard_map/ppermute | solution.py:522
  192.6 10.6 %collective-permute-start.27 = (f32[200,128]{1,0:T(8,128)S(1)}, f32[200,128]{1,0:T(8,128)S(1)}, u32[]{:S(2)}, u32[]{:S(2)}) collective-permute-start(f32[200,128]{1,0:T(8,128)S(1)} %get-tuple-element.72), channel_id=1, source_target_pairs={{0,24},{2,26},{4,28},{6,30},{8,0},{10,2},{12,4},{14,6},{16,8},{18,... | collective-permute-start | bytes 307208 | tf_op jit(solution)/shard_map/ppermute | solution.py:522
  (29 other events, 919.9 us)

commit v2 on v1

--- a/solution.py
+++ b/solution.py
@@ -142,8 +142,10 @@
 
 def toeplitz_tables(spectrum, block):
     slots = spectrum.shape[0] // 2
-
-    def body(w_ref, o_ref):
+    cuts = 4
+    cut = slots // cuts
+
+    def body(w_ref, o_ref, made, sem):
         def fill(f, _):
             for side in range(2):
                 lane = w_ref[pl.ds(2 * f + side, 1), :]
@@ -151,15 +153,26 @@
                 rows = pltpu.roll(rows, 0, 1, stride=1, stride_axis=0)[:, block:]
                 high, mid, low = split_parts(rows)
                 for p, part in enumerate((mid, high, low)):
-                    o_ref[f, p * block : (p + 1) * block, side * block : (side + 1) * block] = part
+                    made[f, p * block : (p + 1) * block, side * block : (side + 1) * block] = part
             return 0
 
-        lax.fori_loop(0, slots, fill, 0)
-
+        leave = []
+        for c in range(cuts):
+            lax.fori_loop(c * cut, (c + 1) * cut, fill, 0, unroll=4)
+            part = pl.ds(c * cut, cut)
+            leave.append(pltpu.make_async_copy(made.at[part], o_ref.at[part], sem.at[c]))
+            leave[-1].start()
+        for copy in leave:
+            copy.wait()
+
+    shape = (slots, 3 * block, 2 * block)
     return pl.pallas_call(
         body,
         name="toeplitz_tables",
-        out_shape=jax.ShapeDtypeStruct((slots, 3 * block, 2 * block), BF),
+        in_specs=[VMEM],
+        out_specs=HBM,
+        out_shape=jax.ShapeDtypeStruct(shape, BF),
+        scratch_shapes=[pltpu.VMEM(shape, BF), pltpu.SemaphoreType.DMA((cuts,))],
         compiler_params=pltpu.CompilerParams(vmem_limit_bytes=58 << 20),
         cost_estimate=pl.CostEstimate(
             flops=slots * block * block * 32,
@@ -358,7 +371,7 @@
             product(f, [merge(re, im_s), merge(re_s, im), merge(-im, re_s), merge(-im_s, re)])
             return 0
 
-        lax.fori_loop(1, slots, multiply, 0, unroll=4)
+        lax.fori_loop(1, slots, multiply, 0, unroll=8)
 
         def backward(group, _):
             at = pl.multiple_of(group * GROUP, GROUP)
@@ -554,10 +567,11 @@
     first, sums = pack(view, 0, gx_count, place, None, True)
     first = exchange(first, "gx")
     second, sums = pack(view, 1, gx_count, place, sums, False)
-    second = exchange(second, "gx")
     sums = total_over(sums, "ga")
     spectrum = slope_spectrum(total + cont, block, out_blocks, size)
     tables = toeplitz_tables(jnp.asarray(spectrum), block)
+    second, tables = lax.optimization_barrier((second, tables))
+    second = exchange(second, "gx")
     gram = jnp.concatenate([left_gram, right_gram], axis=1)
     gram = jnp.pad(gram, ((0, -cont % 8), (0, 0)))
     first = line_slopes(first, place, gram, tables, match, sums)

time: 216 us -> 222 us (1.028)
  waiting for transfers between devices: 77.9 us -> 90.4 us
  Pallas kernels: 62 us -> 55.7 us
    all_to_all x2, waiting for transfers between devices: 20.1 us -> 31.6 us  [exchange(): return lax.all_to_all(pieces, axis, split_axis=0, concat_axis=0, tiled=True)]
    pallas_call x1, Pallas kernels: 11.5 us -> 6.53 us  [toeplitz_tables(): pl.pallas_call(body, name='toeplitz_tables', in_specs=[VMEM], out_specs=H...]
  transfers between devices with their start and end apart: 33 -> 33, of which waited for: 13 -> 13; matrix products, arithmetic and copies ran while one was open for 0% -> 0% of each run, Pallas kernels for 16% -> 10%
where the time goes in v2:
time: 222 us; the launch traced here: 221 us
  waiting for transfers between devices  90.4 us (41%)
  starting transfers between devices  73.8 us (33%)
  Pallas kernels  55.7 us (25%)
    ppermute x30, waiting for transfers between devices, exchange(): lax.ppermute(pieces[k], axis, [(i, (i + k) % count) for i in range(count)])  58.9 us
    ppermute x30, starting transfers between devices, exchange(): lax.ppermute(pieces[k], axis, [(i, (i + k) % count) for i in range(count)])  55.5 us
    pallas_call x2, Pallas kernels, line_slopes(): pl.pallas_call(body, name='line_slopes', in_specs=[SMEM, VMEM, HBM] + [VM...  32.9 us
    all_to_all x2, waiting for transfers between devices, exchange(): return lax.all_to_all(pieces, axis, split_axis=0, concat_axis=0, tiled=True)  31.6 us
    all_to_all x2, starting transfers between devices, exchange(): return lax.all_to_all(pieces, axis, split_axis=0, concat_axis=0, tiled=True)  16.7 us
    pallas_call x2, Pallas kernels, advect(): pl.pallas_call(body, name='advect', in_specs=[SMEM, HBM] + [HBM] * kept +...  8.72 us
    pallas_call x2, Pallas kernels, pack(): pl.pallas_call(body, name='pack_pieces' if parts else 'pack_stacked', in_...  7.6 us
    pallas_call x1, Pallas kernels, toeplitz_tables(): pl.pallas_call(body, name='toeplitz_tables', in_specs=[VMEM], out_specs=H...  6.53 us
  transfers between devices with their start and end apart: 33, of which 13 were waited for; matrix products, arithmetic and copies ran while one was open for 0% of the time, Pallas kernels for 10%

profile of v2, /device:TPU:0, one launch (start us, length us, event | category | flops | bytes accessed | tf_op | source)
XLA Modules:
  0.0 221.2 jit_solution(661258374331601401)
XLA Ops:
  0.6 3.7 %pack_pieces.1 = (f32[192,128]{1,0:T(8,128)}, f32[192,128]{1,0:T(8,128)}, f32[192,128]{1,0:T(8,128)}, f32[192,128]{1,0:T(8,128)}, f32[192,128]{1,0:T(8,128)}, /*...) custom-call(s32[1]{0:T(128)} %bitcast.place_ref, ...), custom_call_target="tpu_custom_call" | custom-call | flops 786432 | bytes 3145728 | tf_op jit(solution)/shard_map/pack_pieces/pallas_call | solution.py:260
  4.3 3.9 %pack_stacked.1 = (f32[16,192,128]{2,1,0:T(8,128)}, f32[8,128]{1,0:T(8,128)}) custom-call(s32[1]{0:T(128)} %bitcast.place_ref, f32[3,2,64,2048]{3,2,1,0:T(8,128)} %bitcast.5, f32[8,128]{1,0:T(8,128)} %get-tuple-element.44.refs_0_), custom_call_target="tpu_custom_call" | custom-call | flops 786432 | bytes 3145728 | tf_op jit(solution)/shard_map/pack_stacked/pallas_call | solution.py:260
  8.2 6.5 %toeplitz_tables.1.table_ref = bf16[48,384,256]{2,1,0:T(8,128)(2,1)} custom-call(f32[96,256]{1,0:T(8,128)} %constant.11.clone.w_ref), custom_call_target="tpu_custom_call" | custom-call | flops 25165824 | bytes 9437184 | tf_op jit(solution)/shard_map/toeplitz_tables/pallas_call | solution.py:169
  14.8 7.4 %all-to-all-start = ((f32[16,192,128]{2,1,0:T(8,128)}), f32[16,192,128]{2,1,0:T(8,128)S(1)}, u32[]{:S(2)}, u32[]{:S(2)}) async-start(f32[16,192,128]{2,1,0:T(8,128)} %get-tuple-element.83), calls=%async_computation | async-start | bytes 3145728 | tf_op jit(solution)/shard_map/all_to_all | solution.py:531
  22.5 31.6 %all-to-all-done.refs_0_ = f32[16,192,128]{2,1,0:T(8,128)S(1)} async-done(((f32[16,192,128]{2,1,0:T(8,128)}), f32[16,192,128]{2,1,0:T(8,128)S(1)}, u32[]{:S(2)}, u32[]{:S(2)}) %all-to-all-start) | async-done | bytes 1572896 | tf_op jit(solution)/shard_map/all_to_all | solution.py:531
  54.1 14.6 %line_slopes.3 = f32[16,192,128]{2,1,0:T(8,128)} custom-call(s32[1]{0:T(128)} %bitcast.place_ref, f32[32,10]{1,0:T(8,128)S(1)} %select_maximum_fusion.g_ref, bf16[48,384,256]{2,1,0:T(8,128)(2,1)} %toeplitz_tables.1.table_ref, f32[16,192,128]{2,1,0:T(8,128)S(1)} %all-to-all-done.refs_0_), custom_call_target="tpu_custom_call" | custom-call | flops 3221225472 | bytes 3145728 | tf_op jit(solution)/shard_map/line_slopes/pallas_call | solution.py:403
  68.9 9.3 %all-to-all-start.1 = ((f32[16,192,128]{2,1,0:T(8,128)}), f32[16,192,128]{2,1,0:T(8,128)}, u32[]{:S(2)}, u32[]{:S(2)}) async-start(f32[16,192,128]{2,1,0:T(8,128)} %line_slopes.3), calls=%async_computation.1 | async-start | bytes 3145728 | tf_op jit(solution)/shard_map/all_to_all | solution.py:531
  81.7 2.3 %collective-permute-start.3 = (f32[192,128]{1,0:T(8,128)S(1)}, f32[192,128]{1,0:T(8,128)S(1)}, u32[]{:S(2)}, u32[]{:S(2)}) collective-permute-start(f32[192,128]{1,0:T(8,128)S(1)} %copy-done.17), channel_id=1, source_target_pairs={{0,6},{2,8},{4,10},{6,12},{8,14},{10,16},{12,18},{14,20},{16,22},{... | collective-permute-start | bytes 294920 | tf_op jit(solution)/shard_map/ppermute | solution.py:535
  85.6 25.5 %collective-permute-done.1.refs_2_ = f32[192,128]{1,0:T(8,128)S(1)} collective-permute-done((f32[192,128]{1,0:T(8,128)S(1)}, f32[192,128]{1,0:T(8,128)S(1)}, u32[]{:S(2)}, u32[]{:S(2)}) %collective-permute-start.1) | collective-permute-done | bytes 98336 | tf_op jit(solution)/shard_map/ppermute | solution.py:535
  112.3 9.8 %collective-permute-start.7 = (f32[192,128]{1,0:T(8,128)S(1)}, f32[192,128]{1,0:T(8,128)S(1)}, u32[]{:S(2)}, u32[]{:S(2)}) collective-permute-start(f32[192,128]{1,0:T(8,128)S(1)} %copy-done.13), channel_id=1, source_target_pairs={{0,14},{2,16},{4,18},{6,20},{8,22},{10,24},{12,26},{14,28},{16,30}... | collective-permute-start | bytes 294920 | tf_op jit(solution)/shard_map/ppermute | solution.py:535
  123.4 2.3 %collective-permute-start.9 = (f32[192,128]{1,0:T(8,128)S(1)}, f32[192,128]{1,0:T(8,128)S(1)}, u32[]{:S(2)}, u32[]{:S(2)}) collective-permute-start(f32[192,128]{1,0:T(8,128)S(1)} %copy-done.11), channel_id=1, source_target_pairs={{0,18},{2,20},{4,22},{6,24},{8,26},{10,28},{12,30},{14,0},{16,2},{... | collective-permute-start | bytes 294920 | tf_op jit(solution)/shard_map/ppermute | solution.py:535
  125.7 8.6 %collective-permute-done.5.refs_6_ = f32[192,128]{1,0:T(8,128)S(1)} collective-permute-done((f32[192,128]{1,0:T(8,128)S(1)}, f32[192,128]{1,0:T(8,128)S(1)}, u32[]{:S(2)}, u32[]{:S(2)}) %collective-permute-start.5) | collective-permute-done | bytes 98336 | tf_op jit(solution)/shard_map/ppermute | solution.py:535
  135.7 3.4 %collective-permute-start.12 = (f32[192,128]{1,0:T(8,128)S(1)}, f32[192,128]{1,0:T(8,128)S(1)}, u32[]{:S(2)}, u32[]{:S(2)}) collective-permute-start(f32[192,128]{1,0:T(8,128)S(1)} %copy-done.8), channel_id=1, source_target_pairs={{0,24},{2,26},{4,28},{6,30},{8,0},{10,2},{12,4},{14,6},{16,8},{18,... | collective-permute-start | bytes 294920 | tf_op jit(solution)/shard_map/ppermute | solution.py:535
  139.1 6.0 %collective-permute-start.13 = (f32[192,128]{1,0:T(8,128)S(1)}, f32[192,128]{1,0:T(8,128)S(1)}, u32[]{:S(2)}, u32[]{:S(2)}) collective-permute-start(f32[192,128]{1,0:T(8,128)S(1)} %copy-done.7), channel_id=1, source_target_pairs={{0,26},{2,28},{4,30},{6,0},{8,2},{10,4},{12,6},{14,8},{16,10},{18,... | collective-permute-start | bytes 294920 | tf_op jit(solution)/shard_map/ppermute | solution.py:535
  145.1 2.4 %collective-permute-start.14 = (f32[192,128]{1,0:T(8,128)S(1)}, f32[192,128]{1,0:T(8,128)S(1)}, u32[]{:S(2)}, u32[]{:S(2)}) collective-permute-start(f32[192,128]{1,0:T(8,128)S(1)} %copy-done.6), channel_id=1, source_target_pairs={{0,28},{2,30},{4,0},{6,2},{8,4},{10,6},{12,8},{14,10},{16,12},{18,... | collective-permute-start | bytes 294920 | tf_op jit(solution)/shard_map/ppermute | solution.py:535
  152.1 18.2 %line_slopes.2 = (f32[200,128]{1,0:T(8,128)S(1)}, f32[200,128]{1,0:T(8,128)S(1)}, f32[200,128]{1,0:T(8,128)S(1)}, f32[200,128]{1,0:T(8,128)S(1)}, f32[200,128]{1...) custom-call(s32[1]{0:T(128)} %bitcast.place_ref, ...), custom_call_target="tpu_custom_call" | custom-call | flops 3221225472 | bytes 3145728 | tf_op jit(solution)/shard_map/line_slopes/pallas_call | solution.py:403
  173.4 3.1 %collective-permute-start.20 = (f32[200,128]{1,0:T(8,128)S(1)}, f32[200,128]{1,0:T(8,128)S(1)}, u32[]{:S(2)}, u32[]{:S(2)}) collective-permute-start(f32[200,128]{1,0:T(8,128)S(1)} %get-tuple-element.69), channel_id=1, source_target_pairs={{0,10},{2,12},{4,14},{6,16},{8,18},{10,20},{12,22},{14,24},{16,26}... | collective-permute-start | bytes 307208 | tf_op jit(solution)/shard_map/ppermute | solution.py:535
  177.4 3.0 %collective-permute-done.17.refs_2_ = f32[200,128]{1,0:T(8,128)S(1)} collective-permute-done((f32[200,128]{1,0:T(8,128)S(1)}, f32[200,128]{1,0:T(8,128)S(1)}, u32[]{:S(2)}, u32[]{:S(2)}) %collective-permute-start.17) | collective-permute-done | bytes 102432 | tf_op jit(solution)/shard_map/ppermute | solution.py:535
  181.6 3.0 %collective-permute-start.24 = (f32[200,128]{1,0:T(8,128)S(1)}, f32[200,128]{1,0:T(8,128)S(1)}, u32[]{:S(2)}, u32[]{:S(2)}) collective-permute-start(f32[200,128]{1,0:T(8,128)S(1)} %get-tuple-element.73), channel_id=1, source_target_pairs={{0,18},{2,20},{4,22},{6,24},{8,26},{10,28},{12,30},{14,0},{16,2},{... | collective-permute-start | bytes 307208 | tf_op jit(solution)/shard_map/ppermute | solution.py:535
  184.7 11.6 %collective-permute-done.20.refs_5_ = f32[200,128]{1,0:T(8,128)S(1)} collective-permute-done((f32[200,128]{1,0:T(8,128)S(1)}, f32[200,128]{1,0:T(8,128)S(1)}, u32[]{:S(2)}, u32[]{:S(2)}) %collective-permute-start.20) | collective-permute-done | bytes 102432 | tf_op jit(solution)/shard_map/ppermute | solution.py:535
  201.6 6.0 %collective-permute-start.29 = (f32[200,128]{1,0:T(8,128)S(1)}, f32[200,128]{1,0:T(8,128)S(1)}, u32[]{:S(2)}, u32[]{:S(2)}) collective-permute-start(f32[200,128]{1,0:T(8,128)S(1)} %get-tuple-element.78), channel_id=1, source_target_pairs={{0,28},{2,30},{4,0},{6,2},{8,4},{10,6},{12,8},{14,10},{16,12},{18,... | collective-permute-start | bytes 307208 | tf_op jit(solution)/shard_map/ppermute | solution.py:535
  208.4 2.7 %collective-permute-done.29.refs_14_ = f32[200,128]{1,0:T(8,128)S(1)} collective-permute-done((f32[200,128]{1,0:T(8,128)S(1)}, f32[200,128]{1,0:T(8,128)S(1)}, u32[]{:S(2)}, u32[]{:S(2)}) %collective-permute-start.29) | collective-permute-done | bytes 102432 | tf_op jit(solution)/shard_map/ppermute | solution.py:535
  212.5 5.0 %advect.2 = (f32[3,2,64,2048]{3,2,1,0:T(8,128)}, f32[3,2,64,2048]{3,2,1,0:T(8,128)}, f32[8,128]{1,0:T(8,128)S(1)}) custom-call(s32[1]{0:T(128)} %bitcast.place_ref, f32[3,2,64,2048]{3,2,1,0:T(8,128)S(1)} %bitcast.6, f32[200,128]{1,0:T(8,128)S(1)} %get-tuple-element.64.refs_0_, f32[200,128]{1,0:T(8,128)S(1)} %collective-permute-done.16.refs_1_, ...), custom_call_target="tpu_custom_call" | custom-call | flops 1179648 | bytes 6291456 | tf_op jit(solution)/shard_map/advect/pallas_call | solution.py:499
  217.5 3.7 %advect.3 = (f32[3,2,64,2048]{3,2,1,0:T(8,128)}, f32[3,2,64,2048]{3,2,1,0:T(8,128)}) custom-call(s32[1]{0:T(128)} %bitcast.place_ref, f32[3,2,64,2048]{3,2,1,0:T(8,128)S(1)} %bitcast.7, f32[3,2,64,2048]{3,2,1,0:T(8,128)} %get-tuple-element.80.refs_0_, f32[3,2,64,2048]{3,2,1,0:T(8,128)} %get-tuple-element.81.refs_1_, ...), custom_call_target="tpu_custom_call", output_to_operand_aliasing={{0}: (2, {}), {1}: (3, {})} | custom-call | flops 1179648 | bytes 6291456 | tf_op jit(solution)/shard_map/advect/pallas_call | solution.py:499
  (93 shorter events, 26.4 us)
Async XLA Ops:
  14.8 39.3 %all-to-all-start = ((f32[16,192,128]{2,1,0:T(8,128)}), f32[16,192,128]{2,1,0:T(8,128)S(1)}, u32[]{:S(2)}, u32[]{:S(2)}) async-start(f32[16,192,128]{2,1,0:T(8,128)} %get-tuple-element.83), calls=%async_computation | async-start | bytes 3145728 | tf_op jit(solution)/shard_map/all_to_all | solution.py:531
  68.9 148.6 %all-to-all-start.1 = ((f32[16,192,128]{2,1,0:T(8,128)}), f32[16,192,128]{2,1,0:T(8,128)}, u32[]{:S(2)}, u32[]{:S(2)}) async-start(f32[16,192,128]{2,1,0:T(8,128)} %line_slopes.3), calls=%async_computation.1 | async-start | bytes 3145728 | tf_op jit(solution)/shard_map/all_to_all | solution.py:531
  79.8 31.3 %collective-permute-start.1 = (f32[192,128]{1,0:T(8,128)S(1)}, f32[192,128]{1,0:T(8,128)S(1)}, u32[]{:S(2)}, u32[]{:S(2)}) collective-permute-start(f32[192,128]{1,0:T(8,128)S(1)} %copy-done.19), channel_id=1, source_target_pairs={{0,2},{2,4},{4,6},{6,8},{8,10},{10,12},{12,14},{14,16},{16,18},{18... | collective-permute-start | bytes 294920 | tf_op jit(solution)/shard_map/ppermute | solution.py:535
  79.9 32.4 %collective-permute-start.2 = (f32[192,128]{1,0:T(8,128)S(1)}, f32[192,128]{1,0:T(8,128)S(1)}, u32[]{:S(2)}, u32[]{:S(2)}) collective-permute-start(f32[192,128]{1,0:T(8,128)S(1)} %copy-done.18), channel_id=1, source_target_pairs={{0,4},{2,6},{4,8},{6,10},{8,12},{10,14},{12,16},{14,18},{16,20},{1... | collective-permute-start | bytes 294920 | tf_op jit(solution)/shard_map/ppermute | solution.py:535
  81.7 40.3 %collective-permute-start.3 = (f32[192,128]{1,0:T(8,128)S(1)}, f32[192,128]{1,0:T(8,128)S(1)}, u32[]{:S(2)}, u32[]{:S(2)}) collective-permute-start(f32[192,128]{1,0:T(8,128)S(1)} %copy-done.17), channel_id=1, source_target_pairs={{0,6},{2,8},{4,10},{6,12},{8,14},{10,16},{12,18},{14,20},{16,22},{... | collective-permute-start | bytes 294920 | tf_op jit(solution)/shard_map/ppermute | solution.py:535
  84.0 39.3 %collective-permute-start.4 = (f32[192,128]{1,0:T(8,128)S(1)}, f32[192,128]{1,0:T(8,128)S(1)}, u32[]{:S(2)}, u32[]{:S(2)}) collective-permute-start(f32[192,128]{1,0:T(8,128)S(1)} %copy-done.16), channel_id=1, source_target_pairs={{0,8},{2,10},{4,12},{6,14},{8,16},{10,18},{12,20},{14,22},{16,24},... | collective-permute-start | bytes 294920 | tf_op jit(solution)/shard_map/ppermute | solution.py:535
  85.5 48.8 %collective-permute-start.5 = (f32[192,128]{1,0:T(8,128)S(1)}, f32[192,128]{1,0:T(8,128)S(1)}, u32[]{:S(2)}, u32[]{:S(2)}) collective-permute-start(f32[192,128]{1,0:T(8,128)S(1)} %copy-done.15), channel_id=1, source_target_pairs={{0,10},{2,12},{4,14},{6,16},{8,18},{10,20},{12,22},{14,24},{16,26}... | collective-permute-start | bytes 294920 | tf_op jit(solution)/shard_map/ppermute | solution.py:535
  111.1 24.4 %collective-permute-start.6 = (f32[192,128]{1,0:T(8,128)S(1)}, f32[192,128]{1,0:T(8,128)S(1)}, u32[]{:S(2)}, u32[]{:S(2)}) collective-permute-start(f32[192,128]{1,0:T(8,128)S(1)} %copy-done.14), channel_id=1, source_target_pairs={{0,12},{2,14},{4,16},{6,18},{8,20},{10,22},{12,24},{14,26},{16,28}... | collective-permute-start | bytes 294920 | tf_op jit(solution)/shard_map/ppermute | solution.py:535
  112.3 23.4 %collective-permute-start.7 = (f32[192,128]{1,0:T(8,128)S(1)}, f32[192,128]{1,0:T(8,128)S(1)}, u32[]{:S(2)}, u32[]{:S(2)}) collective-permute-start(f32[192,128]{1,0:T(8,128)S(1)} %copy-done.13), channel_id=1, source_target_pairs={{0,14},{2,16},{4,18},{6,20},{8,22},{10,24},{12,26},{14,28},{16,30}... | collective-permute-start | bytes 294920 | tf_op jit(solution)/shard_map/ppermute | solution.py:535
  122.1 17.0 %collective-permute-start.8 = (f32[192,128]{1,0:T(8,128)S(1)}, f32[192,128]{1,0:T(8,128)S(1)}, u32[]{:S(2)}, u32[]{:S(2)}) collective-permute-start(f32[192,128]{1,0:T(8,128)S(1)} %copy-done.12), channel_id=1, source_target_pairs={{0,16},{2,18},{4,20},{6,22},{8,24},{10,26},{12,28},{14,30},{16,0},... | collective-permute-start | bytes 294920 | tf_op jit(solution)/shard_map/ppermute | solution.py:535
  123.4 21.7 %collective-permute-start.9 = (f32[192,128]{1,0:T(8,128)S(1)}, f32[192,128]{1,0:T(8,128)S(1)}, u32[]{:S(2)}, u32[]{:S(2)}) collective-permute-start(f32[192,128]{1,0:T(8,128)S(1)} %copy-done.11), channel_id=1, source_target_pairs={{0,18},{2,20},{4,22},{6,24},{8,26},{10,28},{12,30},{14,0},{16,2},{... | collective-permute-start | bytes 294920 | tf_op jit(solution)/shard_map/ppermute | solution.py:535
  134.3 13.1 %collective-permute-start.10 = (f32[192,128]{1,0:T(8,128)S(1)}, f32[192,128]{1,0:T(8,128)S(1)}, u32[]{:S(2)}, u32[]{:S(2)}) collective-permute-start(f32[192,128]{1,0:T(8,128)S(1)} %copy-done.10), channel_id=1, source_target_pairs={{0,20},{2,22},{4,24},{6,26},{8,28},{10,30},{12,0},{14,2},{16,4},{1... | collective-permute-start | bytes 294920 | tf_op jit(solution)/shard_map/ppermute | solution.py:535
  135.5 14.0 %collective-permute-start.11 = (f32[192,128]{1,0:T(8,128)S(1)}, f32[192,128]{1,0:T(8,128)S(1)}, u32[]{:S(2)}, u32[]{:S(2)}) collective-permute-start(f32[192,128]{1,0:T(8,128)S(1)} %copy-done.9), channel_id=1, source_target_pairs={{0,22},{2,24},{4,26},{6,28},{8,30},{10,0},{12,2},{14,4},{16,6},{18... | collective-permute-start | bytes 294920 | tf_op jit(solution)/shard_map/ppermute | solution.py:535
  135.7 13.8 %collective-permute-start.12 = (f32[192,128]{1,0:T(8,128)S(1)}, f32[192,128]{1,0:T(8,128)S(1)}, u32[]{:S(2)}, u32[]{:S(2)}) collective-permute-start(f32[192,128]{1,0:T(8,128)S(1)} %copy-done.8), channel_id=1, source_target_pairs={{0,24},{2,26},{4,28},{6,30},{8,0},{10,2},{12,4},{14,6},{16,8},{18,... | collective-permute-start | bytes 294920 | tf_op jit(solution)/shard_map/ppermute | solution.py:535
  139.1 10.4 %collective-permute-start.13 = (f32[192,128]{1,0:T(8,128)S(1)}, f32[192,128]{1,0:T(8,128)S(1)}, u32[]{:S(2)}, u32[]{:S(2)}) collective-permute-start(f32[192,128]{1,0:T(8,128)S(1)} %copy-done.7), channel_id=1, source_target_pairs={{0,26},{2,28},{4,30},{6,0},{8,2},{10,4},{12,6},{14,8},{16,10},{18,... | collective-permute-start | bytes 294920 | tf_op jit(solution)/shard_map/ppermute | solution.py:535
  173.4 22.9 %collective-permute-start.20 = (f32[200,128]{1,0:T(8,128)S(1)}, f32[200,128]{1,0:T(8,128)S(1)}, u32[]{:S(2)}, u32[]{:S(2)}) collective-permute-start(f32[200,128]{1,0:T(8,128)S(1)} %get-tuple-element.69), channel_id=1, source_target_pairs={{0,10},{2,12},{4,14},{6,16},{8,18},{10,20},{12,22},{14,24},{16,26}... | collective-permute-start | bytes 307208 | tf_op jit(solution)/shard_map/ppermute | solution.py:535
  177.3 19.2 %collective-permute-start.21 = (f32[200,128]{1,0:T(8,128)S(1)}, f32[200,128]{1,0:T(8,128)S(1)}, u32[]{:S(2)}, u32[]{:S(2)}) collective-permute-start(f32[200,128]{1,0:T(8,128)S(1)} %get-tuple-element.70), channel_id=1, source_target_pairs={{0,12},{2,14},{4,16},{6,18},{8,20},{10,22},{12,24},{14,26},{16,28}... | collective-permute-start | bytes 307208 | tf_op jit(solution)/shard_map/ppermute | solution.py:535
  180.4 17.4 %collective-permute-start.22 = (f32[200,128]{1,0:T(8,128)S(1)}, f32[200,128]{1,0:T(8,128)S(1)}, u32[]{:S(2)}, u32[]{:S(2)}) collective-permute-start(f32[200,128]{1,0:T(8,128)S(1)} %get-tuple-element.71), channel_id=1, source_target_pairs={{0,14},{2,16},{4,18},{6,20},{8,22},{10,24},{12,26},{14,28},{16,30}... | collective-permute-start | bytes 307208 | tf_op jit(solution)/shard_map/ppermute | solution.py:535
  180.4 19.5 %collective-permute-start.23 = (f32[200,128]{1,0:T(8,128)S(1)}, f32[200,128]{1,0:T(8,128)S(1)}, u32[]{:S(2)}, u32[]{:S(2)}) collective-permute-start(f32[200,128]{1,0:T(8,128)S(1)} %get-tuple-element.72), channel_id=1, source_target_pairs={{0,16},{2,18},{4,20},{6,22},{8,24},{10,26},{12,28},{14,30},{16,0},... | collective-permute-start | bytes 307208 | tf_op jit(solution)/shard_map/ppermute | solution.py:535
  181.6 19.9 %collective-permute-start.24 = (f32[200,128]{1,0:T(8,128)S(1)}, f32[200,128]{1,0:T(8,128)S(1)}, u32[]{:S(2)}, u32[]{:S(2)}) collective-permute-start(f32[200,128]{1,0:T(8,128)S(1)} %get-tuple-element.73), channel_id=1, source_target_pairs={{0,18},{2,20},{4,22},{6,24},{8,26},{10,28},{12,30},{14,0},{16,2},{... | collective-permute-start | bytes 307208 | tf_op jit(solution)/shard_map/ppermute | solution.py:535
  196.3 11.3 %collective-permute-start.25 = (f32[200,128]{1,0:T(8,128)S(1)}, f32[200,128]{1,0:T(8,128)S(1)}, u32[]{:S(2)}, u32[]{:S(2)}) collective-permute-start(f32[200,128]{1,0:T(8,128)S(1)} %get-tuple-element.74), channel_id=1, source_target_pairs={{0,20},{2,22},{4,24},{6,26},{8,28},{10,30},{12,0},{14,2},{16,4},{1... | collective-permute-start | bytes 307208 | tf_op jit(solution)/shard_map/ppermute | solution.py:535
  196.5 11.9 %collective-permute-start.26 = (f32[200,128]{1,0:T(8,128)S(1)}, f32[200,128]{1,0:T(8,128)S(1)}, u32[]{:S(2)}, u32[]{:S(2)}) collective-permute-start(f32[200,128]{1,0:T(8,128)S(1)} %get-tuple-element.75), channel_id=1, source_target_pairs={{0,22},{2,24},{4,26},{6,28},{8,30},{10,0},{12,2},{14,4},{16,6},{18... | collective-permute-start | bytes 307208 | tf_op jit(solution)/shard_map/ppermute | solution.py:535
  197.8 10.6 %collective-permute-start.27 = (f32[200,128]{1,0:T(8,128)S(1)}, f32[200,128]{1,0:T(8,128)S(1)}, u32[]{:S(2)}, u32[]{:S(2)}) collective-permute-start(f32[200,128]{1,0:T(8,128)S(1)} %get-tuple-element.76), channel_id=1, source_target_pairs={{0,24},{2,26},{4,28},{6,30},{8,0},{10,2},{12,4},{14,6},{16,8},{18,... | collective-permute-start | bytes 307208 | tf_op jit(solution)/shard_map/ppermute | solution.py:535
  201.6 9.6 %collective-permute-start.29 = (f32[200,128]{1,0:T(8,128)S(1)}, f32[200,128]{1,0:T(8,128)S(1)}, u32[]{:S(2)}, u32[]{:S(2)}) collective-permute-start(f32[200,128]{1,0:T(8,128)S(1)} %get-tuple-element.78), channel_id=1, source_target_pairs={{0,28},{2,30},{4,0},{6,2},{8,4},{10,6},{12,8},{14,10},{16,12},{18,... | collective-permute-start | bytes 307208 | tf_op jit(solution)/shard_map/ppermute | solution.py:535
  (29 other events, 915.9 us)

commit v3 on v2

--- a/solution.py
+++ b/solution.py
@@ -279,7 +279,7 @@
 
 def line_slopes(arrived, place, gram, tables, match, sums):
     gather = isinstance(arrived, list)
-    spread = sums is not None
+    below = 0 if sums is None else 8
     count = len(arrived) if gather else arrived.shape[0]
     depth, width = arrived[0].shape[-2:]
     slots, block = tables.shape[0], tables.shape[2] // 2
@@ -293,9 +293,9 @@
 
     def body(place_ref, g_ref, table_ref, *refs):
         refs = list(refs)
-        sums_ref = refs.pop(0) if spread else None
+        sums_ref = refs.pop(0) if below else None
         ins = [refs.pop(0) for _ in range(count if gather else 1)]
-        outs = [refs.pop(0) for _ in range(count if spread else 1)]
+        outs = [refs.pop(0) for _ in range(count)]
         t_ref, spec, extra, lines, result, table_sem, in_sem, out_sem, sum_sem = refs
         load = [
             pltpu.make_async_copy(
@@ -386,24 +386,19 @@
             return 0
 
         lax.fori_loop(0, half // GROUP, backward, 0)
-        if spread:
-            copies = far_copies(count, place_ref[0], result, outs, out_sem, True)
+        copies = far_copies(count, place_ref[0], result, outs, out_sem, True)
+        if below:
             for k in range(count):
-                below = outs[k].at[pl.ds(depth, 8)]
-                copies.append(pltpu.make_async_copy(sums_ref, below, sum_sem.at[k]))
-        else:
-            copies = [pltpu.make_async_copy(result, outs[0], out_sem.at[0])]
+                under = outs[k].at[pl.ds(depth, below)]
+                copies.append(pltpu.make_async_copy(sums_ref, under, sum_sem.at[k]))
         run_copies(copies)
 
-    if spread:
-        out_shape = [jax.ShapeDtypeStruct((depth + 8, width), F32)] * count
-    else:
-        out_shape = [jax.ShapeDtypeStruct((count, depth, width), F32)]
+    out_shape = [jax.ShapeDtypeStruct((depth + below, width), F32)] * count
     stacked = pltpu.VMEM((count, depth, width), F32)
     out = pl.pallas_call(
         body,
         name="line_slopes",
-        in_specs=[SMEM, VMEM, HBM] + [VMEM] * spread + [HBM] * (count if gather else 1),
+        in_specs=[SMEM, VMEM, HBM] + [VMEM] * (sums is not None) + [HBM] * (count if gather else 1),
         out_specs=[HBM] * len(out_shape),
         out_shape=out_shape,
         scratch_shapes=[
@@ -423,15 +418,15 @@
             bytes_accessed=8 * count * depth * width,
             transcendentals=0,
         ),
-    )(place, gram, tables, *([sums] if spread else []), *(arrived if gather else [arrived]))
-    return list(out) if spread else out[0]
+    )(place, gram, tables, *([sums] if below else []), *(arrived if gather else [arrived]))
+    return list(out)
 
 
 def advect(view, chunk, arrived, place, points, energy, earlier):
-    gather = isinstance(arrived, list)
+    adding = energy is None
     per, _, half, lines = view.shape
     span = lines // 2
-    count = len(arrived) if gather else arrived.shape[0]
+    count = len(arrived)
     depth, width = per * half, arrived[0].shape[-1]
     quarter = half // 2
     steps = [(b, q * quarter) for b in range(per) for q in range(2)]
@@ -439,10 +434,10 @@
 
     def body(place_ref, v_ref, *refs):
         refs = list(refs)[kept:]
-        energy_in = None if gather else refs.pop(0)
-        ins = [refs.pop(0) for _ in range(count if gather else 1)]
+        energy_in = None if adding else refs.pop(0)
+        ins = [refs.pop(0) for _ in range(count)]
         s_ref, f_ref = refs.pop(0), refs.pop(0)
-        energy_out = refs.pop(0) if gather else None
+        energy_out = refs.pop(0) if adding else None
         v_buf, stacked, tiles, s_buf, f_buf, v_sem, in_sem, sum_sem, s_sem, f_sem = refs
 
         def part(ref, j):
@@ -453,18 +448,16 @@
             pltpu.make_async_copy(part(v_ref, j), v_buf.at[j], v_sem.at[j])
             for j in range(len(steps))
         ]
-        if gather:
-            pieces = far_copies(count, place_ref[0], stacked, ins, in_sem, False)
+        pieces = far_copies(count, place_ref[0], stacked, ins, in_sem, False)
+        if adding:
             for k in range(count):
                 below = ins[k].at[pl.ds(depth, 8)]
                 pieces.append(pltpu.make_async_copy(below, tiles.at[k], sum_sem.at[k]))
-        else:
-            pieces = [pltpu.make_async_copy(ins[0], stacked, in_sem.at[0])]
         for copy in pieces + fields:
             copy.start()
         for copy in pieces:
             copy.wait()
-        if gather:
+        if adding:
             tile = tiles[0]
             for k in range(1, count):
                 tile += tiles[k]
@@ -501,10 +494,11 @@
         name="advect",
         in_specs=[SMEM, HBM]
         + [HBM] * kept
-        + ([HBM] * count if gather else [VMEM, HBM]),
-        out_specs=[HBM, HBM] + [VMEM] * gather,
+        + [VMEM] * (not adding)
+        + [HBM] * count,
+        out_specs=[HBM, HBM] + [VMEM] * adding,
         out_shape=[jax.ShapeDtypeStruct(view.shape, F32)] * 2
-        + [jax.ShapeDtypeStruct((8, width), F32)] * gather,
+        + [jax.ShapeDtypeStruct((8, width), F32)] * adding,
         scratch_shapes=[
             buffer,
             pltpu.VMEM((count, depth, width), F32),
@@ -522,8 +516,8 @@
         cost_estimate=pl.CostEstimate(
             flops=depth * lines * 3, bytes_accessed=depth * lines * 16, transcendentals=0
         ),
-    )(place, view, *(earlier or ()), *(arrived if gather else [energy, arrived]))
-    return out[:2], (out[2] if gather else energy)
+    )(place, view, *(earlier or ()), *(() if adding else [energy]), *arrived)
+    return out[:2], (out[2] if adding else energy)
 
 
 def exchange(pieces, axis):

time: 222 us -> 220 us (level)
  waiting for transfers between devices: 90.4 us -> 72.1 us
  starting transfers between devices: 73.8 us -> 81.7 us
  local copies, waits for them, and re-layouts: 0.29 us -> 5.52 us
  Pallas kernels: 55.7 us -> 59.2 us
    all_to_all x2 -> x1, waiting for transfers between devices: 31.6 us -> 0.01 us  [exchange(): return lax.all_to_all(pieces, axis, split_axis=0, concat_axis=0, tiled=True)]
    ppermute x30 -> x45, starting transfers between devices: 55.5 us -> 72.5 us  [exchange(): lax.ppermute(pieces[k], axis, [(i, (i + k) % count) for i in range(count)])]
    ppermute x30 -> x45, waiting for transfers between devices: 58.9 us -> 72.1 us  [exchange(): lax.ppermute(pieces[k], axis, [(i, (i + k) % count) for i in range(count)])]
    all_to_all x2 -> x1, starting transfers between devices: 16.7 us -> 7.6 us  [exchange(): return lax.all_to_all(pieces, axis, split_axis=0, concat_axis=0, tiled=True)]
    unnamed x42 -> x74, local copies, waits for them, and re-layouts: 0.29 us -> 5.52 us
  transfers between devices with their start and end apart: 33 -> 47, of which waited for: 13 -> 13; matrix products, arithmetic and copies ran while one was open for 0% -> 0% of each run, Pallas kernels for 10% -> 18%
where the time goes in v3:
time: 220 us
  starting transfers between devices  81.7 us (37%)
  waiting for transfers between devices  72.1 us (33%)
  Pallas kernels  59.2 us (27%)
  local copies, waits for them, and re-layouts  5.52 us (3%)
    ppermute x45, starting transfers between devices, exchange(): lax.ppermute(pieces[k], axis, [(i, (i + k) % count) for i in range(count)])  72.5 us
    ppermute x45, waiting for transfers between devices, exchange(): lax.ppermute(pieces[k], axis, [(i, (i + k) % count) for i in range(count)])  72.1 us
    pallas_call x2, Pallas kernels, line_slopes(): pl.pallas_call(body, name='line_slopes', in_specs=[SMEM, VMEM, HBM] + [VM...  35 us
    pallas_call x2, Pallas kernels, advect(): pl.pallas_call(body, name='advect', in_specs=[SMEM, HBM] + [HBM] * kept +...  9.96 us
    pallas_call x2, Pallas kernels, pack(): pl.pallas_call(body, name='pack_pieces' if parts else 'pack_stacked', in_...  7.63 us
    all_to_all x1, starting transfers between devices, exchange(): return lax.all_to_all(pieces, axis, split_axis=0, concat_axis=0, tiled=True)  7.6 us
    pallas_call x1, Pallas kernels, toeplitz_tables(): pl.pallas_call(body, name='toeplitz_tables', in_specs=[VMEM], out_specs=H...  6.55 us
    unnamed x74, local copies, waits for them, and re-layouts  5.52 us
  transfers between devices with their start and end apart: 47, of which 13 were waited for; matrix products, arithmetic and copies ran while one was open for 0% of the time, Pallas kernels for 18%

profile of v3, /device:TPU:0, one launch (start us, length us, event | category | flops | bytes accessed | tf_op | source)
XLA Modules:
  0.0 219.8 jit_solution(12914975514103601253)
XLA Ops:
  0.6 3.7 %pack_pieces.1 = (f32[192,128]{1,0:T(8,128)}, f32[192,128]{1,0:T(8,128)}, f32[192,128]{1,0:T(8,128)}, f32[192,128]{1,0:T(8,128)}, f32[192,128]{1,0:T(8,128)}, /*...) custom-call(s32[1]{0:T(128)} %bitcast.place_ref, ...), custom_call_target="tpu_custom_call" | custom-call | flops 786432 | bytes 3145728 | tf_op jit(solution)/shard_map/pack_pieces/pallas_call | solution.py:260
  4.3 3.9 %pack_stacked.1 = (f32[16,192,128]{2,1,0:T(8,128)}, f32[8,128]{1,0:T(8,128)}) custom-call(s32[1]{0:T(128)} %bitcast.place_ref, f32[3,2,64,2048]{3,2,1,0:T(8,128)} %bitcast.5, f32[8,128]{1,0:T(8,128)} %get-tuple-element.60.refs_0_), custom_call_target="tpu_custom_call" | custom-call | flops 786432 | bytes 3145728 | tf_op jit(solution)/shard_map/pack_stacked/pallas_call | solution.py:260
  8.3 6.6 %toeplitz_tables.1.table_ref = bf16[48,384,256]{2,1,0:T(8,128)(2,1)} custom-call(f32[96,256]{1,0:T(8,128)} %constant.11.clone.w_ref), custom_call_target="tpu_custom_call" | custom-call | flops 25165824 | bytes 9437184 | tf_op jit(solution)/shard_map/toeplitz_tables/pallas_call | solution.py:169
  15.0 7.6 %all-to-all-start = ((f32[16,192,128]{2,1,0:T(8,128)}), f32[16,192,128]{2,1,0:T(8,128)}, u32[]{:S(2)}, u32[]{:S(2)}) async-start(f32[16,192,128]{2,1,0:T(8,128)} %get-tuple-element.99), calls=%async_computation | async-start | bytes 3145728 | tf_op jit(solution)/shard_map/all_to_all | solution.py:525
  30.0 25.5 %collective-permute-done.1.refs_2_ = f32[192,128]{1,0:T(8,128)S(1)} collective-permute-done((f32[192,128]{1,0:T(8,128)S(1)}, f32[192,128]{1,0:T(8,128)S(1)}, u32[]{:S(2)}, u32[]{:S(2)}) %collective-permute-start.1) | collective-permute-done | bytes 98336 | tf_op jit(solution)/shard_map/ppermute | solution.py:529
  56.7 9.8 %collective-permute-start.7 = (f32[192,128]{1,0:T(8,128)S(1)}, f32[192,128]{1,0:T(8,128)S(1)}, u32[]{:S(2)}, u32[]{:S(2)}) collective-permute-start(f32[192,128]{1,0:T(8,128)S(1)} %copy-done.29), channel_id=1, source_target_pairs={{0,14},{2,16},{4,18},{6,20},{8,22},{10,24},{12,26},{14,28},{16,30}... | collective-permute-start | bytes 294920 | tf_op jit(solution)/shard_map/ppermute | solution.py:529
  70.1 8.6 %collective-permute-done.5.refs_6_ = f32[192,128]{1,0:T(8,128)S(1)} collective-permute-done((f32[192,128]{1,0:T(8,128)S(1)}, f32[192,128]{1,0:T(8,128)S(1)}, u32[]{:S(2)}, u32[]{:S(2)}) %collective-permute-start.5) | collective-permute-done | bytes 98336 | tf_op jit(solution)/shard_map/ppermute | solution.py:529
  80.1 3.4 %collective-permute-start.12 = (f32[192,128]{1,0:T(8,128)S(1)}, f32[192,128]{1,0:T(8,128)S(1)}, u32[]{:S(2)}, u32[]{:S(2)}) collective-permute-start(f32[192,128]{1,0:T(8,128)S(1)} %copy-done.24), channel_id=1, source_target_pairs={{0,24},{2,26},{4,28},{6,30},{8,0},{10,2},{12,4},{14,6},{16,8},{18,... | collective-permute-start | bytes 294920 | tf_op jit(solution)/shard_map/ppermute | solution.py:529
  83.5 6.0 %collective-permute-start.13 = (f32[192,128]{1,0:T(8,128)S(1)}, f32[192,128]{1,0:T(8,128)S(1)}, u32[]{:S(2)}, u32[]{:S(2)}) collective-permute-start(f32[192,128]{1,0:T(8,128)S(1)} %copy-done.23), channel_id=1, source_target_pairs={{0,26},{2,28},{4,30},{6,0},{8,2},{10,4},{12,6},{14,8},{16,10},{18,... | collective-permute-start | bytes 294920 | tf_op jit(solution)/shard_map/ppermute | solution.py:529
  96.5 18.1 %line_slopes.2 = (f32[200,128]{1,0:T(8,128)S(1)}, f32[200,128]{1,0:T(8,128)S(1)}, f32[200,128]{1,0:T(8,128)S(1)}, f32[200,128]{1,0:T(8,128)S(1)}, f32[200,128]{1...) custom-call(s32[1]{0:T(128)} %bitcast.place_ref, ...), custom_call_target="tpu_custom_call" | custom-call | flops 3221225472 | bytes 3145728 | tf_op jit(solution)/shard_map/line_slopes/pallas_call | solution.py:398
  117.6 3.1 %collective-permute-start.20 = (f32[200,128]{1,0:T(8,128)S(1)}, f32[200,128]{1,0:T(8,128)S(1)}, u32[]{:S(2)}, u32[]{:S(2)}) collective-permute-start(f32[200,128]{1,0:T(8,128)S(1)} %get-tuple-element.85), channel_id=1, source_target_pairs={{0,10},{2,12},{4,14},{6,16},{8,18},{10,20},{12,22},{14,24},{16,26}... | collective-permute-start | bytes 307208 | tf_op jit(solution)/shard_map/ppermute | solution.py:529
  121.7 3.0 %collective-permute-done.17.refs_2_ = f32[200,128]{1,0:T(8,128)S(1)} collective-permute-done((f32[200,128]{1,0:T(8,128)S(1)}, f32[200,128]{1,0:T(8,128)S(1)}, u32[]{:S(2)}, u32[]{:S(2)}) %collective-permute-start.17) | collective-permute-done | bytes 102432 | tf_op jit(solution)/shard_map/ppermute | solution.py:529
  126.6 3.0 %collective-permute-start.24 = (f32[200,128]{1,0:T(8,128)S(1)}, f32[200,128]{1,0:T(8,128)S(1)}, u32[]{:S(2)}, u32[]{:S(2)}) collective-permute-start(f32[200,128]{1,0:T(8,128)S(1)} %get-tuple-element.89), channel_id=1, source_target_pairs={{0,18},{2,20},{4,22},{6,24},{8,26},{10,28},{12,30},{14,0},{16,2},{... | collective-permute-start | bytes 307208 | tf_op jit(solution)/shard_map/ppermute | solution.py:529
  129.6 10.9 %collective-permute-done.20.refs_5_ = f32[200,128]{1,0:T(8,128)S(1)} collective-permute-done((f32[200,128]{1,0:T(8,128)S(1)}, f32[200,128]{1,0:T(8,128)S(1)}, u32[]{:S(2)}, u32[]{:S(2)}) %collective-permute-start.20) | collective-permute-done | bytes 102432 | tf_op jit(solution)/shard_map/ppermute | solution.py:529
  147.7 4.3 %collective-permute-start.29 = (f32[200,128]{1,0:T(8,128)}, f32[200,128]{1,0:T(8,128)}, u32[]{:S(2)}, u32[]{:S(2)}) collective-permute-start(f32[200,128]{1,0:T(8,128)} %get-tuple-element.94), channel_id=1, source_target_pairs={{0,28},{2,30},{4,0},{6,2},{8,4},{10,6},{12,8},{14,10},{16,12},{18,... | collective-permute-start | bytes 307208 | tf_op jit(solution)/shard_map/ppermute | solution.py:529
  152.7 2.6 %collective-permute-start.30 = (f32[200,128]{1,0:T(8,128)}, f32[200,128]{1,0:T(8,128)}, u32[]{:S(2)}, u32[]{:S(2)}) collective-permute-start(f32[200,128]{1,0:T(8,128)} %get-tuple-element.95), channel_id=1, source_target_pairs={{0,30},{2,0},{4,2},{6,4},{8,6},{10,8},{12,10},{14,12},{16,14},{18,... | collective-permute-start | bytes 307208 | tf_op jit(solution)/shard_map/ppermute | solution.py:529
  156.1 17.0 %line_slopes.3 = (f32[192,128]{1,0:T(8,128)S(1)}, f32[192,128]{1,0:T(8,128)S(1)}, f32[192,128]{1,0:T(8,128)S(1)}, f32[192,128]{1,0:T(8,128)S(1)}, f32[192,128]{1...) custom-call(s32[1]{0:T(128)} %bitcast.place_ref, ...), custom_call_target="tpu_custom_call" | custom-call | flops 3221225472 | bytes 3145728 | tf_op jit(solution)/shard_map/line_slopes/pallas_call | solution.py:398
  175.1 4.9 %collective-permute-done.31.refs_4_ = f32[192,128]{1,0:T(8,128)S(1)} collective-permute-done((f32[192,128]{1,0:T(8,128)S(1)}, f32[192,128]{1,0:T(8,128)S(1)}, u32[]{:S(2)}, u32[]{:S(2)}) %collective-permute-start.31) | collective-permute-done | bytes 98336 | tf_op jit(solution)/shard_map/ppermute | solution.py:529
  185.8 11.8 %collective-permute-done.35.refs_8_ = f32[192,128]{1,0:T(8,128)S(1)} collective-permute-done((f32[192,128]{1,0:T(8,128)S(1)}, f32[192,128]{1,0:T(8,128)S(1)}, u32[]{:S(2)}, u32[]{:S(2)}) %collective-permute-start.35) | collective-permute-done | bytes 98336 | tf_op jit(solution)/shard_map/ppermute | solution.py:529
  199.1 3.0 %collective-permute-start.42 = (f32[192,128]{1,0:T(8,128)S(1)}, f32[192,128]{1,0:T(8,128)S(1)}, u32[]{:S(2)}, u32[]{:S(2)}) collective-permute-start(f32[192,128]{1,0:T(8,128)S(1)} %get-tuple-element.112), channel_id=1, source_target_pairs={{0,24},{2,26},{4,28},{6,30},{8,0},{10,2},{12,4},{14,6},{16,8},{18,... | collective-permute-start | bytes 294920 | tf_op jit(solution)/shard_map/ppermute | solution.py:529
  202.1 2.6 %collective-permute-start.43 = (f32[192,128]{1,0:T(8,128)S(1)}, f32[192,128]{1,0:T(8,128)S(1)}, u32[]{:S(2)}, u32[]{:S(2)}) collective-permute-start(f32[192,128]{1,0:T(8,128)S(1)} %get-tuple-element.113), channel_id=1, source_target_pairs={{0,26},{2,28},{4,30},{6,0},{8,2},{10,4},{12,6},{14,8},{16,10},{18,... | collective-permute-start | bytes 294920 | tf_op jit(solution)/shard_map/ppermute | solution.py:529
  207.0 2.6 %collective-permute-start.45 = (f32[192,128]{1,0:T(8,128)S(1)}, f32[192,128]{1,0:T(8,128)S(1)}, u32[]{:S(2)}, u32[]{:S(2)}) collective-permute-start(f32[192,128]{1,0:T(8,128)S(1)} %get-tuple-element.115), channel_id=1, source_target_pairs={{0,30},{2,0},{4,2},{6,4},{8,6},{10,8},{12,10},{14,12},{16,14},{18,... | collective-permute-start | bytes 294920 | tf_op jit(solution)/shard_map/ppermute | solution.py:529
  209.6 5.1 %advect.2 = (f32[3,2,64,2048]{3,2,1,0:T(8,128)}, f32[3,2,64,2048]{3,2,1,0:T(8,128)}, f32[8,128]{1,0:T(8,128)S(1)}) custom-call(s32[1]{0:T(128)} %bitcast.place_ref, f32[3,2,64,2048]{3,2,1,0:T(8,128)S(1)} %bitcast.6, f32[200,128]{1,0:T(8,128)S(1)} %get-tuple-element.80.refs_0_, f32[200,128]{1,0:T(8,128)S(1)} %collective-permute-done.16.refs_1_, ...), custom_call_target="tpu_custom_call" | custom-call | flops 1179648 | bytes 6291456 | tf_op jit(solution)/shard_map/advect/pallas_call | solution.py:492
  214.8 4.9 %advect.3 = (f32[3,2,64,2048]{3,2,1,0:T(8,128)}, f32[3,2,64,2048]{3,2,1,0:T(8,128)}) custom-call(s32[1]{0:T(128)} %bitcast.place_ref, f32[3,2,64,2048]{3,2,1,0:T(8,128)S(1)} %bitcast.7, f32[3,2,64,2048]{3,2,1,0:T(8,128)} %get-tuple-element.96.refs_0_, f32[3,2,64,2048]{3,2,1,0:T(8,128)} %get-tuple-element.97.refs_1_, ...), custom_call_target="tpu_custom_call", output_to_operand_aliasing={{0}: (2, {}), {1}: (3, {})} | custom-call | flops 1179648 | bytes 6291456 | tf_op jit(solution)/shard_map/advect/pallas_call | solution.py:492
  (153 shorter events, 46.5 us)
Async XLA Ops:
  15.0 140.3 %all-to-all-start = ((f32[16,192,128]{2,1,0:T(8,128)}), f32[16,192,128]{2,1,0:T(8,128)}, u32[]{:S(2)}, u32[]{:S(2)}) async-start(f32[16,192,128]{2,1,0:T(8,128)} %get-tuple-element.99), calls=%async_computation | async-start | bytes 3145728 | tf_op jit(solution)/shard_map/all_to_all | solution.py:525
  24.2 31.3 %collective-permute-start.1 = (f32[192,128]{1,0:T(8,128)S(1)}, f32[192,128]{1,0:T(8,128)S(1)}, u32[]{:S(2)}, u32[]{:S(2)}) collective-permute-start(f32[192,128]{1,0:T(8,128)S(1)} %copy-done.35), channel_id=1, source_target_pairs={{0,2},{2,4},{4,6},{6,8},{8,10},{10,12},{12,14},{14,16},{16,18},{18... | collective-permute-start | bytes 294920 | tf_op jit(solution)/shard_map/ppermute | solution.py:529
  24.3 32.4 %collective-permute-start.2 = (f32[192,128]{1,0:T(8,128)S(1)}, f32[192,128]{1,0:T(8,128)S(1)}, u32[]{:S(2)}, u32[]{:S(2)}) collective-permute-start(f32[192,128]{1,0:T(8,128)S(1)} %copy-done.34), channel_id=1, source_target_pairs={{0,4},{2,6},{4,8},{6,10},{8,12},{10,14},{12,16},{14,18},{16,20},{1... | collective-permute-start | bytes 294920 | tf_op jit(solution)/shard_map/ppermute | solution.py:529
  26.2 40.3 %collective-permute-start.3 = (f32[192,128]{1,0:T(8,128)S(1)}, f32[192,128]{1,0:T(8,128)S(1)}, u32[]{:S(2)}, u32[]{:S(2)}) collective-permute-start(f32[192,128]{1,0:T(8,128)S(1)} %copy-done.33), channel_id=1, source_target_pairs={{0,6},{2,8},{4,10},{6,12},{8,14},{10,16},{12,18},{14,20},{16,22},{... | collective-permute-start | bytes 294920 | tf_op jit(solution)/shard_map/ppermute | solution.py:529
  28.5 39.3 %collective-permute-start.4 = (f32[192,128]{1,0:T(8,128)S(1)}, f32[192,128]{1,0:T(8,128)S(1)}, u32[]{:S(2)}, u32[]{:S(2)}) collective-permute-start(f32[192,128]{1,0:T(8,128)S(1)} %copy-done.32), channel_id=1, source_target_pairs={{0,8},{2,10},{4,12},{6,14},{8,16},{10,18},{12,20},{14,22},{16,24},... | collective-permute-start | bytes 294920 | tf_op jit(solution)/shard_map/ppermute | solution.py:529
  29.9 48.8 %collective-permute-start.5 = (f32[192,128]{1,0:T(8,128)S(1)}, f32[192,128]{1,0:T(8,128)S(1)}, u32[]{:S(2)}, u32[]{:S(2)}) collective-permute-start(f32[192,128]{1,0:T(8,128)S(1)} %copy-done.31), channel_id=1, source_target_pairs={{0,10},{2,12},{4,14},{6,16},{8,18},{10,20},{12,22},{14,24},{16,26}... | collective-permute-start | bytes 294920 | tf_op jit(solution)/shard_map/ppermute | solution.py:529
  55.5 24.4 %collective-permute-start.6 = (f32[192,128]{1,0:T(8,128)S(1)}, f32[192,128]{1,0:T(8,128)S(1)}, u32[]{:S(2)}, u32[]{:S(2)}) collective-permute-start(f32[192,128]{1,0:T(8,128)S(1)} %copy-done.30), channel_id=1, source_target_pairs={{0,12},{2,14},{4,16},{6,18},{8,20},{10,22},{12,24},{14,26},{16,28}... | collective-permute-start | bytes 294920 | tf_op jit(solution)/shard_map/ppermute | solution.py:529
  56.7 23.4 %collective-permute-start.7 = (f32[192,128]{1,0:T(8,128)S(1)}, f32[192,128]{1,0:T(8,128)S(1)}, u32[]{:S(2)}, u32[]{:S(2)}) collective-permute-start(f32[192,128]{1,0:T(8,128)S(1)} %copy-done.29), channel_id=1, source_target_pairs={{0,14},{2,16},{4,18},{6,20},{8,22},{10,24},{12,26},{14,28},{16,30}... | collective-permute-start | bytes 294920 | tf_op jit(solution)/shard_map/ppermute | solution.py:529
  67.8 21.7 %collective-permute-start.9 = (f32[192,128]{1,0:T(8,128)S(1)}, f32[192,128]{1,0:T(8,128)S(1)}, u32[]{:S(2)}, u32[]{:S(2)}) collective-permute-start(f32[192,128]{1,0:T(8,128)S(1)} %copy-done.27), channel_id=1, source_target_pairs={{0,18},{2,20},{4,22},{6,24},{8,26},{10,28},{12,30},{14,0},{16,2},{... | collective-permute-start | bytes 294920 | tf_op jit(solution)/shard_map/ppermute | solution.py:529
  117.6 22.8 %collective-permute-start.20 = (f32[200,128]{1,0:T(8,128)S(1)}, f32[200,128]{1,0:T(8,128)S(1)}, u32[]{:S(2)}, u32[]{:S(2)}) collective-permute-start(f32[200,128]{1,0:T(8,128)S(1)} %get-tuple-element.85), channel_id=1, source_target_pairs={{0,10},{2,12},{4,14},{6,16},{8,18},{10,20},{12,22},{14,24},{16,26}... | collective-permute-start | bytes 307208 | tf_op jit(solution)/shard_map/ppermute | solution.py:529
  121.6 19.5 %collective-permute-start.21 = (f32[200,128]{1,0:T(8,128)S(1)}, f32[200,128]{1,0:T(8,128)S(1)}, u32[]{:S(2)}, u32[]{:S(2)}) collective-permute-start(f32[200,128]{1,0:T(8,128)S(1)} %get-tuple-element.86), channel_id=1, source_target_pairs={{0,12},{2,14},{4,16},{6,18},{8,20},{10,22},{12,24},{14,26},{16,28}... | collective-permute-start | bytes 307208 | tf_op jit(solution)/shard_map/ppermute | solution.py:529
  124.7 17.9 %collective-permute-start.22 = (f32[200,128]{1,0:T(8,128)S(1)}, f32[200,128]{1,0:T(8,128)S(1)}, u32[]{:S(2)}, u32[]{:S(2)}) collective-permute-start(f32[200,128]{1,0:T(8,128)S(1)} %get-tuple-element.87), channel_id=1, source_target_pairs={{0,14},{2,16},{4,18},{6,20},{8,22},{10,24},{12,26},{14,28},{16,30}... | collective-permute-start | bytes 307208 | tf_op jit(solution)/shard_map/ppermute | solution.py:529
  124.7 20.8 %collective-permute-start.23 = (f32[200,128]{1,0:T(8,128)S(1)}, f32[200,128]{1,0:T(8,128)S(1)}, u32[]{:S(2)}, u32[]{:S(2)}) collective-permute-start(f32[200,128]{1,0:T(8,128)S(1)} %get-tuple-element.88), channel_id=1, source_target_pairs={{0,16},{2,18},{4,20},{6,22},{8,24},{10,26},{12,28},{14,30},{16,0},... | collective-permute-start | bytes 307208 | tf_op jit(solution)/shard_map/ppermute | solution.py:529
  126.6 20.5 %collective-permute-start.24 = (f32[200,128]{1,0:T(8,128)S(1)}, f32[200,128]{1,0:T(8,128)S(1)}, u32[]{:S(2)}, u32[]{:S(2)}) collective-permute-start(f32[200,128]{1,0:T(8,128)S(1)} %get-tuple-element.89), channel_id=1, source_target_pairs={{0,18},{2,20},{4,22},{6,24},{8,26},{10,28},{12,30},{14,0},{16,2},{... | collective-permute-start | bytes 307208 | tf_op jit(solution)/shard_map/ppermute | solution.py:529
  141.8 31.3 %collective-permute-start.26 = (f32[200,128]{1,0:T(8,128)}, f32[200,128]{1,0:T(8,128)}, u32[]{:S(2)}, u32[]{:S(2)}) collective-permute-start(f32[200,128]{1,0:T(8,128)} %get-tuple-element.91), channel_id=1, source_target_pairs={{0,22},{2,24},{4,26},{6,28},{8,30},{10,0},{12,2},{14,4},{16,6},{18... | collective-permute-start | bytes 307208 | tf_op jit(solution)/shard_map/ppermute | solution.py:529
  143.2 30.2 %collective-permute-start.27 = (f32[200,128]{1,0:T(8,128)}, f32[200,128]{1,0:T(8,128)}, u32[]{:S(2)}, u32[]{:S(2)}) collective-permute-start(f32[200,128]{1,0:T(8,128)} %get-tuple-element.92), channel_id=1, source_target_pairs={{0,24},{2,26},{4,28},{6,30},{8,0},{10,2},{12,4},{14,6},{16,8},{18,... | collective-permute-start | bytes 307208 | tf_op jit(solution)/shard_map/ppermute | solution.py:529
  146.1 28.8 %collective-permute-start.28 = (f32[200,128]{1,0:T(8,128)}, f32[200,128]{1,0:T(8,128)}, u32[]{:S(2)}, u32[]{:S(2)}) collective-permute-start(f32[200,128]{1,0:T(8,128)} %get-tuple-element.93), channel_id=1, source_target_pairs={{0,26},{2,28},{4,30},{6,0},{8,2},{10,4},{12,6},{14,8},{16,10},{18,... | collective-permute-start | bytes 307208 | tf_op jit(solution)/shard_map/ppermute | solution.py:529
  147.7 27.2 %collective-permute-start.29 = (f32[200,128]{1,0:T(8,128)}, f32[200,128]{1,0:T(8,128)}, u32[]{:S(2)}, u32[]{:S(2)}) collective-permute-start(f32[200,128]{1,0:T(8,128)} %get-tuple-element.94), channel_id=1, source_target_pairs={{0,28},{2,30},{4,0},{6,2},{8,4},{10,6},{12,8},{14,10},{16,12},{18,... | collective-permute-start | bytes 307208 | tf_op jit(solution)/shard_map/ppermute | solution.py:529
  152.7 22.3 %collective-permute-start.30 = (f32[200,128]{1,0:T(8,128)}, f32[200,128]{1,0:T(8,128)}, u32[]{:S(2)}, u32[]{:S(2)}) collective-permute-start(f32[200,128]{1,0:T(8,128)} %get-tuple-element.95), channel_id=1, source_target_pairs={{0,30},{2,0},{4,2},{6,4},{8,6},{10,8},{12,10},{14,12},{16,14},{18,... | collective-permute-start | bytes 307208 | tf_op jit(solution)/shard_map/ppermute | solution.py:529
  175.0 22.6 %collective-permute-start.35 = (f32[192,128]{1,0:T(8,128)S(1)}, f32[192,128]{1,0:T(8,128)S(1)}, u32[]{:S(2)}, u32[]{:S(2)}) collective-permute-start(f32[192,128]{1,0:T(8,128)S(1)} %get-tuple-element.105), channel_id=1, source_target_pairs={{0,10},{2,12},{4,14},{6,16},{8,18},{10,20},{12,22},{14,24},{16,26}... | collective-permute-start | bytes 294920 | tf_op jit(solution)/shard_map/ppermute | solution.py:529
  180.0 17.8 %collective-permute-start.36 = (f32[192,128]{1,0:T(8,128)S(1)}, f32[192,128]{1,0:T(8,128)S(1)}, u32[]{:S(2)}, u32[]{:S(2)}) collective-permute-start(f32[192,128]{1,0:T(8,128)S(1)} %get-tuple-element.106), channel_id=1, source_target_pairs={{0,12},{2,14},{4,16},{6,18},{8,20},{10,22},{12,24},{14,26},{16,28}... | collective-permute-start | bytes 294920 | tf_op jit(solution)/shard_map/ppermute | solution.py:529
  181.7 17.4 %collective-permute-start.37 = (f32[192,128]{1,0:T(8,128)S(1)}, f32[192,128]{1,0:T(8,128)S(1)}, u32[]{:S(2)}, u32[]{:S(2)}) collective-permute-start(f32[192,128]{1,0:T(8,128)S(1)} %get-tuple-element.107), channel_id=1, source_target_pairs={{0,14},{2,16},{4,18},{6,20},{8,22},{10,24},{12,26},{14,28},{16,30}... | collective-permute-start | bytes 294920 | tf_op jit(solution)/shard_map/ppermute | solution.py:529
  181.7 20.4 %collective-permute-start.38 = (f32[192,128]{1,0:T(8,128)S(1)}, f32[192,128]{1,0:T(8,128)S(1)}, u32[]{:S(2)}, u32[]{:S(2)}) collective-permute-start(f32[192,128]{1,0:T(8,128)S(1)} %get-tuple-element.108), channel_id=1, source_target_pairs={{0,16},{2,18},{4,20},{6,22},{8,24},{10,26},{12,28},{14,30},{16,0},... | collective-permute-start | bytes 294920 | tf_op jit(solution)/shard_map/ppermute | solution.py:529
  183.8 20.9 %collective-permute-start.39 = (f32[192,128]{1,0:T(8,128)S(1)}, f32[192,128]{1,0:T(8,128)S(1)}, u32[]{:S(2)}, u32[]{:S(2)}) collective-permute-start(f32[192,128]{1,0:T(8,128)S(1)} %get-tuple-element.109), channel_id=1, source_target_pairs={{0,18},{2,20},{4,22},{6,24},{8,26},{10,28},{12,30},{14,0},{16,2},{... | collective-permute-start | bytes 294920 | tf_op jit(solution)/shard_map/ppermute | solution.py:529
  (59 other events, 1566.3 us)

commit v4 on v3

--- a/solution.py
+++ b/solution.py
@@ -182,21 +182,25 @@
     )(spectrum)
 
 
-def far_copies(count, place, stacked, pieces, sem, outward):
-    rows = stacked.shape[1]
+def far_copies(count, place, stacked, pieces, sem, outward, batch):
+    size = stacked.shape[1] // 2
+    rows = pl.ds(batch * size, size)
     out = []
     for k in range(count):
         other = lax.rem(place + (k if outward else count - k), count)
-        mine = stacked.at[other]
-        piece = pieces[k].at[pl.ds(0, rows)]
+        mine = stacked.at[other, rows]
+        piece = pieces[k].at[rows]
         pair = (mine, piece) if outward else (piece, mine)
-        out.append(pltpu.make_async_copy(pair[0], pair[1], sem.at[k]))
+        out.append(pltpu.make_async_copy(pair[0], pair[1], sem.at[batch * count + k]))
     return out
 
 
-def run_copies(copies):
+def start_all(copies):
     for copy in copies:
         copy.start()
+
+
+def wait_all(copies):
     for copy in copies:
         copy.wait()
 
@@ -212,7 +216,7 @@
     width = span // count * 2
     depth = per * half
     quarter = half // 2
-    steps = [(b, q * quarter) for b in range(per) for q in range(2)]
+    steps = [(b, q * quarter) for q in range(2) for b in range(per)]
 
     def body(place_ref, v_ref, *refs):
         refs = list(refs)
@@ -232,7 +236,7 @@
         leave = []
         for j, (b, r) in enumerate(steps):
             arrive[j].wait()
-            rows = pl.ds(b * half + r, quarter)
+            rows = pl.ds(j * quarter, quarter)
             for tile in range(count // 2):
                 top = buf[j, 0, :, tile * width : (tile + 1) * width]
                 low = buf[j, 1, :, tile * width : (tile + 1) * width]
@@ -245,13 +249,12 @@
                     pltpu.make_async_copy(packed.at[:, rows], outs[0].at[:, rows], out_sem.at[j])
                 )
                 leave[-1].start()
+            elif b == per - 1:
+                batch = far_copies(count, place_ref[0], packed, outs, out_sem, True, j // per)
+                start_all(batch)
+                leave += batch
         sums[...] = total
-        if parts:
-            leave = far_copies(count, place_ref[0], packed, outs, out_sem, True)
-            for copy in leave:
-                copy.start()
-        for copy in leave:
-            copy.wait()
+        wait_all(leave)
 
     if parts:
         outs = [jax.ShapeDtypeStruct((depth, width), F32)] * count
@@ -267,7 +270,7 @@
             pltpu.VMEM((len(steps), 2, quarter, span), F32),
             pltpu.VMEM((count, depth, width), F32),
             pltpu.SemaphoreType.DMA((len(steps),)),
-            pltpu.SemaphoreType.DMA((max(count, len(steps)),)),
+            pltpu.SemaphoreType.DMA((max(2 * count, len(steps)),)),
         ],
         compiler_params=pltpu.CompilerParams(vmem_limit_bytes=58 << 20),
         cost_estimate=pl.CostEstimate(
@@ -284,6 +287,7 @@
     depth, width = arrived[0].shape[-2:]
     slots, block = tables.shape[0], tables.shape[2] // 2
     half = block // 2
+    quarter = half // 2
     per = depth // half
     out_blocks = per * count
     size = 2 * slots
@@ -303,18 +307,47 @@
             )
             for c in range(cuts)
         ]
-        if gather:
-            copies = far_copies(count, place_ref[0], lines, ins, in_sem, False)
-        else:
-            copies = [pltpu.make_async_copy(ins[0], lines, in_sem.at[0])]
-        for copy in copies + load:
-            copy.start()
-        for copy in copies:
-            copy.wait()
-
-        def at_block(b, at):
-            return b // per, pl.ds((b % per) * half + at, GROUP), slice(None)
-
+        arrive = []
+        for batch in range(2):
+            rows = pl.ds(batch * per * quarter, per * quarter)
+            if gather:
+                arrive.append(far_copies(count, place_ref[0], lines, ins, in_sem, False, batch))
+            else:
+                arrive.append(
+                    [
+                        pltpu.make_async_copy(
+                            ins[0].at[:, rows], lines.at[:, rows], in_sem.at[batch]
+                        )
+                    ]
+                )
+        start_all(arrive[1] + arrive[0] + load)
+
+        def at_block(b, batch, at):
+            row = (batch * per + b % per) * quarter
+            return b // per, pl.ds(row + at, GROUP), slice(None)
+
+        def forward(batch):
+            def step(group, _):
+                at = pl.multiple_of(group * GROUP, GROUP)
+                here = pl.ds(batch * quarter + at, GROUP)
+                seq = [lines[at_block(b, batch, at)] for b in range(out_blocks)]
+                seq.append(extra[here, :])
+                out = real_transform(seq + [None] * (size - out_blocks - 1))
+                spec[0, here, :width] = out[0][0]
+                spec[0, here, width:] = out[slots][0]
+                for f in range(1, slots):
+                    spec[f, here, :width] = out[f][0]
+                    spec[f, here, width:] = out[f][1]
+                return 0
+
+            lax.fori_loop(0, quarter // GROUP, step, 0)
+
+        extra[...] = jnp.zeros_like(extra)
+        wait_all(arrive[1])
+        early = ext_rows <= quarter
+        if early:
+            forward(1)
+        wait_all(arrive[0])
         ext = jnp.zeros((ext_rows, width), F32)
         for j in range(match):
             ext += g_ref[:, j : j + 1] * lines[0, j : j + 1, :]
@@ -322,24 +355,12 @@
             row = depth - match + j
             tail = swap(lines[count - 1, row : row + 1, :])
             ext += g_ref[:, match + j : match + j + 1] * tail
-        extra[...] = jnp.zeros_like(extra)
         extra[:ext_rows, :] = merge(ext, jnp.zeros_like(ext))
 
-        def forward(group, _):
-            at = pl.multiple_of(group * GROUP, GROUP)
-            seq = [lines[at_block(b, at)] for b in range(out_blocks)]
-            seq.append(extra[pl.ds(at, GROUP), :])
-            out = real_transform(seq + [None] * (size - out_blocks - 1))
-            spec[0, pl.ds(at, GROUP), :width] = out[0][0]
-            spec[0, pl.ds(at, GROUP), width:] = out[slots][0]
-            for f in range(1, slots):
-                spec[f, pl.ds(at, GROUP), :width] = out[f][0]
-                spec[f, pl.ds(at, GROUP), width:] = out[f][1]
-            return 0
-
-        lax.fori_loop(0, half // GROUP, forward, 0)
-        for copy in load:
-            copy.wait()
+        forward(0)
+        if not early:
+            forward(1)
+        wait_all(load)
 
         def product(f, blocks):
             high, mid, low = split_parts(jnp.concatenate(blocks, 0))
@@ -373,25 +394,32 @@
 
         lax.fori_loop(1, slots, multiply, 0, unroll=8)
 
-        def backward(group, _):
-            at = pl.multiple_of(group * GROUP, GROUP)
-            values = [(spec[0, pl.ds(at, GROUP), :width], None)]
-            for f in range(1, slots):
-                values.append(
-                    (spec[f, pl.ds(at, GROUP), :width], spec[f, pl.ds(at, GROUP), width:])
-                )
-            values.append((spec[0, pl.ds(at, GROUP), width:], None))
-            for b, value in enumerate(real_inverse(values, size, out_blocks)):
-                result[at_block(b, at)] = value
-            return 0
-
-        lax.fori_loop(0, half // GROUP, backward, 0)
-        copies = far_copies(count, place_ref[0], result, outs, out_sem, True)
+        def backward(batch):
+            def step(group, _):
+                at = pl.multiple_of(group * GROUP, GROUP)
+                here = pl.ds(batch * quarter + at, GROUP)
+                values = [(spec[0, here, :width], None)]
+                for f in range(1, slots):
+                    values.append((spec[f, here, :width], spec[f, here, width:]))
+                values.append((spec[0, here, width:], None))
+                for b, value in enumerate(real_inverse(values, size, out_blocks)):
+                    result[at_block(b, batch, at)] = value
+                return 0
+
+            lax.fori_loop(0, quarter // GROUP, step, 0)
+
+        leave = []
         if below:
             for k in range(count):
                 under = outs[k].at[pl.ds(depth, below)]
-                copies.append(pltpu.make_async_copy(sums_ref, under, sum_sem.at[k]))
-        run_copies(copies)
+                leave.append(pltpu.make_async_copy(sums_ref, under, sum_sem.at[k]))
+            start_all(leave)
+        for batch in range(2):
+            backward(batch)
+            copies = far_copies(count, place_ref[0], result, outs, out_sem, True, batch)
+            start_all(copies)
+            leave += copies
+        wait_all(leave)
 
     out_shape = [jax.ShapeDtypeStruct((depth + below, width), F32)] * count
     stacked = pltpu.VMEM((count, depth, width), F32)
@@ -408,8 +436,8 @@
             stacked,
             stacked,
             pltpu.SemaphoreType.DMA((cuts,)),
-            pltpu.SemaphoreType.DMA((count,)),
-            pltpu.SemaphoreType.DMA((count,)),
+            pltpu.SemaphoreType.DMA((2 * count,)),
+            pltpu.SemaphoreType.DMA((2 * count,)),
             pltpu.SemaphoreType.DMA((count,)),
         ],
         compiler_params=pltpu.CompilerParams(vmem_limit_bytes=50 << 20),
@@ -429,7 +457,7 @@
     count = len(arrived)
     depth, width = per * half, arrived[0].shape[-1]
     quarter = half // 2
-    steps = [(b, q * quarter) for b in range(per) for q in range(2)]
+    steps = [(b, q * quarter) for q in range(2) for b in range(per)]
     kept = 0 if earlier is None else 2
 
     def body(place_ref, v_ref, *refs):
@@ -448,15 +476,17 @@
             pltpu.make_async_copy(part(v_ref, j), v_buf.at[j], v_sem.at[j])
             for j in range(len(steps))
         ]
-        pieces = far_copies(count, place_ref[0], stacked, ins, in_sem, False)
+        pieces = [
+            far_copies(count, place_ref[0], stacked, ins, in_sem, False, batch)
+            for batch in range(2)
+        ]
+        below = []
         if adding:
             for k in range(count):
-                below = ins[k].at[pl.ds(depth, 8)]
-                pieces.append(pltpu.make_async_copy(below, tiles.at[k], sum_sem.at[k]))
-        for copy in pieces + fields:
-            copy.start()
-        for copy in pieces:
-            copy.wait()
+                under = ins[k].at[pl.ds(depth, 8)]
+                below.append(pltpu.make_async_copy(under, tiles.at[k], sum_sem.at[k]))
+        start_all(below + fields[:per] + pieces[0] + fields[per:] + pieces[1])
+        wait_all(below)
         if adding:
             tile = tiles[0]
             for k in range(1, count):
@@ -469,8 +499,10 @@
         rate = jnp.broadcast_to(courant / jnp.sqrt(mean_square + epsilon), (quarter, width))
         leave = []
         for j, (b, r) in enumerate(steps):
+            if b == 0:
+                wait_all(pieces[j // per])
             fields[j].wait()
-            rows = pl.ds(b * half + r, quarter)
+            rows = pl.ds(j * quarter, quarter)
             for tile in range(count // 2):
                 lanes = slice(tile * width, (tile + 1) * width)
                 one = stacked[2 * tile, rows, :]
@@ -481,14 +513,12 @@
                     f_buf[j, side, :, lanes] = field - rate * field * slope
             leave.append(pltpu.make_async_copy(s_buf.at[j], part(s_ref, j), s_sem.at[j]))
             leave.append(pltpu.make_async_copy(f_buf.at[j], part(f_ref, j), f_sem.at[j]))
-            leave[-2].start()
-            leave[-1].start()
-        for copy in leave:
-            copy.wait()
+            start_all(leave[-2:])
+        wait_all(leave)
 
     buffer = pltpu.VMEM((len(steps), 2, quarter, span), F32)
     step_sem = pltpu.SemaphoreType.DMA((len(steps),))
-    piece_sem = pltpu.SemaphoreType.DMA((count,))
+    piece_sem = pltpu.SemaphoreType.DMA((2 * count,))
     out = pl.pallas_call(
         body,
         name="advect",

time: 220 us -> 220 us (level)
  no operation moved by 1% of the time
where the time goes in v4:
time: 220 us
  starting transfers between devices  81.7 us (37%)
  waiting for transfers between devices  72.1 us (33%)
  Pallas kernels  59.2 us (27%)
  local copies, waits for them, and re-layouts  5.52 us (3%)
    ppermute x45, starting transfers between devices, exchange(): lax.ppermute(pieces[k], axis, [(i, (i + k) % count) for i in range(count)])  72.5 us
    ppermute x45, waiting for transfers between devices, exchange(): lax.ppermute(pieces[k], axis, [(i, (i + k) % count) for i in range(count)])  72.1 us
    pallas_call x2, Pallas kernels, line_slopes(): pl.pallas_call(body, name='line_slopes', in_specs=[SMEM, VMEM, HBM] + [VM...  35 us
    pallas_call x2, Pallas kernels, advect(): pl.pallas_call(body, name='advect', in_specs=[SMEM, HBM] + [HBM] * kept +...  9.99 us
    pallas_call x2, Pallas kernels, pack(): pl.pallas_call(body, name='pack_pieces' if parts else 'pack_stacked', in_...  7.66 us
    all_to_all x1, starting transfers between devices, exchange(): return lax.all_to_all(pieces, axis, split_axis=0, concat_axis=0, tiled=True)  7.6 us
    pallas_call x1, Pallas kernels, toeplitz_tables(): pl.pallas_call(body, name='toeplitz_tables', in_specs=[VMEM], out_specs=H...  6.55 us
    unnamed x74, local copies, waits for them, and re-layouts  5.52 us
  transfers between devices with their start and end apart: 47, of which 13 were waited for; matrix products, arithmetic and copies ran while one was open for 0% of the time, Pallas kernels for 18%

profile of v4, /device:TPU:0, one launch (start us, length us, event | category | flops | bytes accessed | tf_op | source)
XLA Modules:
  0.0 219.9 jit_solution(7760059903126438735)
XLA Ops:
  0.6 3.6 %pack_pieces.1 = (f32[192,128]{1,0:T(8,128)}, f32[192,128]{1,0:T(8,128)}, f32[192,128]{1,0:T(8,128)}, f32[192,128]{1,0:T(8,128)}, f32[192,128]{1,0:T(8,128)}, /*...) custom-call(s32[1]{0:T(128)} %bitcast.place_ref, ...), custom_call_target="tpu_custom_call" | custom-call | flops 786432 | bytes 3145728 | tf_op jit(solution)/shard_map/pack_pieces/pallas_call | solution.py:263
  4.2 4.1 %pack_stacked.1 = (f32[16,192,128]{2,1,0:T(8,128)}, f32[8,128]{1,0:T(8,128)}) custom-call(s32[1]{0:T(128)} %bitcast.place_ref, f32[3,2,64,2048]{3,2,1,0:T(8,128)} %bitcast.5, f32[8,128]{1,0:T(8,128)} %get-tuple-element.60.refs_0_), custom_call_target="tpu_custom_call" | custom-call | flops 786432 | bytes 3145728 | tf_op jit(solution)/shard_map/pack_stacked/pallas_call | solution.py:263
  8.3 6.6 %toeplitz_tables.1.table_ref = bf16[48,384,256]{2,1,0:T(8,128)(2,1)} custom-call(f32[96,256]{1,0:T(8,128)} %constant.11.clone.w_ref), custom_call_target="tpu_custom_call" | custom-call | flops 25165824 | bytes 9437184 | tf_op jit(solution)/shard_map/toeplitz_tables/pallas_call | solution.py:169
  15.1 7.6 %all-to-all-start = ((f32[16,192,128]{2,1,0:T(8,128)}), f32[16,192,128]{2,1,0:T(8,128)}, u32[]{:S(2)}, u32[]{:S(2)}) async-start(f32[16,192,128]{2,1,0:T(8,128)} %get-tuple-element.99), calls=%async_computation | async-start | bytes 3145728 | tf_op jit(solution)/shard_map/all_to_all | solution.py:555
  30.0 25.5 %collective-permute-done.1.refs_2_ = f32[192,128]{1,0:T(8,128)S(1)} collective-permute-done((f32[192,128]{1,0:T(8,128)S(1)}, f32[192,128]{1,0:T(8,128)S(1)}, u32[]{:S(2)}, u32[]{:S(2)}) %collective-permute-start.1) | collective-permute-done | bytes 98336 | tf_op jit(solution)/shard_map/ppermute | solution.py:559
  56.7 9.8 %collective-permute-start.7 = (f32[192,128]{1,0:T(8,128)S(1)}, f32[192,128]{1,0:T(8,128)S(1)}, u32[]{:S(2)}, u32[]{:S(2)}) collective-permute-start(f32[192,128]{1,0:T(8,128)S(1)} %copy-done.29), channel_id=1, source_target_pairs={{0,14},{2,16},{4,18},{6,20},{8,22},{10,24},{12,26},{14,28},{16,30}... | collective-permute-start | bytes 294920 | tf_op jit(solution)/shard_map/ppermute | solution.py:559
  70.1 8.6 %collective-permute-done.5.refs_6_ = f32[192,128]{1,0:T(8,128)S(1)} collective-permute-done((f32[192,128]{1,0:T(8,128)S(1)}, f32[192,128]{1,0:T(8,128)S(1)}, u32[]{:S(2)}, u32[]{:S(2)}) %collective-permute-start.5) | collective-permute-done | bytes 98336 | tf_op jit(solution)/shard_map/ppermute | solution.py:559
  80.1 3.4 %collective-permute-start.12 = (f32[192,128]{1,0:T(8,128)S(1)}, f32[192,128]{1,0:T(8,128)S(1)}, u32[]{:S(2)}, u32[]{:S(2)}) collective-permute-start(f32[192,128]{1,0:T(8,128)S(1)} %copy-done.24), channel_id=1, source_target_pairs={{0,24},{2,26},{4,28},{6,30},{8,0},{10,2},{12,4},{14,6},{16,8},{18,... | collective-permute-start | bytes 294920 | tf_op jit(solution)/shard_map/ppermute | solution.py:559
  83.5 6.0 %collective-permute-start.13 = (f32[192,128]{1,0:T(8,128)S(1)}, f32[192,128]{1,0:T(8,128)S(1)}, u32[]{:S(2)}, u32[]{:S(2)}) collective-permute-start(f32[192,128]{1,0:T(8,128)S(1)} %copy-done.23), channel_id=1, source_target_pairs={{0,26},{2,28},{4,30},{6,0},{8,2},{10,4},{12,6},{14,8},{16,10},{18,... | collective-permute-start | bytes 294920 | tf_op jit(solution)/shard_map/ppermute | solution.py:559
  96.6 18.4 %line_slopes.2 = (f32[200,128]{1,0:T(8,128)S(1)}, f32[200,128]{1,0:T(8,128)S(1)}, f32[200,128]{1,0:T(8,128)S(1)}, f32[200,128]{1,0:T(8,128)S(1)}, f32[200,128]{1...) custom-call(s32[1]{0:T(128)} %bitcast.place_ref, ...), custom_call_target="tpu_custom_call" | custom-call | flops 3221225472 | bytes 3145728 | tf_op jit(solution)/shard_map/line_slopes/pallas_call | solution.py:426
  118.0 3.1 %collective-permute-start.20 = (f32[200,128]{1,0:T(8,128)S(1)}, f32[200,128]{1,0:T(8,128)S(1)}, u32[]{:S(2)}, u32[]{:S(2)}) collective-permute-start(f32[200,128]{1,0:T(8,128)S(1)} %get-tuple-element.85), channel_id=1, source_target_pairs={{0,10},{2,12},{4,14},{6,16},{8,18},{10,20},{12,22},{14,24},{16,26}... | collective-permute-start | bytes 307208 | tf_op jit(solution)/shard_map/ppermute | solution.py:559
  122.1 3.0 %collective-permute-done.17.refs_2_ = f32[200,128]{1,0:T(8,128)S(1)} collective-permute-done((f32[200,128]{1,0:T(8,128)S(1)}, f32[200,128]{1,0:T(8,128)S(1)}, u32[]{:S(2)}, u32[]{:S(2)}) %collective-permute-start.17) | collective-permute-done | bytes 102432 | tf_op jit(solution)/shard_map/ppermute | solution.py:559
  126.9 3.0 %collective-permute-start.24 = (f32[200,128]{1,0:T(8,128)S(1)}, f32[200,128]{1,0:T(8,128)S(1)}, u32[]{:S(2)}, u32[]{:S(2)}) collective-permute-start(f32[200,128]{1,0:T(8,128)S(1)} %get-tuple-element.89), channel_id=1, source_target_pairs={{0,18},{2,20},{4,22},{6,24},{8,26},{10,28},{12,30},{14,0},{16,2},{... | collective-permute-start | bytes 307208 | tf_op jit(solution)/shard_map/ppermute | solution.py:559
  129.9 10.9 %collective-permute-done.20.refs_5_ = f32[200,128]{1,0:T(8,128)S(1)} collective-permute-done((f32[200,128]{1,0:T(8,128)S(1)}, f32[200,128]{1,0:T(8,128)S(1)}, u32[]{:S(2)}, u32[]{:S(2)}) %collective-permute-start.20) | collective-permute-done | bytes 102432 | tf_op jit(solution)/shard_map/ppermute | solution.py:559
  148.1 4.3 %collective-permute-start.29 = (f32[200,128]{1,0:T(8,128)}, f32[200,128]{1,0:T(8,128)}, u32[]{:S(2)}, u32[]{:S(2)}) collective-permute-start(f32[200,128]{1,0:T(8,128)} %get-tuple-element.94), channel_id=1, source_target_pairs={{0,28},{2,30},{4,0},{6,2},{8,4},{10,6},{12,8},{14,10},{16,12},{18,... | collective-permute-start | bytes 307208 | tf_op jit(solution)/shard_map/ppermute | solution.py:559
  153.1 2.6 %collective-permute-start.30 = (f32[200,128]{1,0:T(8,128)}, f32[200,128]{1,0:T(8,128)}, u32[]{:S(2)}, u32[]{:S(2)}) collective-permute-start(f32[200,128]{1,0:T(8,128)} %get-tuple-element.95), channel_id=1, source_target_pairs={{0,30},{2,0},{4,2},{6,4},{8,6},{10,8},{12,10},{14,12},{16,14},{18,... | collective-permute-start | bytes 307208 | tf_op jit(solution)/shard_map/ppermute | solution.py:559
  156.5 16.6 %line_slopes.3 = (f32[192,128]{1,0:T(8,128)S(1)}, f32[192,128]{1,0:T(8,128)S(1)}, f32[192,128]{1,0:T(8,128)S(1)}, f32[192,128]{1,0:T(8,128)S(1)}, f32[192,128]{1...) custom-call(s32[1]{0:T(128)} %bitcast.place_ref, ...), custom_call_target="tpu_custom_call" | custom-call | flops 3221225472 | bytes 3145728 | tf_op jit(solution)/shard_map/line_slopes/pallas_call | solution.py:426
  175.2 4.9 %collective-permute-done.31.refs_4_ = f32[192,128]{1,0:T(8,128)S(1)} collective-permute-done((f32[192,128]{1,0:T(8,128)S(1)}, f32[192,128]{1,0:T(8,128)S(1)}, u32[]{:S(2)}, u32[]{:S(2)}) %collective-permute-start.31) | collective-permute-done | bytes 98336 | tf_op jit(solution)/shard_map/ppermute | solution.py:559
  185.9 11.8 %collective-permute-done.35.refs_8_ = f32[192,128]{1,0:T(8,128)S(1)} collective-permute-done((f32[192,128]{1,0:T(8,128)S(1)}, f32[192,128]{1,0:T(8,128)S(1)}, u32[]{:S(2)}, u32[]{:S(2)}) %collective-permute-start.35) | collective-permute-done | bytes 98336 | tf_op jit(solution)/shard_map/ppermute | solution.py:559
  199.1 3.0 %collective-permute-start.42 = (f32[192,128]{1,0:T(8,128)S(1)}, f32[192,128]{1,0:T(8,128)S(1)}, u32[]{:S(2)}, u32[]{:S(2)}) collective-permute-start(f32[192,128]{1,0:T(8,128)S(1)} %get-tuple-element.112), channel_id=1, source_target_pairs={{0,24},{2,26},{4,28},{6,30},{8,0},{10,2},{12,4},{14,6},{16,8},{18,... | collective-permute-start | bytes 294920 | tf_op jit(solution)/shard_map/ppermute | solution.py:559
  202.1 2.6 %collective-permute-start.43 = (f32[192,128]{1,0:T(8,128)S(1)}, f32[192,128]{1,0:T(8,128)S(1)}, u32[]{:S(2)}, u32[]{:S(2)}) collective-permute-start(f32[192,128]{1,0:T(8,128)S(1)} %get-tuple-element.113), channel_id=1, source_target_pairs={{0,26},{2,28},{4,30},{6,0},{8,2},{10,4},{12,6},{14,8},{16,10},{18,... | collective-permute-start | bytes 294920 | tf_op jit(solution)/shard_map/ppermute | solution.py:559
  207.0 2.6 %collective-permute-start.45 = (f32[192,128]{1,0:T(8,128)S(1)}, f32[192,128]{1,0:T(8,128)S(1)}, u32[]{:S(2)}, u32[]{:S(2)}) collective-permute-start(f32[192,128]{1,0:T(8,128)S(1)} %get-tuple-element.115), channel_id=1, source_target_pairs={{0,30},{2,0},{4,2},{6,4},{8,6},{10,8},{12,10},{14,12},{16,14},{18,... | collective-permute-start | bytes 294920 | tf_op jit(solution)/shard_map/ppermute | solution.py:559
  209.7 4.8 %advect.2 = (f32[3,2,64,2048]{3,2,1,0:T(8,128)}, f32[3,2,64,2048]{3,2,1,0:T(8,128)}, f32[8,128]{1,0:T(8,128)S(1)}) custom-call(s32[1]{0:T(128)} %bitcast.place_ref, f32[3,2,64,2048]{3,2,1,0:T(8,128)S(1)} %bitcast.6, f32[200,128]{1,0:T(8,128)S(1)} %get-tuple-element.80.refs_0_, f32[200,128]{1,0:T(8,128)S(1)} %collective-permute-done.16.refs_1_, ...), custom_call_target="tpu_custom_call" | custom-call | flops 1179648 | bytes 6291456 | tf_op jit(solution)/shard_map/advect/pallas_call | solution.py:522
  214.5 5.2 %advect.3 = (f32[3,2,64,2048]{3,2,1,0:T(8,128)}, f32[3,2,64,2048]{3,2,1,0:T(8,128)}) custom-call(s32[1]{0:T(128)} %bitcast.place_ref, f32[3,2,64,2048]{3,2,1,0:T(8,128)S(1)} %bitcast.7, f32[3,2,64,2048]{3,2,1,0:T(8,128)} %get-tuple-element.96.refs_0_, f32[3,2,64,2048]{3,2,1,0:T(8,128)} %get-tuple-element.97.refs_1_, ...), custom_call_target="tpu_custom_call", output_to_operand_aliasing={{0}: (2, {}), {1}: (3, {})} | custom-call | flops 1179648 | bytes 6291456 | tf_op jit(solution)/shard_map/advect/pallas_call | solution.py:522
  (153 shorter events, 46.5 us)
Async XLA Ops:
  15.1 140.6 %all-to-all-start = ((f32[16,192,128]{2,1,0:T(8,128)}), f32[16,192,128]{2,1,0:T(8,128)}, u32[]{:S(2)}, u32[]{:S(2)}) async-start(f32[16,192,128]{2,1,0:T(8,128)} %get-tuple-element.99), calls=%async_computation | async-start | bytes 3145728 | tf_op jit(solution)/shard_map/all_to_all | solution.py:555
  24.2 31.3 %collective-permute-start.1 = (f32[192,128]{1,0:T(8,128)S(1)}, f32[192,128]{1,0:T(8,128)S(1)}, u32[]{:S(2)}, u32[]{:S(2)}) collective-permute-start(f32[192,128]{1,0:T(8,128)S(1)} %copy-done.35), channel_id=1, source_target_pairs={{0,2},{2,4},{4,6},{6,8},{8,10},{10,12},{12,14},{14,16},{16,18},{18... | collective-permute-start | bytes 294920 | tf_op jit(solution)/shard_map/ppermute | solution.py:559
  24.3 32.4 %collective-permute-start.2 = (f32[192,128]{1,0:T(8,128)S(1)}, f32[192,128]{1,0:T(8,128)S(1)}, u32[]{:S(2)}, u32[]{:S(2)}) collective-permute-start(f32[192,128]{1,0:T(8,128)S(1)} %copy-done.34), channel_id=1, source_target_pairs={{0,4},{2,6},{4,8},{6,10},{8,12},{10,14},{12,16},{14,18},{16,20},{1... | collective-permute-start | bytes 294920 | tf_op jit(solution)/shard_map/ppermute | solution.py:559
  26.2 40.3 %collective-permute-start.3 = (f32[192,128]{1,0:T(8,128)S(1)}, f32[192,128]{1,0:T(8,128)S(1)}, u32[]{:S(2)}, u32[]{:S(2)}) collective-permute-start(f32[192,128]{1,0:T(8,128)S(1)} %copy-done.33), channel_id=1, source_target_pairs={{0,6},{2,8},{4,10},{6,12},{8,14},{10,16},{12,18},{14,20},{16,22},{... | collective-permute-start | bytes 294920 | tf_op jit(solution)/shard_map/ppermute | solution.py:559
  28.5 39.3 %collective-permute-start.4 = (f32[192,128]{1,0:T(8,128)S(1)}, f32[192,128]{1,0:T(8,128)S(1)}, u32[]{:S(2)}, u32[]{:S(2)}) collective-permute-start(f32[192,128]{1,0:T(8,128)S(1)} %copy-done.32), channel_id=1, source_target_pairs={{0,8},{2,10},{4,12},{6,14},{8,16},{10,18},{12,20},{14,22},{16,24},... | collective-permute-start | bytes 294920 | tf_op jit(solution)/shard_map/ppermute | solution.py:559
  30.0 48.8 %collective-permute-start.5 = (f32[192,128]{1,0:T(8,128)S(1)}, f32[192,128]{1,0:T(8,128)S(1)}, u32[]{:S(2)}, u32[]{:S(2)}) collective-permute-start(f32[192,128]{1,0:T(8,128)S(1)} %copy-done.31), channel_id=1, source_target_pairs={{0,10},{2,12},{4,14},{6,16},{8,18},{10,20},{12,22},{14,24},{16,26}... | collective-permute-start | bytes 294920 | tf_op jit(solution)/shard_map/ppermute | solution.py:559
  55.6 24.4 %collective-permute-start.6 = (f32[192,128]{1,0:T(8,128)S(1)}, f32[192,128]{1,0:T(8,128)S(1)}, u32[]{:S(2)}, u32[]{:S(2)}) collective-permute-start(f32[192,128]{1,0:T(8,128)S(1)} %copy-done.30), channel_id=1, source_target_pairs={{0,12},{2,14},{4,16},{6,18},{8,20},{10,22},{12,24},{14,26},{16,28}... | collective-permute-start | bytes 294920 | tf_op jit(solution)/shard_map/ppermute | solution.py:559
  56.7 23.4 %collective-permute-start.7 = (f32[192,128]{1,0:T(8,128)S(1)}, f32[192,128]{1,0:T(8,128)S(1)}, u32[]{:S(2)}, u32[]{:S(2)}) collective-permute-start(f32[192,128]{1,0:T(8,128)S(1)} %copy-done.29), channel_id=1, source_target_pairs={{0,14},{2,16},{4,18},{6,20},{8,22},{10,24},{12,26},{14,28},{16,30}... | collective-permute-start | bytes 294920 | tf_op jit(solution)/shard_map/ppermute | solution.py:559
  67.9 21.7 %collective-permute-start.9 = (f32[192,128]{1,0:T(8,128)S(1)}, f32[192,128]{1,0:T(8,128)S(1)}, u32[]{:S(2)}, u32[]{:S(2)}) collective-permute-start(f32[192,128]{1,0:T(8,128)S(1)} %copy-done.27), channel_id=1, source_target_pairs={{0,18},{2,20},{4,22},{6,24},{8,26},{10,28},{12,30},{14,0},{16,2},{... | collective-permute-start | bytes 294920 | tf_op jit(solution)/shard_map/ppermute | solution.py:559
  118.0 22.8 %collective-permute-start.20 = (f32[200,128]{1,0:T(8,128)S(1)}, f32[200,128]{1,0:T(8,128)S(1)}, u32[]{:S(2)}, u32[]{:S(2)}) collective-permute-start(f32[200,128]{1,0:T(8,128)S(1)} %get-tuple-element.85), channel_id=1, source_target_pairs={{0,10},{2,12},{4,14},{6,16},{8,18},{10,20},{12,22},{14,24},{16,26}... | collective-permute-start | bytes 307208 | tf_op jit(solution)/shard_map/ppermute | solution.py:559
  122.0 19.5 %collective-permute-start.21 = (f32[200,128]{1,0:T(8,128)S(1)}, f32[200,128]{1,0:T(8,128)S(1)}, u32[]{:S(2)}, u32[]{:S(2)}) collective-permute-start(f32[200,128]{1,0:T(8,128)S(1)} %get-tuple-element.86), channel_id=1, source_target_pairs={{0,12},{2,14},{4,16},{6,18},{8,20},{10,22},{12,24},{14,26},{16,28}... | collective-permute-start | bytes 307208 | tf_op jit(solution)/shard_map/ppermute | solution.py:559
  125.0 17.9 %collective-permute-start.22 = (f32[200,128]{1,0:T(8,128)S(1)}, f32[200,128]{1,0:T(8,128)S(1)}, u32[]{:S(2)}, u32[]{:S(2)}) collective-permute-start(f32[200,128]{1,0:T(8,128)S(1)} %get-tuple-element.87), channel_id=1, source_target_pairs={{0,14},{2,16},{4,18},{6,20},{8,22},{10,24},{12,26},{14,28},{16,30}... | collective-permute-start | bytes 307208 | tf_op jit(solution)/shard_map/ppermute | solution.py:559
  125.0 20.8 %collective-permute-start.23 = (f32[200,128]{1,0:T(8,128)S(1)}, f32[200,128]{1,0:T(8,128)S(1)}, u32[]{:S(2)}, u32[]{:S(2)}) collective-permute-start(f32[200,128]{1,0:T(8,128)S(1)} %get-tuple-element.88), channel_id=1, source_target_pairs={{0,16},{2,18},{4,20},{6,22},{8,24},{10,26},{12,28},{14,30},{16,0},... | collective-permute-start | bytes 307208 | tf_op jit(solution)/shard_map/ppermute | solution.py:559
  126.9 20.5 %collective-permute-start.24 = (f32[200,128]{1,0:T(8,128)S(1)}, f32[200,128]{1,0:T(8,128)S(1)}, u32[]{:S(2)}, u32[]{:S(2)}) collective-permute-start(f32[200,128]{1,0:T(8,128)S(1)} %get-tuple-element.89), channel_id=1, source_target_pairs={{0,18},{2,20},{4,22},{6,24},{8,26},{10,28},{12,30},{14,0},{16,2},{... | collective-permute-start | bytes 307208 | tf_op jit(solution)/shard_map/ppermute | solution.py:559
  142.1 31.0 %collective-permute-start.26 = (f32[200,128]{1,0:T(8,128)}, f32[200,128]{1,0:T(8,128)}, u32[]{:S(2)}, u32[]{:S(2)}) collective-permute-start(f32[200,128]{1,0:T(8,128)} %get-tuple-element.91), channel_id=1, source_target_pairs={{0,22},{2,24},{4,26},{6,28},{8,30},{10,0},{12,2},{14,4},{16,6},{18... | collective-permute-start | bytes 307208 | tf_op jit(solution)/shard_map/ppermute | solution.py:559
  143.6 29.9 %collective-permute-start.27 = (f32[200,128]{1,0:T(8,128)}, f32[200,128]{1,0:T(8,128)}, u32[]{:S(2)}, u32[]{:S(2)}) collective-permute-start(f32[200,128]{1,0:T(8,128)} %get-tuple-element.92), channel_id=1, source_target_pairs={{0,24},{2,26},{4,28},{6,30},{8,0},{10,2},{12,4},{14,6},{16,8},{18,... | collective-permute-start | bytes 307208 | tf_op jit(solution)/shard_map/ppermute | solution.py:559
  146.5 28.5 %collective-permute-start.28 = (f32[200,128]{1,0:T(8,128)}, f32[200,128]{1,0:T(8,128)}, u32[]{:S(2)}, u32[]{:S(2)}) collective-permute-start(f32[200,128]{1,0:T(8,128)} %get-tuple-element.93), channel_id=1, source_target_pairs={{0,26},{2,28},{4,30},{6,0},{8,2},{10,4},{12,6},{14,8},{16,10},{18,... | collective-permute-start | bytes 307208 | tf_op jit(solution)/shard_map/ppermute | solution.py:559
  148.1 26.9 %collective-permute-start.29 = (f32[200,128]{1,0:T(8,128)}, f32[200,128]{1,0:T(8,128)}, u32[]{:S(2)}, u32[]{:S(2)}) collective-permute-start(f32[200,128]{1,0:T(8,128)} %get-tuple-element.94), channel_id=1, source_target_pairs={{0,28},{2,30},{4,0},{6,2},{8,4},{10,6},{12,8},{14,10},{16,12},{18,... | collective-permute-start | bytes 307208 | tf_op jit(solution)/shard_map/ppermute | solution.py:559
  153.1 22.0 %collective-permute-start.30 = (f32[200,128]{1,0:T(8,128)}, f32[200,128]{1,0:T(8,128)}, u32[]{:S(2)}, u32[]{:S(2)}) collective-permute-start(f32[200,128]{1,0:T(8,128)} %get-tuple-element.95), channel_id=1, source_target_pairs={{0,30},{2,0},{4,2},{6,4},{8,6},{10,8},{12,10},{14,12},{16,14},{18,... | collective-permute-start | bytes 307208 | tf_op jit(solution)/shard_map/ppermute | solution.py:559
  175.1 22.6 %collective-permute-start.35 = (f32[192,128]{1,0:T(8,128)S(1)}, f32[192,128]{1,0:T(8,128)S(1)}, u32[]{:S(2)}, u32[]{:S(2)}) collective-permute-start(f32[192,128]{1,0:T(8,128)S(1)} %get-tuple-element.105), channel_id=1, source_target_pairs={{0,10},{2,12},{4,14},{6,16},{8,18},{10,20},{12,22},{14,24},{16,26}... | collective-permute-start | bytes 294920 | tf_op jit(solution)/shard_map/ppermute | solution.py:559
  180.1 17.8 %collective-permute-start.36 = (f32[192,128]{1,0:T(8,128)S(1)}, f32[192,128]{1,0:T(8,128)S(1)}, u32[]{:S(2)}, u32[]{:S(2)}) collective-permute-start(f32[192,128]{1,0:T(8,128)S(1)} %get-tuple-element.106), channel_id=1, source_target_pairs={{0,12},{2,14},{4,16},{6,18},{8,20},{10,22},{12,24},{14,26},{16,28}... | collective-permute-start | bytes 294920 | tf_op jit(solution)/shard_map/ppermute | solution.py:559
  181.7 17.4 %collective-permute-start.37 = (f32[192,128]{1,0:T(8,128)S(1)}, f32[192,128]{1,0:T(8,128)S(1)}, u32[]{:S(2)}, u32[]{:S(2)}) collective-permute-start(f32[192,128]{1,0:T(8,128)S(1)} %get-tuple-element.107), channel_id=1, source_target_pairs={{0,14},{2,16},{4,18},{6,20},{8,22},{10,24},{12,26},{14,28},{16,30}... | collective-permute-start | bytes 294920 | tf_op jit(solution)/shard_map/ppermute | solution.py:559
  181.7 20.4 %collective-permute-start.38 = (f32[192,128]{1,0:T(8,128)S(1)}, f32[192,128]{1,0:T(8,128)S(1)}, u32[]{:S(2)}, u32[]{:S(2)}) collective-permute-start(f32[192,128]{1,0:T(8,128)S(1)} %get-tuple-element.108), channel_id=1, source_target_pairs={{0,16},{2,18},{4,20},{6,22},{8,24},{10,26},{12,28},{14,30},{16,0},... | collective-permute-start | bytes 294920 | tf_op jit(solution)/shard_map/ppermute | solution.py:559
  183.8 20.9 %collective-permute-start.39 = (f32[192,128]{1,0:T(8,128)S(1)}, f32[192,128]{1,0:T(8,128)S(1)}, u32[]{:S(2)}, u32[]{:S(2)}) collective-permute-start(f32[192,128]{1,0:T(8,128)S(1)} %get-tuple-element.109), channel_id=1, source_target_pairs={{0,18},{2,20},{4,22},{6,24},{8,26},{10,28},{12,30},{14,0},{16,2},{... | collective-permute-start | bytes 294920 | tf_op jit(solution)/shard_map/ppermute | solution.py:559
  (59 other events, 1562.5 us)
